TPU v7x, 256 devices: a whole 4x4x8 slice. The times are simulated.
256 devices in a mesh: cls: 8 (over x_hi, y), ptl: 32 (over x_lo, z, core).
Axes of the slice: x: 4 (x_hi: 2, x_lo: 2; x = x_hi * 2 + x_lo), y: 4, z: 8, core: 2. Of those that a mesh axis runs over, the one named last changes fastest.
Arguments:
- references: bfloat16 [8, 256, 4096], P('cls', 'ptl')
- particles: bfloat16 [131072, 4096], P(('cls', 'ptl'))
- class_ids: int32 [131072], P(('cls', 'ptl')), may hold values from 0 to 7, as said below
- orient_ids: int32 [131072], P(('cls', 'ptl')), may hold values from 0 to 255
- offsets: int32 [131072], P(('cls', 'ptl')), may hold values from -3 to 3
- weights: float32 [131072], P(('cls', 'ptl'))
Outputs:
- class_sums: float32 [8, 4096], P('cls', 'ptl')
Inputs may be any that keep to these rules, and one draw needn't show every extreme that they name: `class_ids`: every class is the class of some particle; populations are uneven.
All inputs are finite; a program needn't handle non-finite values.
Results may differ from a plain program's by a relative error of at most 0.0028.
Values may be sent and summed in bfloat16 or wider, within the bound.
No kernel may reach another device: no remote copies, remote signals or barrier semaphores. Data moves between devices by JAX's collectives and lax.ppermute only.
A program may use at most 64 MiB of HBM per device.

v0:
```python
import math

import jax
import jax.numpy as jnp
from jax import lax
from jax.sharding import PartitionSpec as P

NX = 64
SHIFT = 3


def body(references, particles, class_ids, orient_ids, offsets, weights):
    n_cls = lax.axis_size("cls")
    n_ptl = lax.axis_size("ptl")
    per_owner, local_ori, voxels = references.shape
    orients = local_ori * n_ptl
    classes = per_owner * n_cls
    count = particles.shape[0]
    scale = 1.0 / math.sqrt(voxels)
    class_block = lax.all_gather(references, "ptl", axis=1, tiled=True)
    piece = lax.all_gather(class_block, "cls", axis=0, tiled=True)
    rows = piece.reshape(piece.shape[0] * orients, voxels)
    place = jnp.arange(rows.shape[0], dtype=jnp.int32)
    top = jnp.full((count,), -1e30, jnp.float32)
    scores = (
        lax.dot_general(
            particles, rows, (((1,), (1,)), ((), ())), preferred_element_type=jnp.float32
        )
        * scale
    )
    newtop = jnp.maximum(top, jnp.max(scores, axis=1))
    total = jnp.sum(jnp.exp(scores - newtop[:, None]), axis=1)
    picked = (class_ids[:, None] == (place // orients)[None, :]) & (
        orient_ids[:, None] == (place % orients)[None, :]
    )
    chosen = jnp.sum(jnp.where(picked, scores, 0.0), axis=1)
    top, total, chosen = (newtop, total, chosen)
    gain = (weights * (classes * orients) * jnp.exp(chosen - top) / total).astype(jnp.bfloat16)
    member = class_ids[None, :] == jnp.arange(classes, dtype=jnp.int32)[:, None]
    partial_sums = jnp.zeros((classes, voxels), jnp.float32)
    for step in range(-SHIFT, SHIFT + 1):
        coef = jnp.where(
            member & (offsets[None, :] == step), gain[None, :], jnp.zeros((), jnp.bfloat16)
        )
        moved = jnp.dot(coef, particles, preferred_element_type=jnp.float32)
        moved = jnp.roll(moved.reshape(classes, voxels // NX, NX), step, axis=2).reshape(
            classes, voxels
        )
        partial_sums = partial_sums + moved
    owned = lax.psum_scatter(partial_sums, "cls", scatter_dimension=0, tiled=True)
    owned = lax.psum_scatter(owned, "ptl", scatter_dimension=1, tiled=True)
    population = count * n_cls * n_ptl / classes
    return owned / jnp.sqrt(jnp.float32(population))


def solution(mesh):
    placed = (
        P("cls", "ptl", None),
        P(("cls", "ptl"), None),
        P(("cls", "ptl")),
        P(("cls", "ptl")),
        P(("cls", "ptl")),
        P(("cls", "ptl")),
    )
    return jax.shard_map(
        body, mesh=mesh, in_specs=placed, out_specs=P("cls", "ptl"), check_vma=False
    )
```

profile of v0, /device:TPU:1, one launch (start us, length us, event | category | flops | bytes accessed | tf_op | source)
XLA Modules:
  0.0 516.4 jit_solution(1313199074914181118)
XLA Ops:
  6.5 0.7 all-gather.3.cloned.1.call-update
  7.3 0.0 all-gather.5.cloned.1.call-start
  7.3 70.8 %all-gather.3.cloned.1.call-done = bf16[1,256,4096]{2,1,0:T(8,128)(2,1)} async-done(((bf16[1,8,4096]{2,1,0:T(8,128)(2,1)}), bf16[1,256,4096]{2,1,0:T(8,128)(2,1)}) %all-gather.3.cloned.1.call-update) | async-done | bytes 2097168 | tf_op jit(solution)/shard_map/all_gather | solution.py:20
  78.1 0.0 all-gather.5.cloned.1.call-update
  78.1 0.0 all-reduce.3.cloned.1.call-start
  78.2 0.7 broadcast_compare_fusion.3
  78.9 188.6 %all-gather.5.cloned.1.call-done = bf16[8,256,4096]{2,1,0:T(8,128)(2,1)} async-done(((bf16[1,256,4096]{2,1,0:T(8,128)(2,1)}), bf16[8,256,4096]{2,1,0:T(8,128)(2,1)}) %all-gather.5.cloned.1.call-update) | async-done | bytes 16777232 | tf_op jit(solution)/shard_map/all_gather | solution.py:21
  267.5 13.8 %select_reduce_fusion = (f32[512]{0:T(512)S(1)}, f32[512]{0:T(512)S(1)}, f32[512,2048]{1,0:T(8,128)S(1)}) fusion(s32[2048]{0:T(1024)S(1)} %get-tuple-element.15, s32[2048]{0:T(1024)S(1)} %get-tuple-element.16, s32[512]{0:T(512)} %param.9, s32[512]{0:T(512)} %param.8, bf16[512,4096]{1,0:T(8,128)(2,1)} %param.7, bf16[2048,4096]{1,0:T(8,128)(2,1)} %bitcast.27), kind=kOutput, calls=%fused_computation.5 | convolution fusion | flops 8597274624 | bytes 25190400 | tf_op jit(solution)/shard_map/dot_general | solution.py:26
  281.3 0.0 copy-start
  281.4 0.8 exponential_reduce_fusion
  282.2 1.3 copy-done
  283.5 0.7 fusion.35
  284.2 0.1 reshape.81
  284.3 0.1 slice.60
  284.4 2.8 fusion.33
  287.3 0.1 reshape.82
  287.4 0.1 slice.62
  287.5 2.8 fusion.31
  290.4 0.1 reshape.83
  290.5 0.1 slice.64
  290.6 0.3 fusion.3
  290.9 0.1 add.44
  291.0 2.8 fusion.28
  293.8 0.1 reshape.84
  293.9 0.1 slice.66
  294.1 0.1 pad_maximum_fusion
  294.2 0.1 reshape.85
  294.3 2.8 fusion.26
  297.2 0.1 reshape.86
  297.3 0.1 slice.68
  297.4 0.1 pad_maximum_fusion.1
  297.6 0.1 reshape.87
  297.7 2.8 fusion.24
  300.5 0.1 reshape.88
  300.6 0.1 slice.70
  300.8 0.1 pad_maximum_fusion.2
  300.9 0.1 reshape.89
  301.0 3.5 fusion.2
  304.5 0.0 all-reduce.3.cloned.1.call-update
  304.6 0.0 reduce-scatter.4.cloned.1.call-start
  304.6 0.6 dynamic-slice
  305.2 81.3 %all-reduce.3.cloned.1.call-done = f32[8,4096]{1,0:T(8,128)} async-done(((f32[8,4096]{1,0:T(8,128)}), f32[8,4096]{1,0:T(8,128)}) %all-reduce.3.cloned.1.call-update) | async-done | bytes 131088
  386.6 1.6 constant_dynamic-slice_fusion
  388.1 2.0 copy.7
  390.1 0.0 reduce-scatter.4.cloned.1.call-update
  390.1 118.3 %reduce-scatter.4.cloned.1.call-done = f32[128,1]{1,0:T(8,128)} async-done(((f32[4096,1]{1,0:T(8,128)}), f32[128,1]{1,0:T(8,128)}) %reduce-scatter.4.cloned.1.call-update) | async-done | bytes 528
  508.5 0.9 copy.8
  509.4 0.5 broadcast_multiply_fusion
  (10 shorter events, 0.0 us)
Async XLA Ops:
  6.5 71.6 %all-gather.3.cloned.1.call-start = ((), (), s32[]{:S(2)}) async-start(), calls=%async_computation.1 | async-start | bytes 2162688 | tf_op jit(solution)/shard_map/all_gather | solution.py:20
  7.3 260.3 %all-gather.5.cloned.1.call-start = ((), (), s32[]{:S(2)}) async-start(), calls=%async_computation.2 | async-start | bytes 18874368 | tf_op jit(solution)/shard_map/all_gather | solution.py:21
  78.1 308.4 %all-reduce.3.cloned.1.call-start = ((), (), s32[]{:S(2)}) async-start(), calls=%async_computation.4 | async-start | bytes 262144
  281.3 0.9 copy-start.2
  281.3 2.2 copy-start
  281.3 2.2 copy-start.1
  300.5 4.1 copy-start.3
  304.6 203.9 %reduce-scatter.4.cloned.1.call-start = ((), (), s32[]{:S(2)}) async-start(), calls=%async_computation.3 | async-start | bytes 2162688
Sparse Core Ops, SparseCore 0:
  9.2 68.8 all-gather.2
  80.8 186.6 all-gather.4
  304.7 81.8 all-reduce.2
  390.3 118.1 reduce-scatter.3
where the time goes:
time: 520 us; the launch traced here: 516 us
  waiting for transfers between devices  460 us (88%)
  matrix products  32.2 us (6%)
  between operations  13.3 us (3%)
  local copies, waits for them, and re-layouts  8.21 us (2%)
    unnamed x6, waiting for transfers between devices  200 us
    all_gather x1, waiting for transfers between devices, body(): piece = lax.all_gather(class_block, 'cls', axis=0, tiled=True)  189 us
    all_gather x1, waiting for transfers between devices, body(): class_block = lax.all_gather(references, 'ptl', axis=1, tiled=True)  70.8 us
    dot_general x7, matrix products, body(): moved = jnp.dot(coef, particles, preferred_element_type=jnp.float32)  18.4 us
    dot_general x1, matrix products, body(): lax.dot_general(particles, rows, (((1,), (1,)), ((), ())), preferred_elem...  13.8 us
  transfers between devices with their start and end apart: 4, of which 4 were waited for; matrix products, arithmetic and copies ran while one was open for 0% of the time, Pallas kernels for 0%

commit v1 on v0

v1 whole, which is shorter than its diff:
```python
import math

import jax
import jax.numpy as jnp
import numpy as np
from jax import lax
from jax.experimental import pallas as pl
from jax.experimental.pallas import tpu as pltpu
from jax.sharding import Mesh
from jax.sharding import PartitionSpec as P

NX = 64
SHIFT = 3
XH, YN, XL, ZN, CORES = 2, 4, 2, 8, 2
XN = XH * XL
ALL = ("xh", "y", "xl", "z", "core")
AX, AY, AZ = 0, 1, 2
SIZES = (XN, YN, ZN)
STAGES = ((AX, AY), (AY, AZ), (AZ, AX))


def flat_device(x, y, z, core):
    return (((x // XL * YN + y) * XL + x % XL) * ZN + z) * CORES + core


def pairs(move):
    out = []
    for x in range(XN):
        for y in range(YN):
            for z in range(ZN):
                for core in range(CORES):
                    (tx, ty, tz), tc = move([x, y, z], core)
                    out.append((flat_device(x, y, z, core), flat_device(tx % XN, ty % YN, tz % ZN, tc)))
    return out


def swap_cores(value):
    return lax.ppermute(value, ALL, pairs(lambda at, core: (at, 1 - core)))


class Piece:
    def __init__(self, rows, offsets):
        self.rows, self.offsets = rows, offsets

    def part(self, start, stop):
        return Piece(self.rows[start:stop], [o[start:stop] for o in self.offsets])

    def fetch(self, axes, steps):
        def move(at, core):
            at[axes[core]] -= steps
            return at, core

        moved = [o + steps * np.eye(4, dtype=np.int32)[axis] for o, axis in zip(self.offsets, axes)]
        return Piece(lax.ppermute(self.rows, ALL, pairs(move)), moved)


def join(pieces):
    return Piece(
        jnp.concatenate([p.rows for p in pieces], axis=0),
        [np.concatenate([p.offsets[c] for p in pieces], axis=0) for c in range(CORES)],
    )


def ring(piece, axes):
    half = piece.rows.shape[0] // 2
    ahead, behind = piece.fetch(axes, 1), piece.fetch(axes, -1)
    far_a = ahead.part(0, half).fetch(axes, 1)
    far_b = behind.part(half, 2 * half).fetch(axes, -1)
    return [piece, ahead, behind, far_a, far_b]


def row_ids(piece, here, local):
    core = here[3]
    d = jnp.where(core == 0, jnp.asarray(piece.offsets[0]), jnp.asarray(piece.offsets[1]))
    x, y, z = (here[0] + d[:, 0]) % XN, (here[1] + d[:, 1]) % YN, (here[2] + d[:, 2]) % ZN
    return flat_device(x, y, z, core) * local + d[:, 3]


def sums_kernel(key_ref, gain_ref, particles_ref, out_ref):
    steps = 2 * SHIFT + 1
    classes, width = out_ref.shape
    rows = lax.broadcasted_iota(jnp.int32, (steps * classes, key_ref.shape[1]), 0)
    coef = jnp.where(rows == key_ref[...], gain_ref[...], 0.0).astype(jnp.bfloat16)
    moved = jnp.dot(coef, particles_ref[...], preferred_element_type=jnp.float32)
    lane = lax.broadcasted_iota(jnp.int32, (classes, width), 1) % NX
    total = jnp.zeros((classes, width), jnp.float32)
    for k in range(steps):
        step = k - SHIFT
        part = moved[k * classes : (k + 1) * classes]
        if step == 0:
            total = total + part
            continue
        inside = (lane >= step) if step > 0 else (lane < NX + step)
        wrapped = step - NX if step > 0 else step + NX
        total = total + jnp.where(
            inside, pltpu.roll(part, step % width, 1), pltpu.roll(part, wrapped % width, 1)
        )
    out_ref[...] = total


def class_sums(key, gain, particles, classes):
    count, voxels = particles.shape
    width = 512
    return pl.pallas_call(
        sums_kernel,
        out_shape=jax.ShapeDtypeStruct((classes, voxels), jnp.float32),
        grid=(voxels // width,),
        in_specs=[
            pl.BlockSpec((1, count), lambda i: (0, 0)),
            pl.BlockSpec((1, count), lambda i: (0, 0)),
            pl.BlockSpec((count, width), lambda i: (0, i)),
        ],
        out_specs=pl.BlockSpec((classes, width), lambda i: (0, i)),
        name="class_sums",
    )(key, gain, particles)


def body(references, particles, class_ids, orient_ids, offsets, weights):
    per_owner, local, voxels = references.shape
    devices = XN * YN * ZN * CORES
    classes = per_owner * XH * YN
    orients = local * XL * ZN * CORES
    count = particles.shape[0]
    scale = 1.0 / math.sqrt(voxels)
    xh, y, xl, z, core = (lax.axis_index(a) for a in ALL)
    here = (xh * XL + xl, y, z, core)

    wanted = class_ids * orients + orient_ids
    other = swap_cores(particles)
    other_wanted = swap_cores(wanted.astype(jnp.float32)).astype(jnp.int32)

    start = np.zeros((local, 4), np.int32)
    start[:, 3] = np.arange(local)
    piece = Piece(references.reshape(local, voxels), [start, start])
    piece = join([piece, piece.fetch((AZ, AZ), ZN // 2)])
    first = STAGES[0]
    piece = join([piece, piece.fetch(first, 1), piece.fetch(first, -1), piece.fetch(first, 2)])
    piece = join(ring(piece, STAGES[1]))
    pieces = ring(piece, STAGES[2])

    def stats(part, ids, whose):
        scores = (
            lax.dot_general(
                part.rows, whose[0], (((1,), (1,)), ((), ())), preferred_element_type=jnp.float32
            )
            * scale
        )
        top = jnp.max(scores, axis=0)
        total = jnp.sum(jnp.exp(scores - top[None, :]), axis=0)
        chosen = jnp.sum(jnp.where(ids[:, None] == whose[1][None, :], scores, 0.0), axis=0)
        return top, total, chosen

    def merge(parts):
        tops = jnp.stack([p[0] for p in parts])
        totals = jnp.stack([p[1] for p in parts])
        chosen = jnp.stack([p[2] for p in parts])
        top = jnp.max(tops, axis=0)
        return top, jnp.sum(totals * jnp.exp(tops - top[None, :]), axis=0), jnp.sum(chosen, axis=0)

    mine, theirs = [], []
    for part in pieces:
        ids = row_ids(part, here, local)
        mine.append(stats(part, ids, (particles, wanted)))
        theirs.append(stats(part, ids, (other, other_wanted)))
    got = swap_cores(jnp.stack(merge(theirs)))
    top, total, chosen = merge([merge(mine), (got[0], got[1], got[2])])
    gain = (weights * (classes * orients) * jnp.exp(chosen - top) / total).astype(jnp.bfloat16)
    key = class_ids + classes * (offsets + SHIFT)
    partial_sums = class_sums(key[None, :], gain.astype(jnp.float32)[None, :], particles, classes)
    sent = partial_sums.reshape(devices, classes * voxels // devices)
    owned = jnp.sum(lax.all_to_all(sent, ALL, 0, 0, tiled=True), axis=0, keepdims=True)
    population = count * devices / classes
    return owned / jnp.sqrt(jnp.float32(population))


def solution(mesh):
    fine = Mesh(np.asarray(mesh.devices).reshape(XH, YN, XL, ZN, CORES), ALL)
    cls, ptl = ("xh", "y"), ("xl", "z", "core")
    placed = (P(cls, ptl, None), P(ALL, None), P(ALL), P(ALL), P(ALL), P(ALL))
    return jax.shard_map(
        body, mesh=fine, in_specs=placed, out_specs=P(cls, ptl), check_vma=False
    )
```

time: 520 us -> 158 us (0.30)
  waiting for transfers between devices: 460 us -> 35.3 us
  starting transfers between devices: 0.12 us -> 34.6 us
  blocking collectives: 0 us -> 21.5 us
  between operations: 13.3 us -> 0.4 us
  matrix products: 32.2 us -> 41.8 us
  Pallas kernels: 0 us -> 6.75 us
    all_gather x2 -> x0, waiting for transfers between devices: 259 us -> none  [the longest x1 189 us: body(): piece = lax.all_gather(class_block, 'cls', axis=0, tiled=True)]
    unnamed x6 -> x0, waiting for transfers between devices: 200 us -> none
    ppermute x0 -> x15, waiting for transfers between devices: none -> 35.3 us  [the longest x12 29.8 us: fetch(): return Piece(lax.ppermute(self.rows, ALL, pairs(move)), moved)]
    ppermute x0 -> x15, starting transfers between devices: none -> 34.6 us  [the longest x12 25.3 us: fetch(): return Piece(lax.ppermute(self.rows, ALL, pairs(move)), moved)]
    all_to_all x0 -> x1, blocking collectives: none -> 21.5 us  [body(): lax.all_to_all(sent, ALL, 0, 0, tiled=True)]
    dot_general x8 -> x10, matrix products: 32.2 us -> 41.8 us  [stats(): lax.dot_general(part.rows, whose[0], (((1,), (1,)), ((), ())), preferred_...]
    pallas_call x0 -> x1, Pallas kernels: none -> 6.75 us  [class_sums(): pl.pallas_call(sums_kernel, out_shape=jax.ShapeDtypeStruct((classes, voxe...]
  transfers between devices with their start and end apart: 4 -> 15, of which waited for: 4 -> 9; matrix products, arithmetic and copies ran while one was open for 0% -> 19% of each run, Pallas kernels for 0% -> 0%
where the time goes in v1:
time: 158 us; the launch traced here: 157 us
  matrix products  41.8 us (26%)
  waiting for transfers between devices  35.3 us (22%)
  starting transfers between devices  34.6 us (22%)
  blocking collectives  21.5 us (14%)
  local copies, waits for them, and re-layouts  11.4 us (7%)
  Pallas kernels  6.75 us (4%)
  other arithmetic  5.44 us (3%)
    dot_general x10, matrix products, stats(): lax.dot_general(part.rows, whose[0], (((1,), (1,)), ((), ())), preferred_...  41.8 us
    ppermute x12, waiting for transfers between devices, fetch(): return Piece(lax.ppermute(self.rows, ALL, pairs(move)), moved)  29.8 us
    ppermute x12, starting transfers between devices, fetch(): return Piece(lax.ppermute(self.rows, ALL, pairs(move)), moved)  25.3 us
    all_to_all x1, blocking collectives, body(): lax.all_to_all(sent, ALL, 0, 0, tiled=True)  21.5 us
    ppermute x3, starting transfers between devices, swap_cores(): return lax.ppermute(value, ALL, pairs(lambda at, core: (at, 1 - core)))  9.34 us
    unnamed x45, local copies, waits for them, and re-layouts  7.37 us
    pallas_call x1, Pallas kernels, class_sums(): pl.pallas_call(sums_kernel, out_shape=jax.ShapeDtypeStruct((classes, voxe...  6.75 us
    ppermute x3, waiting for transfers between devices, swap_cores(): return lax.ppermute(value, ALL, pairs(lambda at, core: (at, 1 - core)))  5.5 us
  transfers between devices with their start and end apart: 15, of which 9 were waited for; matrix products, arithmetic and copies ran while one was open for 19% of the time, Pallas kernels for 0%

profile of v1, /device:TPU:1, one launch (start us, length us, event | category | flops | bytes accessed | tf_op | source)
XLA Modules:
  0.0 157.2 jit_solution(14672224055082212639)
XLA Ops:
  0.0 7.7 %collective-permute-start = (bf16[8,4096]{1,0:T(8,128)(2,1)}, bf16[8,4096]{1,0:T(8,128)(2,1)S(1)}, u32[]{:S(2)}, u32[]{:S(2)}) collective-permute-start(bf16[8,4096]{1,0:T(8,128)(2,1)} %bitcast.62), channel_id=1, source_target_pairs={{0,8},{1,9},{2,10},{3,11},{4,12},{5,13},{6,14},{7,15},{8,0},{9,1},... | collective-permute-start | bytes 196616 | tf_op jit(solution)/shard_map/ppermute | solution.py:54
  7.7 1.5 constant_dynamic-update-slice_fusion.4
  9.3 0.5 collective-permute-done
  9.7 0.8 pad_maximum_fusion
  10.6 2.8 %collective-permute-start.1 = (bf16[16,4096]{1,0:T(8,128)(2,1)S(1)}, bf16[16,4096]{1,0:T(8,128)(2,1)S(1)}, u32[]{:S(2)}, u32[]{:S(2)}) collective-permute-start(bf16[16,4096]{1,0:T(8,128)(2,1)S(1)} %pad_maximum_fusion), channel_id=1, source_target_pairs={{0,144},{1,97},{2,146},{3,99},{4,148},{5,101},{6,150},{7,103},{8,1... | collective-permute-start | bytes 393224 | tf_op jit(solution)/shard_map/ppermute | solution.py:54
  13.4 1.6 %collective-permute-start.3 = (bf16[16,4096]{1,0:T(8,128)(2,1)S(1)}, bf16[16,4096]{1,0:T(8,128)(2,1)S(1)}, u32[]{:S(2)}, u32[]{:S(2)}) collective-permute-start(bf16[16,4096]{1,0:T(8,128)(2,1)S(1)} %pad_maximum_fusion), channel_id=1, source_target_pairs={{0,128},{1,65},{2,130},{3,67},{4,132},{5,69},{6,134},{7,71},{8,136... | collective-permute-start | bytes 393224 | tf_op jit(solution)/shard_map/ppermute | solution.py:54
  15.0 0.6 constant_dynamic-update-slice_fusion.3
  15.6 0.7 constant_dynamic-update-slice_fusion.2
  16.3 3.8 %collective-permute-done.2 = bf16[16,4096]{1,0:T(8,128)(2,1)S(1)} collective-permute-done((bf16[16,4096]{1,0:T(8,128)(2,1)S(1)}, bf16[16,4096]{1,0:T(8,128)(2,1)S(1)}, u32[]{:S(2)}, u32[]{:S(2)}) %collective-permute-start.2) | collective-permute-done | bytes 131104 | tf_op jit(solution)/shard_map/ppermute | solution.py:54
  20.1 0.7 constant_dynamic-update-slice_fusion.1
  20.8 0.7 constant_dynamic-update-slice_fusion
  21.5 4.5 %collective-permute-start.4 = (bf16[64,4096]{1,0:T(8,128)(2,1)S(1)}, bf16[64,4096]{1,0:T(8,128)(2,1)S(1)}, u32[]{:S(2)}, u32[]{:S(2)}) collective-permute-start(bf16[64,4096]{1,0:T(8,128)(2,1)S(1)} %get-tuple-element.45), channel_id=1, source_target_pairs={{0,96},{1,15},{2,98},{3,1},{4,100},{5,3},{6,102},{7,5},{8,104},{9,... | collective-permute-start | bytes 1572872 | tf_op jit(solution)/shard_map/ppermute | solution.py:54
  26.0 6.1 %collective-permute-done.4 = bf16[64,4096]{1,0:T(8,128)(2,1)S(1)} collective-permute-done((bf16[64,4096]{1,0:T(8,128)(2,1)S(1)}, bf16[64,4096]{1,0:T(8,128)(2,1)S(1)}, u32[]{:S(2)}, u32[]{:S(2)}) %collective-permute-start.4) | collective-permute-done | bytes 524320 | tf_op jit(solution)/shard_map/ppermute | solution.py:54
  32.2 3.2 %collective-permute-start.6 = (bf16[32,4096]{1,0:T(8,128)(2,1)S(1)}, bf16[32,4096]{1,0:T(8,128)(2,1)S(1)}, u32[]{:S(2)}, u32[]{:S(2)}) collective-permute-start(bf16[32,4096]{1,0:T(8,128)(2,1)S(1)} %slice.112), channel_id=1, source_target_pairs={{0,96},{1,15},{2,98},{3,1},{4,100},{5,3},{6,102},{7,5},{8,104},{9,... | collective-permute-start | bytes 786440 | tf_op jit(solution)/shard_map/ppermute | solution.py:54
  35.7 0.9 constant_dynamic-update-slice_fusion.8
  36.6 0.8 constant_dynamic-update-slice_fusion.7
  37.4 1.3 collective-permute-done.6
  38.7 0.7 constant_dynamic-update-slice_fusion.6
  39.4 3.0 %collective-permute-done.7 = bf16[32,4096]{1,0:T(8,128)(2,1)S(1)} collective-permute-done((bf16[32,4096]{1,0:T(8,128)(2,1)S(1)}, bf16[32,4096]{1,0:T(8,128)(2,1)S(1)}, u32[]{:S(2)}, u32[]{:S(2)}) %collective-permute-start.7) | collective-permute-done | bytes 262176 | tf_op jit(solution)/shard_map/ppermute | solution.py:54
  42.4 0.7 constant_dynamic-update-slice_fusion.5
  43.1 1.2 collective-permute-start.9
  44.3 3.7 %collective-permute-start.12 = (bf16[512,4096]{1,0:T(8,128)(2,1)}, bf16[512,4096]{1,0:T(8,128)(2,1)}, u32[]{:S(2)}, u32[]{:S(2)}) collective-permute-start(bf16[512,4096]{1,0:T(8,128)(2,1)} %particles_ref.1), channel_id=1, source_target_pairs={{0,1},{1,0},{2,3},{3,2},{4,5},{5,4},{6,7},{7,6},{8,9},{9,8},{10,11... | collective-permute-start | bytes 12582920 | tf_op jit(solution)/shard_map/ppermute | solution.py:38
  48.0 0.6 fusion.34
  48.6 1.2 collective-permute-start.8
  50.0 4.7 %collective-permute-done.13 = f32[512]{0:T(512)S(1)} collective-permute-done((f32[512]{0:T(512)S(1)}, f32[512]{0:T(512)S(1)}, u32[]{:S(2)}, u32[]{:S(2)}) %collective-permute-start.13) | collective-permute-done | bytes 2080 | tf_op jit(solution)/shard_map/ppermute | solution.py:38
  54.7 15.0 %collective-permute-done.9 = bf16[256,4096]{1,0:T(8,128)(2,1)S(1)} collective-permute-done((bf16[256,4096]{1,0:T(8,128)(2,1)}, bf16[256,4096]{1,0:T(8,128)(2,1)S(1)}, u32[]{:S(2)}, u32[]{:S(2)}) %collective-permute-start.9) | collective-permute-done | bytes 2097184 | tf_op jit(solution)/shard_map/ppermute | solution.py:54
  69.7 1.3 copy-done.2
  71.3 4.1 %fusion.40 = (f32[512]{0:T(512)S(1)}, f32[256,512]{1,0:T(8,128)S(1)}) fusion(bf16[256,4096]{1,0:T(8,128)(2,1)} %constant_dynamic-update-slice_fusion.5, bf16[512,4096]{1,0:T(8,128)(2,1)} %particles_ref.1), kind=kOutput, calls=%fused_computation.189 | convolution fusion | flops 1074003456 | bytes 6817792 | tf_op jit(solution)/shard_map/dot_general | solution.py:143
  75.4 1.5 slice.122
  76.9 2.9 %collective-permute-start.10 = (bf16[128,4096]{1,0:T(8,128)(2,1)S(1)}, bf16[128,4096]{1,0:T(8,128)(2,1)S(1)}, u32[]{:S(2)}, u32[]{:S(2)}) collective-permute-start(bf16[128,4096]{1,0:T(8,128)(2,1)S(1)} %slice.122), channel_id=1, source_target_pairs={{0,14},{1,145},{2,0},{3,147},{4,2},{5,149},{6,4},{7,151},{8,6},{9,... | collective-permute-start | bytes 3145736 | tf_op jit(solution)/shard_map/ppermute | solution.py:54
  79.8 4.3 %fusion.41 = (f32[512]{0:T(512)S(1)}, f32[256,512]{1,0:T(8,128)}) fusion(bf16[256,4096]{1,0:T(8,128)(2,1)S(1)} %copy-done.3, bf16[512,4096]{1,0:T(8,128)(2,1)} %particles_ref.1), kind=kOutput, calls=%fused_computation.190 | convolution fusion | flops 1074003456 | bytes 6817792 | tf_op jit(solution)/shard_map/dot_general | solution.py:143
  84.1 4.9 %fusion.42 = (f32[512]{0:T(512)S(1)}, f32[256,512]{1,0:T(8,128)}) fusion(bf16[256,4096]{1,0:T(8,128)(2,1)} %collective-permute-done.8, bf16[512,4096]{1,0:T(8,128)(2,1)} %particles_ref.1), kind=kOutput, calls=%fused_computation.191 | convolution fusion | flops 1074003456 | bytes 6817792 | tf_op jit(solution)/shard_map/dot_general | solution.py:143
  89.0 3.7 %fusion.36 = (f32[512]{0:T(512)S(1)}, f32[128,512]{1,0:T(8,128)S(1)}) fusion(bf16[128,4096]{1,0:T(8,128)(2,1)S(1)} %collective-permute-done.11, bf16[512,4096]{1,0:T(8,128)(2,1)} %particles_ref.1), kind=kOutput, calls=%fused_computation.185 | convolution fusion | flops 537001472 | bytes 5507072 | tf_op jit(solution)/shard_map/dot_general | solution.py:143
  92.7 3.7 %fusion.37 = (f32[512]{0:T(512)S(1)}, f32[128,512]{1,0:T(8,128)S(1)}) fusion(bf16[128,4096]{1,0:T(8,128)(2,1)S(1)} %collective-permute-done.10, bf16[512,4096]{1,0:T(8,128)(2,1)} %particles_ref.1), kind=kOutput, calls=%fused_computation.186 | convolution fusion | flops 537001472 | bytes 5507072 | tf_op jit(solution)/shard_map/dot_general | solution.py:143
  96.5 3.7 %fusion.35 = (f32[512]{0:T(512)S(1)}, f32[128,512]{1,0:T(8,128)S(1)}) fusion(bf16[128,4096]{1,0:T(8,128)(2,1)S(1)} %collective-permute-done.10, bf16[512,4096]{1,0:T(8,128)(2,1)} %collective-permute-done.12), kind=kOutput, calls=%fused_computation.184 | convolution fusion | flops 537001472 | bytes 5507072 | tf_op jit(solution)/shard_map/dot_general | solution.py:143
  100.3 3.7 %fusion.38 = (f32[512]{0:T(512)S(1)}, f32[128,512]{1,0:T(8,128)S(1)}) fusion(bf16[128,4096]{1,0:T(8,128)(2,1)S(1)} %collective-permute-done.11, bf16[512,4096]{1,0:T(8,128)(2,1)} %collective-permute-done.12), kind=kOutput, calls=%fused_computation.187 | convolution fusion | flops 537001472 | bytes 5507072 | tf_op jit(solution)/shard_map/dot_general | solution.py:143
  104.0 4.3 %fusion.39 = (f32[512]{0:T(512)S(1)}, f32[256,512]{1,0:T(8,128)S(1)}) fusion(bf16[256,4096]{1,0:T(8,128)(2,1)} %collective-permute-done.8, bf16[512,4096]{1,0:T(8,128)(2,1)} %collective-permute-done.12), kind=kOutput, calls=%fused_computation.188 | convolution fusion | flops 1074003456 | bytes 6817792 | tf_op jit(solution)/shard_map/dot_general | solution.py:143
  108.3 4.3 %fusion.43 = (f32[512]{0:T(512)S(1)}, f32[256,512]{1,0:T(8,128)}) fusion(bf16[256,4096]{1,0:T(8,128)(2,1)S(1)} %copy-done.4, bf16[512,4096]{1,0:T(8,128)(2,1)} %collective-permute-done.12), kind=kOutput, calls=%fused_computation.192 | convolution fusion | flops 1074003456 | bytes 6817792 | tf_op jit(solution)/shard_map/dot_general | solution.py:143
  112.6 5.0 %fusion.44 = (f32[512]{0:T(512)S(1)}, f32[256,512]{1,0:T(8,128)}) fusion(bf16[256,4096]{1,0:T(8,128)(2,1)} %constant_dynamic-update-slice_fusion.5, bf16[512,4096]{1,0:T(8,128)(2,1)} %collective-permute-done.12), kind=kOutput, calls=%fused_computation.193 | convolution fusion | flops 1074003456 | bytes 6817792 | tf_op jit(solution)/shard_map/dot_general | solution.py:143
  117.6 0.3 exponential_reduce_fusion.9
  118.0 2.0 %exponential_reduce_fusion.4 = (f32[512]{0:T(512)S(1)}, f32[512]{0:T(512)S(1)}, f32[512]{0:T(512)S(1)}, f32[512]{0:T(512)S(1)}, f32[512]{0:T(512)S(1)}, /*index=...) fusion(f32[256,512]{1,0:T(8,128)S(1)} %get-tuple-element.74, ...), kind=kLoop, calls=%fused_computation.17 | loop fusion | flops 3926016 | bytes 3189760 | tf_op jit(solution)/shard_map/reduce_sum | solution.py:149
  120.1 5.7 %collective-permute-start.14 = (f32[3,512]{1,0:T(4,128)S(1)}, f32[3,512]{1,0:T(4,128)S(1)}, u32[]{:S(2)}, u32[]{:S(2)}) collective-permute-start(f32[3,512]{1,0:T(4,128)S(1)} %pad_maximum_fusion.1), channel_id=1, source_target_pairs={{0,1},{1,0},{2,3},{3,2},{4,5},{5,4},{6,7},{7,6},{8,9},{9,8},{10,11... | collective-permute-start | bytes 18440 | tf_op jit(solution)/shard_map/ppermute | solution.py:38
  125.8 0.8 collective-permute-done.14
  126.6 0.6 fusion.21
  127.2 6.8 %class_sums.1 = f32[8,4096]{1,0:T(8,128)} custom-call(s32[1,512]{1,0:T(1,128)} %bitcast.85, f32[1,512]{1,0:T(1,128)} %bitcast.86, bf16[512,4096]{1,0:T(8,128)(2,1)} %particles_ref.1), custom_call_target="tpu_custom_call" | custom-call | tf_op jit(solution)/shard_map/class_sums/pallas_call | solution.py:104
  134.0 0.9 all_to_all.6
  134.9 21.5 %all_to_all.9 = f32[256,1,128]{2,1,0:T(1,128)S(1)} all-to-all(f32[256,1,128]{2,1,0:T(1,128)S(1)} %bitcast.61), channel_id=1, replica_groups=mesh['xh'=2,'y'=4,'xl'=2,'z'=8,'core'=2] {'xh','y','xl','z','core'}, dimensions={0} | all-to-all | bytes 262144 | tf_op jit(solution)/shard_map/all_to_all | solution.py:171
  156.7 0.5 multiply_bitcast_fusion
  (75 shorter events, 1.3 us)
Async XLA Ops:
  0.0 9.7 %collective-permute-start = (bf16[8,4096]{1,0:T(8,128)(2,1)}, bf16[8,4096]{1,0:T(8,128)(2,1)S(1)}, u32[]{:S(2)}, u32[]{:S(2)}) collective-permute-start(bf16[8,4096]{1,0:T(8,128)(2,1)} %bitcast.62), channel_id=1, source_target_pairs={{0,8},{1,9},{2,10},{3,11},{4,12},{5,13},{6,14},{7,15},{8,0},{9,1},... | collective-permute-start | bytes 196616 | tf_op jit(solution)/shard_map/ppermute | solution.py:54
  10.6 5.1 %collective-permute-start.1 = (bf16[16,4096]{1,0:T(8,128)(2,1)S(1)}, bf16[16,4096]{1,0:T(8,128)(2,1)S(1)}, u32[]{:S(2)}, u32[]{:S(2)}) collective-permute-start(bf16[16,4096]{1,0:T(8,128)(2,1)S(1)} %pad_maximum_fusion), channel_id=1, source_target_pairs={{0,144},{1,97},{2,146},{3,99},{4,148},{5,101},{6,150},{7,103},{8,1... | collective-permute-start | bytes 393224 | tf_op jit(solution)/shard_map/ppermute | solution.py:54
  13.4 6.7 %collective-permute-start.2 = (bf16[16,4096]{1,0:T(8,128)(2,1)S(1)}, bf16[16,4096]{1,0:T(8,128)(2,1)S(1)}, u32[]{:S(2)}, u32[]{:S(2)}) collective-permute-start(bf16[16,4096]{1,0:T(8,128)(2,1)S(1)} %pad_maximum_fusion), channel_id=1, source_target_pairs={{0,16},{1,33},{2,18},{3,35},{4,20},{5,37},{6,22},{7,39},{8,24},{9,... | collective-permute-start | bytes 393224 | tf_op jit(solution)/shard_map/ppermute | solution.py:54
  13.4 7.4 %collective-permute-start.3 = (bf16[16,4096]{1,0:T(8,128)(2,1)S(1)}, bf16[16,4096]{1,0:T(8,128)(2,1)S(1)}, u32[]{:S(2)}, u32[]{:S(2)}) collective-permute-start(bf16[16,4096]{1,0:T(8,128)(2,1)S(1)} %pad_maximum_fusion), channel_id=1, source_target_pairs={{0,128},{1,65},{2,130},{3,67},{4,132},{5,69},{6,134},{7,71},{8,136... | collective-permute-start | bytes 393224 | tf_op jit(solution)/shard_map/ppermute | solution.py:54
  21.4 26.5 %copy-start.15 = (s32[512]{0:T(512)S(1)}, s32[512]{0:T(512)}, u32[]{:S(2)}) copy-start(s32[512]{0:T(512)} %param.19) | copy-start | bytes 6148
  21.4 26.5 %copy-start.16 = (s32[512]{0:T(512)S(1)}, s32[512]{0:T(512)}, u32[]{:S(2)}) copy-start(s32[512]{0:T(512)} %param.18) | copy-start | bytes 6148
  21.4 26.5 %copy-start.17 = (s32[512]{0:T(512)S(1)}, s32[512]{0:T(512)}, u32[]{:S(2)}) copy-start(s32[512]{0:T(512)} %param.20) | copy-start | bytes 6148
  21.4 28.3 %copy-start.9 = (s32[256,4]{0,1:T(4,128)S(1)}, s32[256,4]{0,1:T(4,128)}, u32[]{:S(2)}) copy-start(s32[256,4]{0,1:T(4,128)} %constant.230.clone) | copy-start | bytes 12292
  21.4 28.3 %copy-start.10 = (s32[256,4]{0,1:T(4,128)S(1)}, s32[256,4]{0,1:T(4,128)}, u32[]{:S(2)}) copy-start(s32[256,4]{0,1:T(4,128)} %constant.231.clone) | copy-start | bytes 12292
  21.4 28.4 %copy-start.13 = (s32[128,4]{0,1:T(4,128)S(1)}, s32[128,4]{0,1:T(4,128)}, u32[]{:S(2)}) copy-start(s32[128,4]{0,1:T(4,128)} %constant.238.clone) | copy-start | bytes 6148
  21.5 28.3 %copy-start.14 = (s32[128,4]{0,1:T(4,128)S(1)}, s32[128,4]{0,1:T(4,128)}, u32[]{:S(2)}) copy-start(s32[128,4]{0,1:T(4,128)} %constant.239.clone) | copy-start | bytes 6148
  21.5 28.4 %copy-start.11 = (s32[128,4]{0,1:T(4,128)S(1)}, s32[128,4]{0,1:T(4,128)}, u32[]{:S(2)}) copy-start(s32[128,4]{0,1:T(4,128)} %constant.236.clone) | copy-start | bytes 6148
  21.5 28.4 %copy-start.12 = (s32[128,4]{0,1:T(4,128)S(1)}, s32[128,4]{0,1:T(4,128)}, u32[]{:S(2)}) copy-start(s32[128,4]{0,1:T(4,128)} %constant.237.clone) | copy-start | bytes 6148
  21.5 28.4 %copy-start.7 = (s32[256,4]{0,1:T(4,128)S(1)}, s32[256,4]{0,1:T(4,128)}, u32[]{:S(2)}) copy-start(s32[256,4]{0,1:T(4,128)} %constant.234.clone) | copy-start | bytes 12292
  21.5 28.4 %copy-start.8 = (s32[256,4]{0,1:T(4,128)S(1)}, s32[256,4]{0,1:T(4,128)}, u32[]{:S(2)}) copy-start(s32[256,4]{0,1:T(4,128)} %constant.235.clone) | copy-start | bytes 12292
  21.5 28.4 %copy-start.5 = (s32[256,4]{0,1:T(4,128)S(1)}, s32[256,4]{0,1:T(4,128)}, u32[]{:S(2)}) copy-start(s32[256,4]{0,1:T(4,128)} %constant.232.clone) | copy-start | bytes 12292
  21.5 28.4 %copy-start.6 = (s32[256,4]{0,1:T(4,128)S(1)}, s32[256,4]{0,1:T(4,128)}, u32[]{:S(2)}) copy-start(s32[256,4]{0,1:T(4,128)} %constant.233.clone) | copy-start | bytes 12292
  21.5 10.6 %collective-permute-start.4 = (bf16[64,4096]{1,0:T(8,128)(2,1)S(1)}, bf16[64,4096]{1,0:T(8,128)(2,1)S(1)}, u32[]{:S(2)}, u32[]{:S(2)}) collective-permute-start(bf16[64,4096]{1,0:T(8,128)(2,1)S(1)} %get-tuple-element.45), channel_id=1, source_target_pairs={{0,96},{1,15},{2,98},{3,1},{4,100},{5,3},{6,102},{7,5},{8,104},{9,... | collective-permute-start | bytes 1572872 | tf_op jit(solution)/shard_map/ppermute | solution.py:54
  26.0 9.5 %collective-permute-start.5 = (bf16[64,4096]{1,0:T(8,128)(2,1)S(1)}, bf16[64,4096]{1,0:T(8,128)(2,1)S(1)}, u32[]{:S(2)}, u32[]{:S(2)}) collective-permute-start(bf16[64,4096]{1,0:T(8,128)(2,1)S(1)} %get-tuple-element.45), channel_id=1, source_target_pairs={{0,32},{1,3},{2,34},{3,5},{4,36},{5,7},{6,38},{7,9},{8,40},{9,11},... | collective-permute-start | bytes 1572872 | tf_op jit(solution)/shard_map/ppermute | solution.py:54
  32.2 6.5 %collective-permute-start.6 = (bf16[32,4096]{1,0:T(8,128)(2,1)S(1)}, bf16[32,4096]{1,0:T(8,128)(2,1)S(1)}, u32[]{:S(2)}, u32[]{:S(2)}) collective-permute-start(bf16[32,4096]{1,0:T(8,128)(2,1)S(1)} %slice.112), channel_id=1, source_target_pairs={{0,96},{1,15},{2,98},{3,1},{4,100},{5,3},{6,102},{7,5},{8,104},{9,... | collective-permute-start | bytes 786440 | tf_op jit(solution)/shard_map/ppermute | solution.py:54
  35.6 6.8 %collective-permute-start.7 = (bf16[32,4096]{1,0:T(8,128)(2,1)S(1)}, bf16[32,4096]{1,0:T(8,128)(2,1)S(1)}, u32[]{:S(2)}, u32[]{:S(2)}) collective-permute-start(bf16[32,4096]{1,0:T(8,128)(2,1)S(1)} %slice.113), channel_id=1, source_target_pairs={{0,32},{1,3},{2,34},{3,5},{4,36},{5,7},{6,38},{7,9},{8,40},{9,11},... | collective-permute-start | bytes 786440 | tf_op jit(solution)/shard_map/ppermute | solution.py:54
  43.1 26.6 %collective-permute-start.9 = (bf16[256,4096]{1,0:T(8,128)(2,1)}, bf16[256,4096]{1,0:T(8,128)(2,1)S(1)}, u32[]{:S(2)}, u32[]{:S(2)}) collective-permute-start(bf16[256,4096]{1,0:T(8,128)(2,1)} %constant_dynamic-update-slice_fusion.5), channel_id=1, source_target_pairs={{0,2},{1,17},{2,4},{3,19},{4,6},{5,21},{6,8},{7,23},{8,10},{9,25},... | collective-permute-start | bytes 6291464 | tf_op jit(solution)/shard_map/ppermute | solution.py:54
  44.3 52.2 %collective-permute-start.12 = (bf16[512,4096]{1,0:T(8,128)(2,1)}, bf16[512,4096]{1,0:T(8,128)(2,1)}, u32[]{:S(2)}, u32[]{:S(2)}) collective-permute-start(bf16[512,4096]{1,0:T(8,128)(2,1)} %particles_ref.1), channel_id=1, source_target_pairs={{0,1},{1,0},{2,3},{3,2},{4,5},{5,4},{6,7},{7,6},{8,9},{9,8},{10,11... | collective-permute-start | bytes 12582920 | tf_op jit(solution)/shard_map/ppermute | solution.py:38
  48.5 6.2 %collective-permute-start.13 = (f32[512]{0:T(512)S(1)}, f32[512]{0:T(512)S(1)}, u32[]{:S(2)}, u32[]{:S(2)}) collective-permute-start(f32[512]{0:T(512)S(1)} %get-tuple-element.43), channel_id=1, source_target_pairs={{0,1},{1,0},{2,3},{3,2},{4,5},{5,4},{6,7},{7,6},{8,9},{9,8},{10,11... | collective-permute-start | bytes 6152 | tf_op jit(solution)/shard_map/ppermute | solution.py:38
  48.6 26.8 %collective-permute-start.8 = (bf16[256,4096]{1,0:T(8,128)(2,1)}, bf16[256,4096]{1,0:T(8,128)(2,1)}, u32[]{:S(2)}, u32[]{:S(2)}) collective-permute-start(bf16[256,4096]{1,0:T(8,128)(2,1)} %constant_dynamic-update-slice_fusion.5), channel_id=1, source_target_pairs={{0,14},{1,145},{2,0},{3,147},{4,2},{5,149},{6,4},{7,151},{8,6},{9,... | collective-permute-start | bytes 6291464 | tf_op jit(solution)/shard_map/ppermute | solution.py:54
  69.7 1.3 copy-start.2
  71.1 17.8 %collective-permute-start.11 = (bf16[128,4096]{1,0:T(8,128)(2,1)S(1)}, bf16[128,4096]{1,0:T(8,128)(2,1)S(1)}, u32[]{:S(2)}, u32[]{:S(2)}) collective-permute-start(bf16[128,4096]{1,0:T(8,128)(2,1)S(1)} %slice.123), channel_id=1, source_target_pairs={{0,2},{1,17},{2,4},{3,19},{4,6},{5,21},{6,8},{7,23},{8,10},{9,25},... | collective-permute-start | bytes 3145736 | tf_op jit(solution)/shard_map/ppermute | solution.py:54
  75.4 4.4 %copy-start.3 = (bf16[256,4096]{1,0:T(8,128)(2,1)S(1)}, bf16[256,4096]{1,0:T(8,128)(2,1)}, u32[]{:S(2)}) copy-start(bf16[256,4096]{1,0:T(8,128)(2,1)} %copy-done.2) | copy-start | bytes 6291460
  76.9 15.8 %collective-permute-start.10 = (bf16[128,4096]{1,0:T(8,128)(2,1)S(1)}, bf16[128,4096]{1,0:T(8,128)(2,1)S(1)}, u32[]{:S(2)}, u32[]{:S(2)}) collective-permute-start(bf16[128,4096]{1,0:T(8,128)(2,1)S(1)} %slice.122), channel_id=1, source_target_pairs={{0,14},{1,145},{2,0},{3,147},{4,2},{5,149},{6,4},{7,151},{8,6},{9,... | collective-permute-start | bytes 3145736 | tf_op jit(solution)/shard_map/ppermute | solution.py:54
  104.0 4.3 %copy-start.4 = (bf16[256,4096]{1,0:T(8,128)(2,1)S(1)}, bf16[256,4096]{1,0:T(8,128)(2,1)}, u32[]{:S(2)}) copy-start(bf16[256,4096]{1,0:T(8,128)(2,1)} %copy-done.2) | copy-start | bytes 6291460
  112.6 5.4 %copy-start = (f32[256,512]{1,0:T(8,128)S(1)}, f32[256,512]{1,0:T(8,128)}, u32[]{:S(2)}) copy-start(f32[256,512]{1,0:T(8,128)} %get-tuple-element.78) | copy-start | bytes 1572868
  112.6 5.4 %copy-start.1 = (f32[256,512]{1,0:T(8,128)S(1)}, f32[256,512]{1,0:T(8,128)}, u32[]{:S(2)}) copy-start(f32[256,512]{1,0:T(8,128)} %get-tuple-element.80) | copy-start | bytes 1572868
  117.6 9.0 %copy-start.18 = (f32[512]{0:T(512)S(1)}, f32[512]{0:T(512)}, u32[]{:S(2)}) copy-start(f32[512]{0:T(512)} %param.21) | copy-start | bytes 6148
  120.1 6.5 %collective-permute-start.14 = (f32[3,512]{1,0:T(4,128)S(1)}, f32[3,512]{1,0:T(4,128)S(1)}, u32[]{:S(2)}, u32[]{:S(2)}) collective-permute-start(f32[3,512]{1,0:T(4,128)S(1)} %pad_maximum_fusion.1), channel_id=1, source_target_pairs={{0,1},{1,0},{2,3},{3,2},{4,5},{5,4},{6,7},{7,6},{8,9},{9,8},{10,11... | collective-permute-start | bytes 18440 | tf_op jit(solution)/shard_map/ppermute | solution.py:38

commit v2 on v1

v2 whole, which is shorter than its diff:
```python
import functools
import math

import jax
import jax.numpy as jnp
import numpy as np
from jax import lax
from jax.experimental import pallas as pl
from jax.experimental.pallas import tpu as pltpu
from jax.sharding import Mesh
from jax.sharding import PartitionSpec as P

NX = 64
SHIFT = 3
XH, YN, XL, ZN, CORES = 2, 4, 2, 8, 2
XN = XH * XL
ALL = ("xh", "y", "xl", "z", "core")
AX, AY, AZ = 0, 1, 2
SIZES = (XN, YN, ZN)
STAGES = ((AX, AY), (AY, AZ), (AZ, AX))


def flat_device(x, y, z, core):
    return (((x // XL * YN + y) * XL + x % XL) * ZN + z) * CORES + core


def pairs(move):
    out = []
    for x in range(XN):
        for y in range(YN):
            for z in range(ZN):
                for core in range(CORES):
                    (tx, ty, tz), tc = move([x, y, z], core)
                    out.append((flat_device(x, y, z, core), flat_device(tx % XN, ty % YN, tz % ZN, tc)))
    return out


def swap_cores(value):
    return lax.ppermute(value, ALL, pairs(lambda at, core: (at, 1 - core)))


class Piece:
    def __init__(self, rows, offsets):
        self.rows, self.offsets = rows, offsets

    def part(self, start, stop):
        return Piece(self.rows[start:stop], [o[start:stop] for o in self.offsets])

    def fetch(self, axes, steps):
        def move(at, core):
            at[axes[core]] -= steps
            return at, core

        moved = [o + steps * np.eye(4, dtype=np.int32)[axis] for o, axis in zip(self.offsets, axes)]
        return Piece(lax.ppermute(self.rows, ALL, pairs(move)), moved)


def join(pieces):
    return Piece(
        jnp.concatenate([p.rows for p in pieces], axis=0),
        [np.concatenate([p.offsets[c] for p in pieces], axis=0) for c in range(CORES)],
    )


def ring(piece, axes):
    half = piece.rows.shape[0] // 2
    ahead, behind = piece.fetch(axes, 1), piece.fetch(axes, -1)
    far_a = ahead.part(0, half).fetch(axes, 1)
    far_b = behind.part(half, 2 * half).fetch(axes, -1)
    return [piece, ahead, behind, far_a, far_b]


def row_ids(pieces, here, local):
    packed = []
    for core in range(CORES):
        d = np.concatenate([p.offsets[core] for p in pieces], axis=0)
        x, y, z = d[:, 0] % XN, d[:, 1] % YN, d[:, 2] % ZN
        packed.append((((x * YN + y) * ZN + z) * local + d[:, 3]).astype(np.int32))
    d = jnp.where(here[3] == 0, jnp.asarray(packed[0]), jnp.asarray(packed[1]))
    r, d = d % local, d // local
    z, d = (here[2] + d % ZN) % ZN, d // ZN
    y, x = (here[1] + d % YN) % YN, (here[0] + d // YN) % XN
    return (flat_device(x, y, z, here[3]) * local + r).astype(jnp.float32)[None, :]


LANES = 128
BLOCK = 256


def score_kernel(scale, n, first, ids_ref, wanted_ref, other_wanted_ref, own_ref, other_ref, *refs):
    pieces, refs = refs[:n], refs[n:]
    before, after = (None, None) if first else refs[:2], refs[-2:]
    count = own_ref.shape[0]
    ids, at = [], 0
    for piece in pieces:
        rows = piece.shape[0]
        column = jnp.broadcast_to(ids_ref[0:1, at : at + rows], (LANES, rows)).T
        ids.append(jnp.concatenate([column] * (BLOCK // LANES), axis=1))
        at += rows
    for side, (particles, wanted) in enumerate(((own_ref, wanted_ref), (other_ref, other_wanted_ref))):
        for start in range(0, count, BLOCK):
            cols = slice(start, start + BLOCK)
            block = particles[cols, :]
            want = wanted[0:1, cols]
            scores = [
                lax.dot_general(
                    piece[...], block, (((1,), (1,)), ((), ())), preferred_element_type=jnp.float32
                )
                * scale
                for piece in pieces
            ]
            top = functools.reduce(jnp.maximum, [jnp.max(s, axis=0, keepdims=True) for s in scores])
            if not first:
                old_top = before[side][0:1, cols]
                top = jnp.maximum(top, old_top)
            total = sum(jnp.sum(jnp.exp(s - top), axis=0, keepdims=True) for s in scores)
            chosen = sum(
                jnp.sum(jnp.where(i == want, s, 0.0), axis=0, keepdims=True) for i, s in zip(ids, scores)
            )
            if not first:
                total = total + before[side][1:2, cols] * jnp.exp(old_top - top)
                chosen = chosen + before[side][2:3, cols]
            after[side][0:1, cols] = top
            after[side][1:2, cols] = total
            after[side][2:3, cols] = chosen


def score(pieces, ids, wanted, other_wanted, own, other, before, scale):
    count, voxels = own.shape
    rows = sum(p.rows.shape[0] for p in pieces)
    whole = pl.BlockSpec(memory_space=pltpu.VMEM)
    operands = [ids, wanted, other_wanted, own, other, *(p.rows for p in pieces), *(before or ())]
    return pl.pallas_call(
        functools.partial(score_kernel, scale, len(pieces), before is None),
        out_shape=[jax.ShapeDtypeStruct((8, count), jnp.float32)] * 2,
        in_specs=[whole] * len(operands),
        out_specs=[whole] * 2,
        compiler_params=pltpu.CompilerParams(vmem_limit_bytes=28 << 20),
        cost_estimate=pl.CostEstimate(
            flops=4 * rows * count * voxels, transcendentals=2 * rows * count, bytes_accessed=rows * voxels * 2
        ),
        name="score",
    )(*operands)


def sums_kernel(classes, orients, key_ref, weights_ref, mine_ref, got_ref, particles_ref, out_ref):
    count, voxels = particles_ref.shape
    top = jnp.maximum(mine_ref[0:1, :], got_ref[0:1, :])
    total = mine_ref[1:2, :] * jnp.exp(mine_ref[0:1, :] - top) + got_ref[1:2, :] * jnp.exp(got_ref[0:1, :] - top)
    chosen = mine_ref[2:3, :] + got_ref[2:3, :]
    gain = weights_ref[...] * (classes * orients) * jnp.exp(chosen - top) / total
    steps = 2 * SHIFT + 1
    rows = lax.broadcasted_iota(jnp.int32, (steps * classes, count), 0)
    coef = jnp.where(rows == key_ref[...], gain, 0.0).astype(jnp.bfloat16)
    width = 512
    lane = lax.broadcasted_iota(jnp.int32, (classes, width), 1) % NX
    for base in range(0, voxels, width):
        moved = jnp.dot(coef, particles_ref[:, base : base + width], preferred_element_type=jnp.float32)
        summed = jnp.zeros((classes, width), jnp.float32)
        for k in range(steps):
            step = k - SHIFT
            part = moved[k * classes : (k + 1) * classes]
            if step != 0:
                inside = (lane >= step) if step > 0 else (lane < NX + step)
                wrapped = step - NX if step > 0 else step + NX
                part = jnp.where(
                    inside, pltpu.roll(part, step % width, 1), pltpu.roll(part, wrapped % width, 1)
                )
            summed = summed + part
        for j in range(width // LANES):
            out_ref[:, base // LANES + j, :] = summed[:, j * LANES : (j + 1) * LANES]


def class_sums(key, weights, mine, got, particles, classes, orients):
    count, voxels = particles.shape
    whole = pl.BlockSpec(memory_space=pltpu.VMEM)
    return pl.pallas_call(
        functools.partial(sums_kernel, classes, orients),
        out_shape=jax.ShapeDtypeStruct((classes, voxels // LANES, LANES), jnp.float32),
        in_specs=[whole] * 5,
        out_specs=whole,
        compiler_params=pltpu.CompilerParams(vmem_limit_bytes=16 << 20),
        name="class_sums",
    )(key, weights, mine, got, particles)


def body(references, particles, class_ids, orient_ids, offsets, weights):
    per_owner, local, voxels = references.shape
    devices = XN * YN * ZN * CORES
    classes = per_owner * XH * YN
    orients = local * XL * ZN * CORES
    count = particles.shape[0]
    scale = 1.0 / math.sqrt(voxels)
    xh, y, xl, z, core = (lax.axis_index(a) for a in ALL)
    here = (xh * XL + xl, y, z, core)

    other = swap_cores(particles)
    wanted = (class_ids * orients + orient_ids).astype(jnp.float32)[None, :]
    other_wanted = swap_cores(wanted)

    start = np.zeros((local, 4), np.int32)
    start[:, 3] = np.arange(local)
    piece = Piece(references.reshape(local, voxels), [start, start])
    piece = join([piece, piece.fetch((AZ, AZ), ZN // 2)])
    first = STAGES[0]
    piece = join([piece, piece.fetch(first, 1), piece.fetch(first, -1), piece.fetch(first, 2)])
    piece = join(ring(piece, STAGES[1]))
    pieces = ring(piece, STAGES[2])

    stats = None
    for group in (pieces[:1], pieces[1:3], pieces[3:]):
        ids = row_ids(group, here, local)
        stats = score(group, ids, wanted, other_wanted, particles, other, stats, scale)
    mine, theirs = stats
    got = swap_cores(theirs)
    key = class_ids + classes * (offsets + SHIFT)
    partial_sums = class_sums(key[None, :], weights[None, :], mine, got, particles, classes, orients)
    sent = partial_sums.reshape(devices, classes * voxels // devices)
    owned = jnp.sum(lax.all_to_all(sent, ALL, 0, 0, tiled=True), axis=0, keepdims=True)
    population = count * devices / classes
    return owned / jnp.sqrt(jnp.float32(population))


def solution(mesh):
    fine = Mesh(np.asarray(mesh.devices).reshape(XH, YN, XL, ZN, CORES), ALL)
    cls, ptl = ("xh", "y"), ("xl", "z", "core")
    placed = (P(cls, ptl, None), P(ALL, None), P(ALL), P(ALL), P(ALL), P(ALL))
    return jax.shard_map(
        body, mesh=fine, in_specs=placed, out_specs=P(cls, ptl), check_vma=False
    )
```

time: 158 us -> 124 us (0.78)
  matrix products: 41.8 us -> 0 us
  Pallas kernels: 6.75 us -> 22.3 us
  local copies, waits for them, and re-layouts: 11.4 us -> 3.75 us
  starting transfers between devices: 34.6 us -> 39.2 us
  other arithmetic: 5.44 us -> 1.83 us
  blocking collectives: 21.5 us -> 18.5 us
  waiting for transfers between devices: 35.3 us -> 38.2 us
    dot_general x10 -> x0, matrix products: 41.8 us -> none  [stats(): lax.dot_general(part.rows, whose[0], (((1,), (1,)), ((), ())), preferred_...]
    pallas_call x1 -> x4, Pallas kernels: 6.75 us -> 22.3 us  [the longest x3 21.3 us: score(): pl.pallas_call(functools.partial(score_kernel, scale, len(pieces), before...]
    ppermute x12, waiting for transfers between devices: 29.8 us -> 37.3 us  [fetch(): return Piece(lax.ppermute(self.rows, ALL, pairs(move)), moved)]
    unnamed x45 -> x29, local copies, waits for them, and re-layouts: 7.37 us -> 1.08 us
    ppermute x3, waiting for transfers between devices: 5.5 us -> 0.84 us  [swap_cores(): return lax.ppermute(value, ALL, pairs(lambda at, core: (at, 1 - core)))]
    ppermute x3, starting transfers between devices: 9.34 us -> 12.7 us  [swap_cores(): return lax.ppermute(value, ALL, pairs(lambda at, core: (at, 1 - core)))]
    all_to_all x1, blocking collectives: 21.5 us -> 18.5 us  [body(): lax.all_to_all(sent, ALL, 0, 0, tiled=True)]
    reduce_sum x6 -> x0, other arithmetic: 2.41 us -> none  [the longest x2 2.31 us: stats(): total = jnp.sum(jnp.exp(scores - top[None, :]), axis=0)]
  transfers between devices with their start and end apart: 15 -> 15, of which waited for: 9 -> 10; matrix products, arithmetic and copies ran while one was open for 19% -> 3% of each run, Pallas kernels for 0% -> 11%
where the time goes in v2:
time: 124 us
  starting transfers between devices  39.2 us (32%)
  waiting for transfers between devices  38.2 us (31%)
  Pallas kernels  22.3 us (18%)
  blocking collectives  18.5 us (15%)
  local copies, waits for them, and re-layouts  3.75 us (3%)
  other arithmetic  1.83 us (1%)
    ppermute x12, waiting for transfers between devices, fetch(): return Piece(lax.ppermute(self.rows, ALL, pairs(move)), moved)  37.3 us
    ppermute x12, starting transfers between devices, fetch(): return Piece(lax.ppermute(self.rows, ALL, pairs(move)), moved)  26.5 us
    pallas_call x3, Pallas kernels, score(): pl.pallas_call(functools.partial(score_kernel, scale, len(pieces), before...  21.3 us
    all_to_all x1, blocking collectives, body(): lax.all_to_all(sent, ALL, 0, 0, tiled=True)  18.5 us
    ppermute x3, starting transfers between devices, swap_cores(): return lax.ppermute(value, ALL, pairs(lambda at, core: (at, 1 - core)))  12.7 us
    slice x4, local copies, waits for them, and re-layouts, part(): return Piece(self.rows[start:stop], [o[start:stop] for o in self.offsets])  2.64 us
  transfers between devices with their start and end apart: 15, of which 10 were waited for; matrix products, arithmetic and copies ran while one was open for 3% of the time, Pallas kernels for 11%

profile of v2, /device:TPU:1, one launch (start us, length us, event | category | flops | bytes accessed | tf_op | source)
XLA Modules:
  0.0 124.0 jit_solution(10429716491354504952)
XLA Ops:
  0.0 7.7 %collective-permute-start.2 = (bf16[8,4096]{1,0:T(8,128)(2,1)}, bf16[8,4096]{1,0:T(8,128)(2,1)S(1)}, u32[]{:S(2)}, u32[]{:S(2)}) collective-permute-start(bf16[8,4096]{1,0:T(8,128)(2,1)} %bitcast.24), channel_id=1, source_target_pairs={{0,8},{1,9},{2,10},{3,11},{4,12},{5,13},{6,14},{7,15},{8,0},{9,1},... | collective-permute-start | bytes 196616 | tf_op jit(solution)/shard_map/ppermute | solution.py:55
  7.7 0.9 constant_dynamic-update-slice_fusion.4
  8.6 1.1 collective-permute-done.2
  9.7 0.8 pad_maximum_fusion
  10.6 2.8 %collective-permute-start.3 = (bf16[16,4096]{1,0:T(8,128)(2,1)S(1)}, bf16[16,4096]{1,0:T(8,128)(2,1)S(1)}, u32[]{:S(2)}, u32[]{:S(2)}) collective-permute-start(bf16[16,4096]{1,0:T(8,128)(2,1)S(1)} %pad_maximum_fusion), channel_id=1, source_target_pairs={{0,144},{1,97},{2,146},{3,99},{4,148},{5,101},{6,150},{7,103},{8,1... | collective-permute-start | bytes 393224 | tf_op jit(solution)/shard_map/ppermute | solution.py:55
  13.4 0.0 collective-permute-start.4
  13.4 1.6 %collective-permute-start.5 = (bf16[16,4096]{1,0:T(8,128)(2,1)S(1)}, bf16[16,4096]{1,0:T(8,128)(2,1)S(1)}, u32[]{:S(2)}, u32[]{:S(2)}) collective-permute-start(bf16[16,4096]{1,0:T(8,128)(2,1)S(1)} %pad_maximum_fusion), channel_id=1, source_target_pairs={{0,128},{1,65},{2,130},{3,67},{4,132},{5,69},{6,134},{7,71},{8,136... | collective-permute-start | bytes 393224 | tf_op jit(solution)/shard_map/ppermute | solution.py:55
  15.0 0.3 collective-permute-done.3
  15.3 4.8 %collective-permute-done.4 = bf16[16,4096]{1,0:T(8,128)(2,1)S(1)} collective-permute-done((bf16[16,4096]{1,0:T(8,128)(2,1)S(1)}, bf16[16,4096]{1,0:T(8,128)(2,1)S(1)}, u32[]{:S(2)}, u32[]{:S(2)}) %collective-permute-start.4) | collective-permute-done | bytes 131104 | tf_op jit(solution)/shard_map/ppermute | solution.py:55
  20.1 0.0 collective-permute-done.5
  20.2 0.0 copy-start.2
  20.2 0.0 copy-start.3
  20.2 0.0 copy-start.4
  20.2 0.0 copy-start.5
  20.2 0.0 copy-start.6
  20.2 4.5 %collective-permute-start.6 = (bf16[64,4096]{1,0:T(8,128)(2,1)S(1)}, bf16[64,4096]{1,0:T(8,128)(2,1)S(1)}, u32[]{:S(2)}, u32[]{:S(2)}) collective-permute-start(bf16[64,4096]{1,0:T(8,128)(2,1)S(1)} %get-tuple-element.17), channel_id=1, source_target_pairs={{0,96},{1,15},{2,98},{3,1},{4,100},{5,3},{6,102},{7,5},{8,104},{9,... | collective-permute-start | bytes 1572872 | tf_op jit(solution)/shard_map/ppermute | solution.py:55
  24.7 1.2 collective-permute-start.1
  25.9 4.9 %collective-permute-done.6 = bf16[64,4096]{1,0:T(8,128)(2,1)S(1)} collective-permute-done((bf16[64,4096]{1,0:T(8,128)(2,1)S(1)}, bf16[64,4096]{1,0:T(8,128)(2,1)S(1)}, u32[]{:S(2)}, u32[]{:S(2)}) %collective-permute-start.6) | collective-permute-done | bytes 524320 | tf_op jit(solution)/shard_map/ppermute | solution.py:55
  30.8 3.2 %collective-permute-start.8 = (bf16[32,4096]{1,0:T(8,128)(2,1)S(1)}, bf16[32,4096]{1,0:T(8,128)(2,1)S(1)}, u32[]{:S(2)}, u32[]{:S(2)}) collective-permute-start(bf16[32,4096]{1,0:T(8,128)(2,1)S(1)} %slice.16), channel_id=1, source_target_pairs={{0,96},{1,15},{2,98},{3,1},{4,100},{5,3},{6,102},{7,5},{8,104},{9,... | collective-permute-start | bytes 786440 | tf_op jit(solution)/shard_map/ppermute | solution.py:55
  34.0 0.2 collective-permute-done.7
  34.3 0.1 collective-permute-start.9
  34.4 2.9 %collective-permute-done.8 = bf16[32,4096]{1,0:T(8,128)(2,1)S(1)} collective-permute-done((bf16[32,4096]{1,0:T(8,128)(2,1)S(1)}, bf16[32,4096]{1,0:T(8,128)(2,1)S(1)}, u32[]{:S(2)}, u32[]{:S(2)}) %collective-permute-start.8) | collective-permute-done | bytes 262176 | tf_op jit(solution)/shard_map/ppermute | solution.py:55
  37.4 3.7 %collective-permute-done.9 = bf16[32,4096]{1,0:T(8,128)(2,1)S(1)} collective-permute-done((bf16[32,4096]{1,0:T(8,128)(2,1)S(1)}, bf16[32,4096]{1,0:T(8,128)(2,1)S(1)}, u32[]{:S(2)}, u32[]{:S(2)}) %collective-permute-start.9) | collective-permute-done | bytes 262176 | tf_op jit(solution)/shard_map/ppermute | solution.py:55
  41.1 2.7 %collective-permute-start.10 = (bf16[256,4096]{1,0:T(8,128)(2,1)S(1)}, bf16[256,4096]{1,0:T(8,128)(2,1)}, u32[]{:S(2)}, u32[]{:S(2)}) collective-permute-start(bf16[256,4096]{1,0:T(8,128)(2,1)S(1)} %constant_dynamic-update-slice_fusion.5.refs_0_), channel_id=1, source_target_pairs={{0,14},{1,145},{2,0},{3,147},{4,2},{5,149},{6,4},{7,151},{8,6},{9,... | collective-permute-start | bytes 6291464 | tf_op jit(solution)/shard_map/ppermute | solution.py:55
  43.7 0.0 collective-permute-start.12
  43.8 4.9 %collective-permute-start = (f32[1,512]{1,0:T(1,128)S(1)}, f32[1,512]{1,0:T(1,128)S(1)}, u32[]{:S(2)}, u32[]{:S(2)}) collective-permute-start(f32[1,512]{1,0:T(1,128)S(1)} %bitcast.15), channel_id=1, source_target_pairs={{0,1},{1,0},{2,3},{3,2},{4,5},{5,4},{6,7},{7,6},{8,9},{9,8},{10,11... | collective-permute-start | bytes 6152 | tf_op jit(solution)/shard_map/ppermute | solution.py:39
  48.7 0.1 fusion.13
  48.7 0.0 copy-start.8
  48.8 0.0 copy-start
  48.8 18.0 %collective-permute-done.10.refs_0_ = bf16[256,4096]{1,0:T(8,128)(2,1)} collective-permute-done((bf16[256,4096]{1,0:T(8,128)(2,1)S(1)}, bf16[256,4096]{1,0:T(8,128)(2,1)}, u32[]{:S(2)}, u32[]{:S(2)}) %collective-permute-start.10) | collective-permute-done | bytes 2097184 | tf_op jit(solution)/shard_map/ppermute | solution.py:55
  66.7 1.3 %slice.18 = bf16[128,4096]{1,0:T(8,128)(2,1)S(1)} slice(bf16[256,4096]{1,0:T(8,128)(2,1)} %collective-permute-done.10.refs_0_), slice={[0:128], [0:4096]} | slice | bytes 2097152 | tf_op jit(solution)/shard_map/slice | solution.py:47
  68.0 3.6 %collective-permute-start.11 = (bf16[128,4096]{1,0:T(8,128)(2,1)S(1)}, bf16[128,4096]{1,0:T(8,128)(2,1)S(1)}, u32[]{:S(2)}, u32[]{:S(2)}) collective-permute-start(bf16[128,4096]{1,0:T(8,128)(2,1)S(1)} %slice.18), channel_id=1, source_target_pairs={{0,14},{1,145},{2,0},{3,147},{4,2},{5,149},{6,4},{7,151},{8,6},{9,... | collective-permute-start | bytes 3145736 | tf_op jit(solution)/shard_map/ppermute | solution.py:55
  71.6 1.3 %slice.19 = bf16[128,4096]{1,0:T(8,128)(2,1)S(1)} slice(bf16[256,4096]{1,0:T(8,128)(2,1)} %collective-permute-done.12.refs_1_), slice={[128:256], [0:4096]} | slice | bytes 2097152 | tf_op jit(solution)/shard_map/slice | solution.py:47
  72.9 0.3 collective-permute-start.13
  73.2 0.1 fusion.38
  73.3 0.1 fusion.39
  73.4 0.0 collective-permute-done.other_wanted_ref
  73.4 0.0 collective-permute-done.1.other_ref
  73.4 4.8 %score.3 = (f32[8,512]{1,0:T(8,128)S(1)}, f32[8,512]{1,0:T(8,128)S(1)}) custom-call(f32[1,256]{1,0:T(1,128)S(1)} %bitcast.21, f32[1,512]{1,0:T(1,128)S(1)} %bitcast.16, f32[1,512]{1,0:T(1,128)S(1)} %collective-permute-done.other_wanted_ref, bf16[512,4096]{1,0:T(8,128)(2,1)S(1)} %copy-done, bf16[512,4096]{1,0:T(8,128)(2,1)} %collective-permute-done.1.other_ref, ...), custom_call_target="tpu_custom_call" | custom-call | flops 2147483648 | bytes 2097152 | tf_op jit(solution)/shard_map/score/pallas_call | solution.py:133
  78.2 8.6 %score.4 = (f32[8,512]{1,0:T(8,128)S(1)}, f32[8,512]{1,0:T(8,128)S(1)}) custom-call(f32[1,512]{1,0:T(1,128)S(1)} %bitcast.23, f32[1,512]{1,0:T(1,128)S(1)} %bitcast.17, f32[1,512]{1,0:T(1,128)S(1)} %collective-permute-done.other_wanted_ref, bf16[512,4096]{1,0:T(8,128)(2,1)S(1)} %copy-done, bf16[512,4096]{1,0:T(8,128)(2,1)} %collective-permute-done.1.other_ref, ...), custom_call_target="tpu_custom_call" | custom-call | flops 4294967296 | bytes 4194304 | tf_op jit(solution)/shard_map/score/pallas_call | solution.py:133
  86.8 1.5 %collective-permute-done.13.refs_1_ = bf16[128,4096]{1,0:T(8,128)(2,1)S(1)} collective-permute-done((bf16[128,4096]{1,0:T(8,128)(2,1)S(1)}, bf16[128,4096]{1,0:T(8,128)(2,1)S(1)}, u32[]{:S(2)}, u32[]{:S(2)}) %collective-permute-start.13) | collective-permute-done | bytes 1048608 | tf_op jit(solution)/shard_map/ppermute | solution.py:55
  88.4 7.9 %score.5 = (f32[8,512]{1,0:T(8,128)S(1)}, f32[8,512]{1,0:T(8,128)S(1)}) custom-call(f32[1,256]{1,0:T(1,128)S(1)} %bitcast.20, f32[1,512]{1,0:T(1,128)S(1)} %bitcast.18, f32[1,512]{1,0:T(1,128)S(1)} %collective-permute-done.other_wanted_ref, bf16[512,4096]{1,0:T(8,128)(2,1)S(1)} %copy-done, bf16[512,4096]{1,0:T(8,128)(2,1)} %collective-permute-done.1.other_ref, ...), custom_call_target="tpu_custom_call" | custom-call | flops 2147483648 | bytes 2097152 | tf_op jit(solution)/shard_map/score/pallas_call | solution.py:133
  96.3 6.6 %collective-permute-start.14 = (f32[8,512]{1,0:T(8,128)S(1)}, f32[8,512]{1,0:T(8,128)S(1)}, u32[]{:S(2)}, u32[]{:S(2)}) collective-permute-start(f32[8,512]{1,0:T(8,128)S(1)} %get-tuple-element.16), channel_id=1, source_target_pairs={{0,1},{1,0},{2,3},{3,2},{4,5},{5,4},{6,7},{7,6},{8,9},{9,8},{10,11... | collective-permute-start | bytes 49160 | tf_op jit(solution)/shard_map/ppermute | solution.py:39
  102.8 0.8 collective-permute-done.14.got_ref
  103.7 1.0 class_sums.1
  104.7 18.5 %all_to_all.9 = f32[256,1,128]{2,1,0:T(1,128)S(1)} all-to-all(f32[256,1,128]{2,1,0:T(1,128)S(1)} %bitcast.14), channel_id=1, replica_groups=mesh['xh'=2,'y'=4,'xl'=2,'z'=8,'core'=2] {'xh','y','xl','z','core'}, dimensions={0} | all-to-all | bytes 262144 | tf_op jit(solution)/shard_map/all_to_all | solution.py:219
  123.2 0.3 reduce_sum.9
  123.5 0.5 multiply_bitcast_fusion
  (29 shorter events, 0.3 us)
Async XLA Ops:
  0.0 9.7 %collective-permute-start.2 = (bf16[8,4096]{1,0:T(8,128)(2,1)}, bf16[8,4096]{1,0:T(8,128)(2,1)S(1)}, u32[]{:S(2)}, u32[]{:S(2)}) collective-permute-start(bf16[8,4096]{1,0:T(8,128)(2,1)} %bitcast.24), channel_id=1, source_target_pairs={{0,8},{1,9},{2,10},{3,11},{4,12},{5,13},{6,14},{7,15},{8,0},{9,1},... | collective-permute-start | bytes 196616 | tf_op jit(solution)/shard_map/ppermute | solution.py:55
  10.6 4.8 %collective-permute-start.3 = (bf16[16,4096]{1,0:T(8,128)(2,1)S(1)}, bf16[16,4096]{1,0:T(8,128)(2,1)S(1)}, u32[]{:S(2)}, u32[]{:S(2)}) collective-permute-start(bf16[16,4096]{1,0:T(8,128)(2,1)S(1)} %pad_maximum_fusion), channel_id=1, source_target_pairs={{0,144},{1,97},{2,146},{3,99},{4,148},{5,101},{6,150},{7,103},{8,1... | collective-permute-start | bytes 393224 | tf_op jit(solution)/shard_map/ppermute | solution.py:55
  13.4 6.7 %collective-permute-start.4 = (bf16[16,4096]{1,0:T(8,128)(2,1)S(1)}, bf16[16,4096]{1,0:T(8,128)(2,1)S(1)}, u32[]{:S(2)}, u32[]{:S(2)}) collective-permute-start(bf16[16,4096]{1,0:T(8,128)(2,1)S(1)} %pad_maximum_fusion), channel_id=1, source_target_pairs={{0,16},{1,33},{2,18},{3,35},{4,20},{5,37},{6,22},{7,39},{8,24},{9,... | collective-permute-start | bytes 393224 | tf_op jit(solution)/shard_map/ppermute | solution.py:55
  13.4 6.7 %collective-permute-start.5 = (bf16[16,4096]{1,0:T(8,128)(2,1)S(1)}, bf16[16,4096]{1,0:T(8,128)(2,1)S(1)}, u32[]{:S(2)}, u32[]{:S(2)}) collective-permute-start(bf16[16,4096]{1,0:T(8,128)(2,1)S(1)} %pad_maximum_fusion), channel_id=1, source_target_pairs={{0,128},{1,65},{2,130},{3,67},{4,132},{5,69},{6,134},{7,71},{8,136... | collective-permute-start | bytes 393224 | tf_op jit(solution)/shard_map/ppermute | solution.py:55
  20.2 23.6 %copy-start.2 = (s32[512]{0:T(512)S(1)}, s32[512]{0:T(512)}, u32[]{:S(2)}) copy-start(s32[512]{0:T(512)} %param.15) | copy-start | bytes 6148
  20.2 23.6 %copy-start.3 = (s32[512]{0:T(512)S(1)}, s32[512]{0:T(512)}, u32[]{:S(2)}) copy-start(s32[512]{0:T(512)} %param.14) | copy-start | bytes 6148
  20.2 23.6 %copy-start.4 = (s32[512]{0:T(512)S(1)}, s32[512]{0:T(512)}, u32[]{:S(2)}) copy-start(s32[512]{0:T(512)} %param.16) | copy-start | bytes 6148
  20.2 28.5 %copy-start.5 = (s32[512]{0:T(512)S(1)}, s32[512]{0:T(512)}, u32[]{:S(2)}) copy-start(s32[512]{0:T(512)} %constant.272.clone) | copy-start | bytes 6148
  20.2 28.5 %copy-start.6 = (s32[512]{0:T(512)S(1)}, s32[512]{0:T(512)}, u32[]{:S(2)}) copy-start(s32[512]{0:T(512)} %constant.273.clone) | copy-start | bytes 6148
  20.2 10.6 %collective-permute-start.6 = (bf16[64,4096]{1,0:T(8,128)(2,1)S(1)}, bf16[64,4096]{1,0:T(8,128)(2,1)S(1)}, u32[]{:S(2)}, u32[]{:S(2)}) collective-permute-start(bf16[64,4096]{1,0:T(8,128)(2,1)S(1)} %get-tuple-element.17), channel_id=1, source_target_pairs={{0,96},{1,15},{2,98},{3,1},{4,100},{5,3},{6,102},{7,5},{8,104},{9,... | collective-permute-start | bytes 1572872 | tf_op jit(solution)/shard_map/ppermute | solution.py:55
  24.7 9.5 %collective-permute-start.7 = (bf16[64,4096]{1,0:T(8,128)(2,1)S(1)}, bf16[64,4096]{1,0:T(8,128)(2,1)S(1)}, u32[]{:S(2)}, u32[]{:S(2)}) collective-permute-start(bf16[64,4096]{1,0:T(8,128)(2,1)S(1)} %get-tuple-element.17), channel_id=1, source_target_pairs={{0,32},{1,3},{2,34},{3,5},{4,36},{5,7},{6,38},{7,9},{8,40},{9,11},... | collective-permute-start | bytes 1572872 | tf_op jit(solution)/shard_map/ppermute | solution.py:55
  24.7 48.7 %collective-permute-start.1 = (bf16[512,4096]{1,0:T(8,128)(2,1)}, bf16[512,4096]{1,0:T(8,128)(2,1)}, u32[]{:S(2)}, u32[]{:S(2)}) collective-permute-start(bf16[512,4096]{1,0:T(8,128)(2,1)} %particles_ref.1), channel_id=1, source_target_pairs={{0,1},{1,0},{2,3},{3,2},{4,5},{5,4},{6,7},{7,6},{8,9},{9,8},{10,11... | collective-permute-start | bytes 12582920 | tf_op jit(solution)/shard_map/ppermute | solution.py:39
  30.8 6.5 %collective-permute-start.8 = (bf16[32,4096]{1,0:T(8,128)(2,1)S(1)}, bf16[32,4096]{1,0:T(8,128)(2,1)S(1)}, u32[]{:S(2)}, u32[]{:S(2)}) collective-permute-start(bf16[32,4096]{1,0:T(8,128)(2,1)S(1)} %slice.16), channel_id=1, source_target_pairs={{0,96},{1,15},{2,98},{3,1},{4,100},{5,3},{6,102},{7,5},{8,104},{9,... | collective-permute-start | bytes 786440 | tf_op jit(solution)/shard_map/ppermute | solution.py:55
  34.3 6.8 %collective-permute-start.9 = (bf16[32,4096]{1,0:T(8,128)(2,1)S(1)}, bf16[32,4096]{1,0:T(8,128)(2,1)S(1)}, u32[]{:S(2)}, u32[]{:S(2)}) collective-permute-start(bf16[32,4096]{1,0:T(8,128)(2,1)S(1)} %slice.17), channel_id=1, source_target_pairs={{0,32},{1,3},{2,34},{3,5},{4,36},{5,7},{6,38},{7,9},{8,40},{9,11},... | collective-permute-start | bytes 786440 | tf_op jit(solution)/shard_map/ppermute | solution.py:55
  41.1 25.6 %collective-permute-start.10 = (bf16[256,4096]{1,0:T(8,128)(2,1)S(1)}, bf16[256,4096]{1,0:T(8,128)(2,1)}, u32[]{:S(2)}, u32[]{:S(2)}) collective-permute-start(bf16[256,4096]{1,0:T(8,128)(2,1)S(1)} %constant_dynamic-update-slice_fusion.5.refs_0_), channel_id=1, source_target_pairs={{0,14},{1,145},{2,0},{3,147},{4,2},{5,149},{6,4},{7,151},{8,6},{9,... | collective-permute-start | bytes 6291464 | tf_op jit(solution)/shard_map/ppermute | solution.py:55
  43.7 27.9 %collective-permute-start.12 = (bf16[256,4096]{1,0:T(8,128)(2,1)S(1)}, bf16[256,4096]{1,0:T(8,128)(2,1)}, u32[]{:S(2)}, u32[]{:S(2)}) collective-permute-start(bf16[256,4096]{1,0:T(8,128)(2,1)S(1)} %constant_dynamic-update-slice_fusion.5.refs_0_), channel_id=1, source_target_pairs={{0,2},{1,17},{2,4},{3,19},{4,6},{5,21},{6,8},{7,23},{8,10},{9,25},... | collective-permute-start | bytes 6291464 | tf_op jit(solution)/shard_map/ppermute | solution.py:55
  43.8 29.6 %collective-permute-start = (f32[1,512]{1,0:T(1,128)S(1)}, f32[1,512]{1,0:T(1,128)S(1)}, u32[]{:S(2)}, u32[]{:S(2)}) collective-permute-start(f32[1,512]{1,0:T(1,128)S(1)} %bitcast.15), channel_id=1, source_target_pairs={{0,1},{1,0},{2,3},{3,2},{4,5},{5,4},{6,7},{7,6},{8,9},{9,8},{10,11... | collective-permute-start | bytes 6152 | tf_op jit(solution)/shard_map/ppermute | solution.py:39
  48.7 24.5 %copy-start.9 = (s32[256]{0:T(256)S(1)}, s32[256]{0:T(256)}, u32[]{:S(2)}) copy-start(s32[256]{0:T(256)} %constant.270.clone) | copy-start | bytes 3076
  48.7 24.6 %copy-start.10 = (s32[256]{0:T(256)S(1)}, s32[256]{0:T(256)}, u32[]{:S(2)}) copy-start(s32[256]{0:T(256)} %constant.271.clone) | copy-start | bytes 3076
  48.7 24.6 %copy-start.7 = (s32[256]{0:T(256)S(1)}, s32[256]{0:T(256)}, u32[]{:S(2)}) copy-start(s32[256]{0:T(256)} %constant.274.clone) | copy-start | bytes 3076
  48.7 24.6 %copy-start.8 = (s32[256]{0:T(256)S(1)}, s32[256]{0:T(256)}, u32[]{:S(2)}) copy-start(s32[256]{0:T(256)} %constant.275.clone) | copy-start | bytes 3076
  48.8 24.6 %copy-start = (bf16[512,4096]{1,0:T(8,128)(2,1)S(1)}, bf16[512,4096]{1,0:T(8,128)(2,1)}, u32[]{:S(2)}) copy-start(bf16[512,4096]{1,0:T(8,128)(2,1)} %particles_ref.1) | copy-start | bytes 12582916
  68.0 18.8 %collective-permute-start.11 = (bf16[128,4096]{1,0:T(8,128)(2,1)S(1)}, bf16[128,4096]{1,0:T(8,128)(2,1)S(1)}, u32[]{:S(2)}, u32[]{:S(2)}) collective-permute-start(bf16[128,4096]{1,0:T(8,128)(2,1)S(1)} %slice.18), channel_id=1, source_target_pairs={{0,14},{1,145},{2,0},{3,147},{4,2},{5,149},{6,4},{7,151},{8,6},{9,... | collective-permute-start | bytes 3145736 | tf_op jit(solution)/shard_map/ppermute | solution.py:55
  72.9 15.4 %collective-permute-start.13 = (bf16[128,4096]{1,0:T(8,128)(2,1)S(1)}, bf16[128,4096]{1,0:T(8,128)(2,1)S(1)}, u32[]{:S(2)}, u32[]{:S(2)}) collective-permute-start(bf16[128,4096]{1,0:T(8,128)(2,1)S(1)} %slice.19), channel_id=1, source_target_pairs={{0,2},{1,17},{2,4},{3,19},{4,6},{5,21},{6,8},{7,23},{8,10},{9,25},... | collective-permute-start | bytes 3145736 | tf_op jit(solution)/shard_map/ppermute | solution.py:55
  88.3 15.3 %copy-start.1 = (f32[512]{0:T(512)S(1)}, f32[512]{0:T(512)}, u32[]{:S(2)}) copy-start(f32[512]{0:T(512)} %param.17) | copy-start | bytes 6148
  96.3 7.4 %collective-permute-start.14 = (f32[8,512]{1,0:T(8,128)S(1)}, f32[8,512]{1,0:T(8,128)S(1)}, u32[]{:S(2)}, u32[]{:S(2)}) collective-permute-start(f32[8,512]{1,0:T(8,128)S(1)} %get-tuple-element.16), channel_id=1, source_target_pairs={{0,1},{1,0},{2,3},{3,2},{4,5},{5,4},{6,7},{7,6},{8,9},{9,8},{10,11... | collective-permute-start | bytes 49160 | tf_op jit(solution)/shard_map/ppermute | solution.py:39

commit v3 on v2

--- a/solution.py
+++ b/solution.py
@@ -91,32 +91,24 @@
     pieces, refs = refs[:n], refs[n:]
     before, after = (None, None) if first else refs[:2], refs[-2:]
     count = own_ref.shape[0]
-    ids, at = [], 0
-    for piece in pieces:
-        rows = piece.shape[0]
-        column = jnp.broadcast_to(ids_ref[0:1, at : at + rows], (LANES, rows)).T
-        ids.append(jnp.concatenate([column] * (BLOCK // LANES), axis=1))
-        at += rows
+    rows = sum(piece.shape[0] for piece in pieces)
+    column = jnp.broadcast_to(ids_ref[...], (LANES, rows)).T
+    ids = jnp.concatenate([column] * (BLOCK // LANES), axis=1)
+    held = jnp.concatenate([piece[...] for piece in pieces], axis=0)
     for side, (particles, wanted) in enumerate(((own_ref, wanted_ref), (other_ref, other_wanted_ref))):
         for start in range(0, count, BLOCK):
             cols = slice(start, start + BLOCK)
             block = particles[cols, :]
             want = wanted[0:1, cols]
-            scores = [
-                lax.dot_general(
-                    piece[...], block, (((1,), (1,)), ((), ())), preferred_element_type=jnp.float32
-                )
-                * scale
-                for piece in pieces
-            ]
-            top = functools.reduce(jnp.maximum, [jnp.max(s, axis=0, keepdims=True) for s in scores])
+            scores = scale * lax.dot_general(
+                held, block, (((1,), (1,)), ((), ())), preferred_element_type=jnp.float32
+            )
+            top = jnp.max(scores, axis=0, keepdims=True)
             if not first:
                 old_top = before[side][0:1, cols]
                 top = jnp.maximum(top, old_top)
-            total = sum(jnp.sum(jnp.exp(s - top), axis=0, keepdims=True) for s in scores)
-            chosen = sum(
-                jnp.sum(jnp.where(i == want, s, 0.0), axis=0, keepdims=True) for i, s in zip(ids, scores)
-            )
+            total = jnp.sum(jnp.exp(scores - top), axis=0, keepdims=True)
+            chosen = jnp.sum(jnp.where(ids == want, scores, 0.0), axis=0, keepdims=True)
             if not first:
                 total = total + before[side][1:2, cols] * jnp.exp(old_top - top)
                 chosen = chosen + before[side][2:3, cols]
@@ -135,7 +127,7 @@
         out_shape=[jax.ShapeDtypeStruct((8, count), jnp.float32)] * 2,
         in_specs=[whole] * len(operands),
         out_specs=[whole] * 2,
-        compiler_params=pltpu.CompilerParams(vmem_limit_bytes=28 << 20),
+        compiler_params=pltpu.CompilerParams(vmem_limit_bytes=16 << 20),
         cost_estimate=pl.CostEstimate(
             flops=4 * rows * count * voxels, transcendentals=2 * rows * count, bytes_accessed=rows * voxels * 2
         ),
@@ -204,11 +196,15 @@
     piece = join([piece, piece.fetch((AZ, AZ), ZN // 2)])
     first = STAGES[0]
     piece = join([piece, piece.fetch(first, 1), piece.fetch(first, -1), piece.fetch(first, 2)])
-    piece = join(ring(piece, STAGES[1]))
-    pieces = ring(piece, STAGES[2])
+    near, ahead, behind, far_a, far_b = ring(piece, STAGES[1])
+    last = STAGES[2]
+    one, two = join([near, ahead]), join([behind, far_a, far_b])
+    ahead_one, behind_one = one.fetch(last, 1), one.fetch(last, -1)
+    ahead_two, behind_two = two.fetch(last, 1), two.fetch(last, -1)
+    far_one, far_two = ahead_one.fetch(last, 1), behind_two.fetch(last, -1)
 
     stats = None
-    for group in (pieces[:1], pieces[1:3], pieces[3:]):
+    for group in ((one, two), (ahead_one, behind_one), (ahead_two, behind_two), (far_one, far_two)):
         ids = row_ids(group, here, local)
         stats = score(group, ids, wanted, other_wanted, particles, other, stats, scale)
     mine, theirs = stats

time: 124 us -> 114 us (0.919)
  waiting for transfers between devices: 38.2 us -> 26.1 us
  blocking collectives: 18.5 us -> 21.7 us
  Pallas kernels: 22.3 us -> 21 us
    ppermute x12 -> x14, waiting for transfers between devices: 37.3 us -> 24.5 us  [fetch(): return Piece(lax.ppermute(self.rows, ALL, pairs(move)), moved)]
    all_to_all x1, blocking collectives: 18.5 us -> 21.7 us  [body(): lax.all_to_all(sent, ALL, 0, 0, tiled=True)]
    ppermute x3, starting transfers between devices: 12.7 us -> 9.8 us  [swap_cores(): return lax.ppermute(value, ALL, pairs(lambda at, core: (at, 1 - core)))]
    ppermute x12 -> x14, starting transfers between devices: 26.5 us -> 29.3 us  [fetch(): return Piece(lax.ppermute(self.rows, ALL, pairs(move)), moved)]
    slice x4 -> x2, local copies, waits for them, and re-layouts: 2.64 us -> 0.04 us  [part(): return Piece(self.rows[start:stop], [o[start:stop] for o in self.offsets])]
    unnamed x29 -> x34, local copies, waits for them, and re-layouts: 1.08 us -> 3.19 us
    pallas_call x3 -> x4, Pallas kernels: 21.3 us -> 20 us  [score(): pl.pallas_call(functools.partial(score_kernel, scale, len(pieces), before...]
  transfers between devices with their start and end apart: 15 -> 17, of which waited for: 10 -> 12; matrix products, arithmetic and copies ran while one was open for 3% -> 2% of each run, Pallas kernels for 11% -> 13%
where the time goes in v3:
time: 114 us; the launch traced here: 113 us
  starting transfers between devices  39.1 us (34%)
  waiting for transfers between devices  26.1 us (23%)
  blocking collectives  21.7 us (19%)
  Pallas kernels  21 us (18%)
  local copies, waits for them, and re-layouts  3.3 us (3%)
  other arithmetic  1.88 us (2%)
    ppermute x14, starting transfers between devices, fetch(): return Piece(lax.ppermute(self.rows, ALL, pairs(move)), moved)  29.3 us
    ppermute x14, waiting for transfers between devices, fetch(): return Piece(lax.ppermute(self.rows, ALL, pairs(move)), moved)  24.5 us
    all_to_all x1, blocking collectives, body(): lax.all_to_all(sent, ALL, 0, 0, tiled=True)  21.7 us
    pallas_call x4, Pallas kernels, score(): pl.pallas_call(functools.partial(score_kernel, scale, len(pieces), before...  20 us
    ppermute x3, starting transfers between devices, swap_cores(): return lax.ppermute(value, ALL, pairs(lambda at, core: (at, 1 - core)))  9.8 us
    unnamed x34, local copies, waits for them, and re-layouts  3.19 us
  transfers between devices with their start and end apart: 17, of which 12 were waited for; matrix products, arithmetic and copies ran while one was open for 2% of the time, Pallas kernels for 13%

profile of v3, /device:TPU:1, one launch (start us, length us, event | category | flops | bytes accessed | tf_op | source)
XLA Modules:
  0.0 113.2 jit_solution(9498845113720416607)
XLA Ops:
  0.0 0.0 copy-start.11
  0.0 0.0 copy-start.8
  0.0 0.0 copy-start.9
  0.0 0.0 copy-start.6
  0.1 0.0 copy-start.7
  0.1 7.8 %collective-permute-start.2 = (bf16[8,4096]{1,0:T(8,128)(2,1)}, bf16[8,4096]{1,0:T(8,128)(2,1)S(1)}, u32[]{:S(2)}, u32[]{:S(2)}) collective-permute-start(bf16[8,4096]{1,0:T(8,128)(2,1)} %bitcast.27), channel_id=1, source_target_pairs={{0,8},{1,9},{2,10},{3,11},{4,12},{5,13},{6,14},{7,15},{8,0},{9,1},... | collective-permute-start | bytes 196616 | tf_op jit(solution)/shard_map/ppermute | solution.py:55
  7.9 1.0 collective-permute-start.1
  8.9 0.8 constant_dynamic-update-slice_fusion.4
  9.7 0.2 collective-permute-done.2
  9.9 0.8 pad_maximum_fusion
  10.7 2.8 %collective-permute-start.3 = (bf16[16,4096]{1,0:T(8,128)(2,1)S(1)}, bf16[16,4096]{1,0:T(8,128)(2,1)S(1)}, u32[]{:S(2)}, u32[]{:S(2)}) collective-permute-start(bf16[16,4096]{1,0:T(8,128)(2,1)S(1)} %pad_maximum_fusion), channel_id=1, source_target_pairs={{0,144},{1,97},{2,146},{3,99},{4,148},{5,101},{6,150},{7,103},{8,1... | collective-permute-start | bytes 393224 | tf_op jit(solution)/shard_map/ppermute | solution.py:55
  13.6 0.0 collective-permute-start.4
  13.6 1.6 %collective-permute-start.5 = (bf16[16,4096]{1,0:T(8,128)(2,1)S(1)}, bf16[16,4096]{1,0:T(8,128)(2,1)S(1)}, u32[]{:S(2)}, u32[]{:S(2)}) collective-permute-start(bf16[16,4096]{1,0:T(8,128)(2,1)S(1)} %pad_maximum_fusion), channel_id=1, source_target_pairs={{0,128},{1,65},{2,130},{3,67},{4,132},{5,69},{6,134},{7,71},{8,136... | collective-permute-start | bytes 393224 | tf_op jit(solution)/shard_map/ppermute | solution.py:55
  15.2 0.3 collective-permute-done.3
  15.5 4.8 %collective-permute-done.4 = bf16[16,4096]{1,0:T(8,128)(2,1)S(1)} collective-permute-done((bf16[16,4096]{1,0:T(8,128)(2,1)S(1)}, bf16[16,4096]{1,0:T(8,128)(2,1)S(1)}, u32[]{:S(2)}, u32[]{:S(2)}) %collective-permute-start.4) | collective-permute-done | bytes 131104 | tf_op jit(solution)/shard_map/ppermute | solution.py:55
  20.3 4.5 %collective-permute-start.6 = (bf16[64,4096]{1,0:T(8,128)(2,1)S(1)}, bf16[64,4096]{1,0:T(8,128)(2,1)S(1)}, u32[]{:S(2)}, u32[]{:S(2)}) collective-permute-start(bf16[64,4096]{1,0:T(8,128)(2,1)S(1)} %get-tuple-element.21), channel_id=1, source_target_pairs={{0,96},{1,15},{2,98},{3,1},{4,100},{5,3},{6,102},{7,5},{8,104},{9,... | collective-permute-start | bytes 1572872 | tf_op jit(solution)/shard_map/ppermute | solution.py:55
  24.8 6.1 %collective-permute-done.6 = bf16[64,4096]{1,0:T(8,128)(2,1)S(1)} collective-permute-done((bf16[64,4096]{1,0:T(8,128)(2,1)S(1)}, bf16[64,4096]{1,0:T(8,128)(2,1)S(1)}, u32[]{:S(2)}, u32[]{:S(2)}) %collective-permute-start.6) | collective-permute-done | bytes 524320 | tf_op jit(solution)/shard_map/ppermute | solution.py:55
  31.0 3.2 %collective-permute-start.10 = (bf16[32,4096]{1,0:T(8,128)(2,1)S(1)}, bf16[32,4096]{1,0:T(8,128)(2,1)S(1)}, u32[]{:S(2)}, u32[]{:S(2)}) collective-permute-start(bf16[32,4096]{1,0:T(8,128)(2,1)S(1)} %slice.8), channel_id=1, source_target_pairs={{0,96},{1,15},{2,98},{3,1},{4,100},{5,3},{6,102},{7,5},{8,104},{9,... | collective-permute-start | bytes 786440 | tf_op jit(solution)/shard_map/ppermute | solution.py:55
  34.2 0.2 collective-permute-done.9
  34.4 0.1 collective-permute-start.11
  34.5 2.7 %collective-permute-start.7 = (bf16[128,4096]{1,0:T(8,128)(2,1)S(1)}, bf16[128,4096]{1,0:T(8,128)(2,1)S(1)}, u32[]{:S(2)}, u32[]{:S(2)}) collective-permute-start(bf16[128,4096]{1,0:T(8,128)(2,1)S(1)} %constant_dynamic-update-slice_fusion.5.refs_0_), channel_id=1, source_target_pairs={{0,14},{1,145},{2,0},{3,147},{4,2},{5,149},{6,4},{7,151},{8,6},{9,... | collective-permute-start | bytes 3145736 | tf_op jit(solution)/shard_map/ppermute | solution.py:55
  37.2 0.3 collective-permute-done.10
  37.5 3.7 %collective-permute-done.11 = bf16[32,4096]{1,0:T(8,128)(2,1)S(1)} collective-permute-done((bf16[32,4096]{1,0:T(8,128)(2,1)S(1)}, bf16[32,4096]{1,0:T(8,128)(2,1)S(1)}, u32[]{:S(2)}, u32[]{:S(2)}) %collective-permute-start.11) | collective-permute-done | bytes 262176 | tf_op jit(solution)/shard_map/ppermute | solution.py:55
  41.2 1.2 %collective-permute-start.12 = (bf16[128,4096]{1,0:T(8,128)(2,1)S(1)}, bf16[128,4096]{1,0:T(8,128)(2,1)}, u32[]{:S(2)}, u32[]{:S(2)}) collective-permute-start(bf16[128,4096]{1,0:T(8,128)(2,1)S(1)} %constant_dynamic-update-slice_fusion.11.refs_1_), channel_id=1, source_target_pairs={{0,2},{1,17},{2,4},{3,19},{4,6},{5,21},{6,8},{7,23},{8,10},{9,25},... | collective-permute-start | bytes 3145736 | tf_op jit(solution)/shard_map/ppermute | solution.py:55
  42.5 3.8 %collective-permute-start = (f32[1,512]{1,0:T(1,128)S(1)}, f32[1,512]{1,0:T(1,128)S(1)}, u32[]{:S(2)}, u32[]{:S(2)}) collective-permute-start(f32[1,512]{1,0:T(1,128)S(1)} %bitcast.16), channel_id=1, source_target_pairs={{0,1},{1,0},{2,3},{3,2},{4,5},{5,4},{6,7},{7,6},{8,9},{9,8},{10,11... | collective-permute-start | bytes 6152 | tf_op jit(solution)/shard_map/ppermute | solution.py:39
  46.2 0.1 fusion.36
  46.3 0.8 collective-permute-done.other_wanted_ref
  47.0 2.0 %collective-permute-start.14 = (bf16[128,4096]{1,0:T(8,128)(2,1)S(1)}, bf16[128,4096]{1,0:T(8,128)(2,1)S(1)}, u32[]{:S(2)}, u32[]{:S(2)}) collective-permute-start(bf16[128,4096]{1,0:T(8,128)(2,1)S(1)} %constant_dynamic-update-slice_fusion.11.refs_1_), channel_id=1, source_target_pairs={{0,14},{1,145},{2,0},{3,147},{4,2},{5,149},{6,4},{7,151},{8,6},{9,... | collective-permute-start | bytes 3145736 | tf_op jit(solution)/shard_map/ppermute | solution.py:55
  49.1 0.1 fusion.37
  49.1 3.3 %collective-permute-start.8 = (bf16[128,4096]{1,0:T(8,128)(2,1)S(1)}, bf16[128,4096]{1,0:T(8,128)(2,1)S(1)}, u32[]{:S(2)}, u32[]{:S(2)}) collective-permute-start(bf16[128,4096]{1,0:T(8,128)(2,1)S(1)} %collective-permute-done.7.refs_0_), channel_id=1, source_target_pairs={{0,14},{1,145},{2,0},{3,147},{4,2},{5,149},{6,4},{7,151},{8,6},{9,... | collective-permute-start | bytes 3145736 | tf_op jit(solution)/shard_map/ppermute | solution.py:55
  52.4 4.1 %collective-permute-done.12.refs_1_ = bf16[128,4096]{1,0:T(8,128)(2,1)} collective-permute-done((bf16[128,4096]{1,0:T(8,128)(2,1)S(1)}, bf16[128,4096]{1,0:T(8,128)(2,1)}, u32[]{:S(2)}, u32[]{:S(2)}) %collective-permute-start.12) | collective-permute-done | bytes 1048608 | tf_op jit(solution)/shard_map/ppermute | solution.py:55
  56.6 0.0 collective-permute-start.13
  56.6 0.1 fusion.38
  56.6 0.1 fusion.39
  56.7 0.0 copy-start
  56.7 2.2 %copy-done = bf16[512,4096]{1,0:T(8,128)(2,1)S(1)} copy-done((bf16[512,4096]{1,0:T(8,128)(2,1)S(1)}, bf16[512,4096]{1,0:T(8,128)(2,1)}, u32[]{:S(2)}) %copy-start) | copy-done | bytes 4194328
  58.9 5.1 %score.4 = (f32[8,512]{1,0:T(8,128)S(1)}, f32[8,512]{1,0:T(8,128)S(1)}) custom-call(f32[1,256]{1,0:T(1,128)S(1)} %bitcast.23, f32[1,512]{1,0:T(1,128)S(1)} %bitcast.17, f32[1,512]{1,0:T(1,128)S(1)} %collective-permute-done.other_wanted_ref, bf16[512,4096]{1,0:T(8,128)(2,1)S(1)} %copy-done, bf16[512,4096]{1,0:T(8,128)(2,1)} %collective-permute-done.1.other_ref, ...), custom_call_target="tpu_custom_call" | custom-call | flops 2147483648 | bytes 2097152 | tf_op jit(solution)/shard_map/score/pallas_call | solution.py:125
  64.0 3.7 %collective-permute-done.15.refs_1_ = bf16[128,4096]{1,0:T(8,128)(2,1)S(1)} collective-permute-done((bf16[128,4096]{1,0:T(8,128)(2,1)S(1)}, bf16[128,4096]{1,0:T(8,128)(2,1)S(1)}, u32[]{:S(2)}, u32[]{:S(2)}) %collective-permute-start.15) | collective-permute-done | bytes 1048608 | tf_op jit(solution)/shard_map/ppermute | solution.py:55
  67.7 4.9 %score.5 = (f32[8,512]{1,0:T(8,128)S(1)}, f32[8,512]{1,0:T(8,128)S(1)}) custom-call(f32[1,256]{1,0:T(1,128)S(1)} %bitcast.24, f32[1,512]{1,0:T(1,128)S(1)} %bitcast.18, f32[1,512]{1,0:T(1,128)S(1)} %collective-permute-done.other_wanted_ref, bf16[512,4096]{1,0:T(8,128)(2,1)S(1)} %copy-done.1, bf16[512,4096]{1,0:T(8,128)(2,1)} %collective-permute-done.1.other_ref, ...), custom_call_target="tpu_custom_call" | custom-call | flops 2147483648 | bytes 2097152 | tf_op jit(solution)/shard_map/score/pallas_call | solution.py:125
  72.6 5.2 %score.6 = (f32[8,512]{1,0:T(8,128)S(1)}, f32[8,512]{1,0:T(8,128)S(1)}) custom-call(f32[1,256]{1,0:T(1,128)S(1)} %bitcast.25, f32[1,512]{1,0:T(1,128)S(1)} %bitcast.19, f32[1,512]{1,0:T(1,128)S(1)} %collective-permute-done.other_wanted_ref, bf16[512,4096]{1,0:T(8,128)(2,1)S(1)} %copy-done.1, bf16[512,4096]{1,0:T(8,128)(2,1)} %collective-permute-done.1.other_ref, ...), custom_call_target="tpu_custom_call" | custom-call | flops 2147483648 | bytes 2097152 | tf_op jit(solution)/shard_map/score/pallas_call | solution.py:125
  77.7 1.2 %collective-permute-done.13.refs_1_ = bf16[128,4096]{1,0:T(8,128)(2,1)S(1)} collective-permute-done((bf16[128,4096]{1,0:T(8,128)(2,1)}, bf16[128,4096]{1,0:T(8,128)(2,1)S(1)}, u32[]{:S(2)}, u32[]{:S(2)}) %collective-permute-start.13) | collective-permute-done | bytes 1048608 | tf_op jit(solution)/shard_map/ppermute | solution.py:55
  78.9 4.8 %score.7 = (f32[8,512]{1,0:T(8,128)S(1)}, f32[8,512]{1,0:T(8,128)S(1)}) custom-call(f32[1,256]{1,0:T(1,128)S(1)} %bitcast.22, f32[1,512]{1,0:T(1,128)S(1)} %bitcast.20, f32[1,512]{1,0:T(1,128)S(1)} %collective-permute-done.other_wanted_ref, bf16[512,4096]{1,0:T(8,128)(2,1)S(1)} %copy-done.1, bf16[512,4096]{1,0:T(8,128)(2,1)} %collective-permute-done.1.other_ref, ...), custom_call_target="tpu_custom_call" | custom-call | flops 2147483648 | bytes 2097152 | tf_op jit(solution)/shard_map/score/pallas_call | solution.py:125
  83.8 5.1 %collective-permute-start.16 = (f32[8,512]{1,0:T(8,128)S(1)}, f32[8,512]{1,0:T(8,128)S(1)}, u32[]{:S(2)}, u32[]{:S(2)}) collective-permute-start(f32[8,512]{1,0:T(8,128)S(1)} %get-tuple-element.20), channel_id=1, source_target_pairs={{0,1},{1,0},{2,3},{3,2},{4,5},{5,4},{6,7},{7,6},{8,9},{9,8},{10,11... | collective-permute-start | bytes 49160 | tf_op jit(solution)/shard_map/ppermute | solution.py:39
  88.9 0.8 collective-permute-done.16.got_ref
  89.7 1.0 class_sums.1
  90.7 21.7 %all_to_all.9 = f32[256,1,128]{2,1,0:T(1,128)S(1)} all-to-all(f32[256,1,128]{2,1,0:T(1,128)S(1)} %bitcast.15), channel_id=1, replica_groups=mesh['xh'=2,'y'=4,'xl'=2,'z'=8,'core'=2] {'xh','y','xl','z','core'}, dimensions={0} | all-to-all | bytes 262144 | tf_op jit(solution)/shard_map/all_to_all | solution.py:215
  112.4 0.3 reduce_sum.9
  112.7 0.5 multiply_bitcast_fusion
  (39 shorter events, 0.3 us)
Async XLA Ops:
  0.0 46.2 %copy-start.12 = (s32[256]{0:T(256)S(1)}, s32[256]{0:T(256)}, u32[]{:S(2)}) copy-start(s32[256]{0:T(256)} %constant.330.clone) | copy-start | bytes 3076
  0.0 46.2 %copy-start.13 = (s32[256]{0:T(256)S(1)}, s32[256]{0:T(256)}, u32[]{:S(2)}) copy-start(s32[256]{0:T(256)} %constant.331.clone) | copy-start | bytes 3076
  0.0 49.0 %copy-start.10 = (s32[256]{0:T(256)S(1)}, s32[256]{0:T(256)}, u32[]{:S(2)}) copy-start(s32[256]{0:T(256)} %constant.332.clone) | copy-start | bytes 3076
  0.0 49.0 %copy-start.11 = (s32[256]{0:T(256)S(1)}, s32[256]{0:T(256)}, u32[]{:S(2)}) copy-start(s32[256]{0:T(256)} %constant.333.clone) | copy-start | bytes 3076
  0.0 56.5 %copy-start.8 = (s32[256]{0:T(256)S(1)}, s32[256]{0:T(256)}, u32[]{:S(2)}) copy-start(s32[256]{0:T(256)} %constant.334.clone) | copy-start | bytes 3076
  0.0 56.5 %copy-start.9 = (s32[256]{0:T(256)S(1)}, s32[256]{0:T(256)}, u32[]{:S(2)}) copy-start(s32[256]{0:T(256)} %constant.335.clone) | copy-start | bytes 3076
  0.0 56.6 %copy-start.6 = (s32[256]{0:T(256)S(1)}, s32[256]{0:T(256)}, u32[]{:S(2)}) copy-start(s32[256]{0:T(256)} %constant.336.clone) | copy-start | bytes 3076
  0.1 56.6 %copy-start.7 = (s32[256]{0:T(256)S(1)}, s32[256]{0:T(256)}, u32[]{:S(2)}) copy-start(s32[256]{0:T(256)} %constant.337.clone) | copy-start | bytes 3076
  0.1 42.4 %copy-start.4 = (s32[512]{0:T(512)S(1)}, s32[512]{0:T(512)}, u32[]{:S(2)}) copy-start(s32[512]{0:T(512)} %param.16) | copy-start | bytes 6148
  0.1 42.4 %copy-start.3 = (s32[512]{0:T(512)S(1)}, s32[512]{0:T(512)}, u32[]{:S(2)}) copy-start(s32[512]{0:T(512)} %param.17) | copy-start | bytes 6148
  0.1 42.4 %copy-start.5 = (s32[512]{0:T(512)S(1)}, s32[512]{0:T(512)}, u32[]{:S(2)}) copy-start(s32[512]{0:T(512)} %param.18) | copy-start | bytes 6148
  0.1 9.8 %collective-permute-start.2 = (bf16[8,4096]{1,0:T(8,128)(2,1)}, bf16[8,4096]{1,0:T(8,128)(2,1)S(1)}, u32[]{:S(2)}, u32[]{:S(2)}) collective-permute-start(bf16[8,4096]{1,0:T(8,128)(2,1)} %bitcast.27), channel_id=1, source_target_pairs={{0,8},{1,9},{2,10},{3,11},{4,12},{5,13},{6,14},{7,15},{8,0},{9,1},... | collective-permute-start | bytes 196616 | tf_op jit(solution)/shard_map/ppermute | solution.py:55
  7.9 48.8 %collective-permute-start.1 = (bf16[512,4096]{1,0:T(8,128)(2,1)}, bf16[512,4096]{1,0:T(8,128)(2,1)}, u32[]{:S(2)}, u32[]{:S(2)}) collective-permute-start(bf16[512,4096]{1,0:T(8,128)(2,1)} %particles_ref.1), channel_id=1, source_target_pairs={{0,1},{1,0},{2,3},{3,2},{4,5},{5,4},{6,7},{7,6},{8,9},{9,8},{10,11... | collective-permute-start | bytes 12582920 | tf_op jit(solution)/shard_map/ppermute | solution.py:39
  10.7 4.8 %collective-permute-start.3 = (bf16[16,4096]{1,0:T(8,128)(2,1)S(1)}, bf16[16,4096]{1,0:T(8,128)(2,1)S(1)}, u32[]{:S(2)}, u32[]{:S(2)}) collective-permute-start(bf16[16,4096]{1,0:T(8,128)(2,1)S(1)} %pad_maximum_fusion), channel_id=1, source_target_pairs={{0,144},{1,97},{2,146},{3,99},{4,148},{5,101},{6,150},{7,103},{8,1... | collective-permute-start | bytes 393224 | tf_op jit(solution)/shard_map/ppermute | solution.py:55
  13.6 6.7 %collective-permute-start.4 = (bf16[16,4096]{1,0:T(8,128)(2,1)S(1)}, bf16[16,4096]{1,0:T(8,128)(2,1)S(1)}, u32[]{:S(2)}, u32[]{:S(2)}) collective-permute-start(bf16[16,4096]{1,0:T(8,128)(2,1)S(1)} %pad_maximum_fusion), channel_id=1, source_target_pairs={{0,16},{1,33},{2,18},{3,35},{4,20},{5,37},{6,22},{7,39},{8,24},{9,... | collective-permute-start | bytes 393224 | tf_op jit(solution)/shard_map/ppermute | solution.py:55
  13.6 6.7 %collective-permute-start.5 = (bf16[16,4096]{1,0:T(8,128)(2,1)S(1)}, bf16[16,4096]{1,0:T(8,128)(2,1)S(1)}, u32[]{:S(2)}, u32[]{:S(2)}) collective-permute-start(bf16[16,4096]{1,0:T(8,128)(2,1)S(1)} %pad_maximum_fusion), channel_id=1, source_target_pairs={{0,128},{1,65},{2,130},{3,67},{4,132},{5,69},{6,134},{7,71},{8,136... | collective-permute-start | bytes 393224 | tf_op jit(solution)/shard_map/ppermute | solution.py:55
  20.3 10.6 %collective-permute-start.6 = (bf16[64,4096]{1,0:T(8,128)(2,1)S(1)}, bf16[64,4096]{1,0:T(8,128)(2,1)S(1)}, u32[]{:S(2)}, u32[]{:S(2)}) collective-permute-start(bf16[64,4096]{1,0:T(8,128)(2,1)S(1)} %get-tuple-element.21), channel_id=1, source_target_pairs={{0,96},{1,15},{2,98},{3,1},{4,100},{5,3},{6,102},{7,5},{8,104},{9,... | collective-permute-start | bytes 1572872 | tf_op jit(solution)/shard_map/ppermute | solution.py:55
  24.8 9.5 %collective-permute-start.9 = (bf16[64,4096]{1,0:T(8,128)(2,1)S(1)}, bf16[64,4096]{1,0:T(8,128)(2,1)S(1)}, u32[]{:S(2)}, u32[]{:S(2)}) collective-permute-start(bf16[64,4096]{1,0:T(8,128)(2,1)S(1)} %get-tuple-element.21), channel_id=1, source_target_pairs={{0,32},{1,3},{2,34},{3,5},{4,36},{5,7},{6,38},{7,9},{8,40},{9,11},... | collective-permute-start | bytes 1572872 | tf_op jit(solution)/shard_map/ppermute | solution.py:55
  31.0 6.5 %collective-permute-start.10 = (bf16[32,4096]{1,0:T(8,128)(2,1)S(1)}, bf16[32,4096]{1,0:T(8,128)(2,1)S(1)}, u32[]{:S(2)}, u32[]{:S(2)}) collective-permute-start(bf16[32,4096]{1,0:T(8,128)(2,1)S(1)} %slice.8), channel_id=1, source_target_pairs={{0,96},{1,15},{2,98},{3,1},{4,100},{5,3},{6,102},{7,5},{8,104},{9,... | collective-permute-start | bytes 786440 | tf_op jit(solution)/shard_map/ppermute | solution.py:55
  34.4 6.8 %collective-permute-start.11 = (bf16[32,4096]{1,0:T(8,128)(2,1)S(1)}, bf16[32,4096]{1,0:T(8,128)(2,1)S(1)}, u32[]{:S(2)}, u32[]{:S(2)}) collective-permute-start(bf16[32,4096]{1,0:T(8,128)(2,1)S(1)} %slice.9), channel_id=1, source_target_pairs={{0,32},{1,3},{2,34},{3,5},{4,36},{5,7},{6,38},{7,9},{8,40},{9,11},... | collective-permute-start | bytes 786440 | tf_op jit(solution)/shard_map/ppermute | solution.py:55
  34.5 14.6 %collective-permute-start.7 = (bf16[128,4096]{1,0:T(8,128)(2,1)S(1)}, bf16[128,4096]{1,0:T(8,128)(2,1)S(1)}, u32[]{:S(2)}, u32[]{:S(2)}) collective-permute-start(bf16[128,4096]{1,0:T(8,128)(2,1)S(1)} %constant_dynamic-update-slice_fusion.5.refs_0_), channel_id=1, source_target_pairs={{0,14},{1,145},{2,0},{3,147},{4,2},{5,149},{6,4},{7,151},{8,6},{9,... | collective-permute-start | bytes 3145736 | tf_op jit(solution)/shard_map/ppermute | solution.py:55
  41.2 15.3 %collective-permute-start.12 = (bf16[128,4096]{1,0:T(8,128)(2,1)S(1)}, bf16[128,4096]{1,0:T(8,128)(2,1)}, u32[]{:S(2)}, u32[]{:S(2)}) collective-permute-start(bf16[128,4096]{1,0:T(8,128)(2,1)S(1)} %constant_dynamic-update-slice_fusion.11.refs_1_), channel_id=1, source_target_pairs={{0,2},{1,17},{2,4},{3,19},{4,6},{5,21},{6,8},{7,23},{8,10},{9,25},... | collective-permute-start | bytes 3145736 | tf_op jit(solution)/shard_map/ppermute | solution.py:55
  42.5 4.6 %collective-permute-start = (f32[1,512]{1,0:T(1,128)S(1)}, f32[1,512]{1,0:T(1,128)S(1)}, u32[]{:S(2)}, u32[]{:S(2)}) collective-permute-start(f32[1,512]{1,0:T(1,128)S(1)} %bitcast.16), channel_id=1, source_target_pairs={{0,1},{1,0},{2,3},{3,2},{4,5},{5,4},{6,7},{7,6},{8,9},{9,8},{10,11... | collective-permute-start | bytes 6152 | tf_op jit(solution)/shard_map/ppermute | solution.py:39
  46.2 21.5 %collective-permute-start.15 = (bf16[128,4096]{1,0:T(8,128)(2,1)S(1)}, bf16[128,4096]{1,0:T(8,128)(2,1)S(1)}, u32[]{:S(2)}, u32[]{:S(2)}) collective-permute-start(bf16[128,4096]{1,0:T(8,128)(2,1)S(1)} %constant_dynamic-update-slice_fusion.5.refs_0_), channel_id=1, source_target_pairs={{0,2},{1,17},{2,4},{3,19},{4,6},{5,21},{6,8},{7,23},{8,10},{9,25},... | collective-permute-start | bytes 3145736 | tf_op jit(solution)/shard_map/ppermute | solution.py:55
  47.0 25.5 %collective-permute-start.14 = (bf16[128,4096]{1,0:T(8,128)(2,1)S(1)}, bf16[128,4096]{1,0:T(8,128)(2,1)S(1)}, u32[]{:S(2)}, u32[]{:S(2)}) collective-permute-start(bf16[128,4096]{1,0:T(8,128)(2,1)S(1)} %constant_dynamic-update-slice_fusion.11.refs_1_), channel_id=1, source_target_pairs={{0,14},{1,145},{2,0},{3,147},{4,2},{5,149},{6,4},{7,151},{8,6},{9,... | collective-permute-start | bytes 3145736 | tf_op jit(solution)/shard_map/ppermute | solution.py:55
  49.1 28.6 %collective-permute-start.8 = (bf16[128,4096]{1,0:T(8,128)(2,1)S(1)}, bf16[128,4096]{1,0:T(8,128)(2,1)S(1)}, u32[]{:S(2)}, u32[]{:S(2)}) collective-permute-start(bf16[128,4096]{1,0:T(8,128)(2,1)S(1)} %collective-permute-done.7.refs_0_), channel_id=1, source_target_pairs={{0,14},{1,145},{2,0},{3,147},{4,2},{5,149},{6,4},{7,151},{8,6},{9,... | collective-permute-start | bytes 3145736 | tf_op jit(solution)/shard_map/ppermute | solution.py:55
  56.6 22.4 %collective-permute-start.13 = (bf16[128,4096]{1,0:T(8,128)(2,1)}, bf16[128,4096]{1,0:T(8,128)(2,1)S(1)}, u32[]{:S(2)}, u32[]{:S(2)}) collective-permute-start(bf16[128,4096]{1,0:T(8,128)(2,1)} %collective-permute-done.12.refs_1_), channel_id=1, source_target_pairs={{0,2},{1,17},{2,4},{3,19},{4,6},{5,21},{6,8},{7,23},{8,10},{9,25},... | collective-permute-start | bytes 3145736 | tf_op jit(solution)/shard_map/ppermute | solution.py:55
  56.7 2.2 %copy-start = (bf16[512,4096]{1,0:T(8,128)(2,1)S(1)}, bf16[512,4096]{1,0:T(8,128)(2,1)}, u32[]{:S(2)}) copy-start(bf16[512,4096]{1,0:T(8,128)(2,1)} %particles_ref.1) | copy-start | bytes 12582916
  58.9 8.8 %copy-start.1 = (bf16[512,4096]{1,0:T(8,128)(2,1)S(1)}, bf16[512,4096]{1,0:T(8,128)(2,1)}, u32[]{:S(2)}) copy-start(bf16[512,4096]{1,0:T(8,128)(2,1)} %particles_ref.1) | copy-start | bytes 12582916
  78.9 10.8 %copy-start.2 = (f32[512]{0:T(512)S(1)}, f32[512]{0:T(512)}, u32[]{:S(2)}) copy-start(f32[512]{0:T(512)} %param.19) | copy-start | bytes 6148
  83.8 5.9 %collective-permute-start.16 = (f32[8,512]{1,0:T(8,128)S(1)}, f32[8,512]{1,0:T(8,128)S(1)}, u32[]{:S(2)}, u32[]{:S(2)}) collective-permute-start(f32[8,512]{1,0:T(8,128)S(1)} %get-tuple-element.20), channel_id=1, source_target_pairs={{0,1},{1,0},{2,3},{3,2},{4,5},{5,4},{6,7},{7,6},{8,9},{9,8},{10,11... | collective-permute-start | bytes 49160 | tf_op jit(solution)/shard_map/ppermute | solution.py:39

commit v4 on v3

--- a/solution.py
+++ b/solution.py
@@ -60,14 +60,6 @@
         jnp.concatenate([p.rows for p in pieces], axis=0),
         [np.concatenate([p.offsets[c] for p in pieces], axis=0) for c in range(CORES)],
     )
-
-
-def ring(piece, axes):
-    half = piece.rows.shape[0] // 2
-    ahead, behind = piece.fetch(axes, 1), piece.fetch(axes, -1)
-    far_a = ahead.part(0, half).fetch(axes, 1)
-    far_b = behind.part(half, 2 * half).fetch(axes, -1)
-    return [piece, ahead, behind, far_a, far_b]
 
 
 def row_ids(pieces, here, local):
@@ -89,13 +81,22 @@
 
 def score_kernel(scale, n, first, ids_ref, wanted_ref, other_wanted_ref, own_ref, other_ref, *refs):
     pieces, refs = refs[:n], refs[n:]
-    before, after = (None, None) if first else refs[:2], refs[-2:]
+    if first:
+        before, (mine, theirs, kept, arrived) = None, refs
+        copy = pltpu.make_async_copy(other_ref, kept, arrived)
+        copy.start()
+    else:
+        before, (mine, theirs), kept = refs[:2], refs[2:], other_ref
     count = own_ref.shape[0]
     rows = sum(piece.shape[0] for piece in pieces)
     column = jnp.broadcast_to(ids_ref[...], (LANES, rows)).T
     ids = jnp.concatenate([column] * (BLOCK // LANES), axis=1)
     held = jnp.concatenate([piece[...] for piece in pieces], axis=0)
-    for side, (particles, wanted) in enumerate(((own_ref, wanted_ref), (other_ref, other_wanted_ref))):
+    for side, (particles, wanted, after) in enumerate(
+        ((own_ref, wanted_ref, mine), (kept, other_wanted_ref, theirs))
+    ):
+        if first and side == 1:
+            copy.wait()
         for start in range(0, count, BLOCK):
             cols = slice(start, start + BLOCK)
             block = particles[cols, :]
@@ -112,21 +113,28 @@
             if not first:
                 total = total + before[side][1:2, cols] * jnp.exp(old_top - top)
                 chosen = chosen + before[side][2:3, cols]
-            after[side][0:1, cols] = top
-            after[side][1:2, cols] = total
-            after[side][2:3, cols] = chosen
+            after[0:1, cols] = top
+            after[1:2, cols] = total
+            after[2:3, cols] = chosen
 
 
 def score(pieces, ids, wanted, other_wanted, own, other, before, scale):
     count, voxels = own.shape
     rows = sum(p.rows.shape[0] for p in pieces)
+    first = before is None
     whole = pl.BlockSpec(memory_space=pltpu.VMEM)
     operands = [ids, wanted, other_wanted, own, other, *(p.rows for p in pieces), *(before or ())]
+    in_specs = [whole] * len(operands)
+    out_shape = [jax.ShapeDtypeStruct((8, count), jnp.float32)] * 2
+    if first:
+        in_specs[4] = pl.BlockSpec(memory_space=pl.ANY)
+        out_shape.append(jax.ShapeDtypeStruct(other.shape, other.dtype))
     return pl.pallas_call(
-        functools.partial(score_kernel, scale, len(pieces), before is None),
-        out_shape=[jax.ShapeDtypeStruct((8, count), jnp.float32)] * 2,
-        in_specs=[whole] * len(operands),
-        out_specs=[whole] * 2,
+        functools.partial(score_kernel, scale, len(pieces), first),
+        out_shape=out_shape,
+        in_specs=in_specs,
+        out_specs=[whole] * len(out_shape),
+        scratch_shapes=[pltpu.SemaphoreType.DMA] if first else [],
         compiler_params=pltpu.CompilerParams(vmem_limit_bytes=16 << 20),
         cost_estimate=pl.CostEstimate(
             flops=4 * rows * count * voxels, transcendentals=2 * rows * count, bytes_accessed=rows * voxels * 2
@@ -196,17 +204,29 @@
     piece = join([piece, piece.fetch((AZ, AZ), ZN // 2)])
     first = STAGES[0]
     piece = join([piece, piece.fetch(first, 1), piece.fetch(first, -1), piece.fetch(first, 2)])
-    near, ahead, behind, far_a, far_b = ring(piece, STAGES[1])
+
+    def take(group, kept, stats):
+        ids = row_ids(group, here, local)
+        out = score(group, ids, wanted, other_wanted, particles, kept, stats, scale)
+        return (out[2] if stats is None else kept), out[:2]
+
+    near, half = piece, piece.rows.shape[0] // 2
+    ahead, behind = near.fetch(STAGES[1], 1), near.fetch(STAGES[1], -1)
+    kept, stats = take([near], other, None)
+    ahead.rows, behind.rows, stats = lax.optimization_barrier((ahead.rows, behind.rows, stats))
+    far_a = ahead.part(0, half).fetch(STAGES[1], 1)
+    far_b = behind.part(half, 2 * half).fetch(STAGES[1], -1)
     last = STAGES[2]
-    one, two = join([near, ahead]), join([behind, far_a, far_b])
-    ahead_one, behind_one = one.fetch(last, 1), one.fetch(last, -1)
-    ahead_two, behind_two = two.fetch(last, 1), two.fetch(last, -1)
-    far_one, far_two = ahead_one.fetch(last, 1), behind_two.fetch(last, -1)
-
-    stats = None
-    for group in ((one, two), (ahead_one, behind_one), (ahead_two, behind_two), (far_one, far_two)):
-        ids = row_ids(group, here, local)
-        stats = score(group, ids, wanted, other_wanted, particles, other, stats, scale)
+    chunks = [near, join([ahead, behind]), join([far_a, far_b])]
+    next_, prev = [c.fetch(last, 1) for c in chunks], [c.fetch(last, -1) for c in chunks]
+    far = [prev[0].fetch(last, -1), next_[1].fetch(last, 1), prev[2].fetch(last, -1)]
+    for group in (
+        chunks[1:] + [next_[0], prev[0]],
+        [next_[1], prev[1]],
+        [next_[2], prev[2], far[0]],
+        far[1:],
+    ):
+        kept, stats = take(group, kept, stats)
     mine, theirs = stats
     got = swap_cores(theirs)
     key = class_ids + classes * (offsets + SHIFT)

time: 114 us -> 113 us (level)
  Pallas kernels: 21 us -> 17.9 us
  starting transfers between devices: 39.1 us -> 36.8 us
  other arithmetic: 1.88 us -> 4 us
  waiting for transfers between devices: 26.1 us -> 27.6 us
    ppermute x3, starting transfers between devices: 9.8 us -> 6.67 us  [swap_cores(): return lax.ppermute(value, ALL, pairs(lambda at, core: (at, 1 - core)))]
    pallas_call x4 -> x5, Pallas kernels: 20 us -> 16.9 us  [score(): pl.pallas_call(functools.partial(score_kernel, scale, len(pieces), first)...]
    ppermute x14 -> x17, waiting for transfers between devices: 24.5 us -> 26.7 us  [fetch(): return Piece(lax.ppermute(self.rows, ALL, pairs(move)), moved)]
    ppermute x14 -> x17, starting transfers between devices: 29.3 us -> 30.1 us  [fetch(): return Piece(lax.ppermute(self.rows, ALL, pairs(move)), moved)]
    unnamed x34 -> x24, local copies, waits for them, and re-layouts: 3.19 us -> 3.19 us
  transfers between devices with their start and end apart: 17 -> 20, of which waited for: 12 -> 9; matrix products, arithmetic and copies ran while one was open for 2% -> 4% of each run, Pallas kernels for 13% -> 12%
where the time goes in v4:
time: 113 us; the launch traced here: 112 us
  starting transfers between devices  36.8 us (33%)
  waiting for transfers between devices  27.6 us (24%)
  blocking collectives  22.5 us (20%)
  Pallas kernels  17.9 us (16%)
  other arithmetic  4 us (4%)
  local copies, waits for them, and re-layouts  3.3 us (3%)
    ppermute x17, starting transfers between devices, fetch(): return Piece(lax.ppermute(self.rows, ALL, pairs(move)), moved)  30.1 us
    ppermute x17, waiting for transfers between devices, fetch(): return Piece(lax.ppermute(self.rows, ALL, pairs(move)), moved)  26.7 us
    all_to_all x1, blocking collectives, body(): lax.all_to_all(sent, ALL, 0, 0, tiled=True)  22.5 us
    pallas_call x5, Pallas kernels, score(): pl.pallas_call(functools.partial(score_kernel, scale, len(pieces), first)...  16.9 us
    ppermute x3, starting transfers between devices, swap_cores(): return lax.ppermute(value, ALL, pairs(lambda at, core: (at, 1 - core)))  6.67 us
    unnamed x24, local copies, waits for them, and re-layouts  3.19 us
  transfers between devices with their start and end apart: 20, of which 9 were waited for; matrix products, arithmetic and copies ran while one was open for 4% of the time, Pallas kernels for 12%

profile of v4, /device:TPU:1, one launch (start us, length us, event | category | flops | bytes accessed | tf_op | source)
XLA Modules:
  0.0 112.3 jit_solution(4489007969012418959)
XLA Ops:
  0.0 3.2 %collective-permute-start.1 = (bf16[512,4096]{1,0:T(8,128)(2,1)}, bf16[512,4096]{1,0:T(8,128)(2,1)}, u32[]{:S(2)}, u32[]{:S(2)}) collective-permute-start(bf16[512,4096]{1,0:T(8,128)(2,1)} %particles_ref.1), channel_id=1, source_target_pairs={{0,1},{1,0},{2,3},{3,2},{4,5},{5,4},{6,7},{7,6},{8,9},{9,8},{10,11... | collective-permute-start | bytes 12582920 | tf_op jit(solution)/shard_map/ppermute | solution.py:39
  3.2 5.2 %collective-permute-start.2 = (bf16[8,4096]{1,0:T(8,128)(2,1)}, bf16[8,4096]{1,0:T(8,128)(2,1)S(1)}, u32[]{:S(2)}, u32[]{:S(2)}) collective-permute-start(bf16[8,4096]{1,0:T(8,128)(2,1)} %bitcast.27), channel_id=1, source_target_pairs={{0,8},{1,9},{2,10},{3,11},{4,12},{5,13},{6,14},{7,15},{8,0},{9,1},... | collective-permute-start | bytes 196616 | tf_op jit(solution)/shard_map/ppermute | solution.py:55
  8.4 0.9 constant_dynamic-update-slice_fusion.4
  9.3 1.8 %collective-permute-done.2 = bf16[8,4096]{1,0:T(8,128)(2,1)S(1)} collective-permute-done((bf16[8,4096]{1,0:T(8,128)(2,1)}, bf16[8,4096]{1,0:T(8,128)(2,1)S(1)}, u32[]{:S(2)}, u32[]{:S(2)}) %collective-permute-start.2) | collective-permute-done | bytes 65568 | tf_op jit(solution)/shard_map/ppermute | solution.py:55
  11.1 0.8 pad_maximum_fusion
  11.9 2.8 %collective-permute-start.3 = (bf16[16,4096]{1,0:T(8,128)(2,1)S(1)}, bf16[16,4096]{1,0:T(8,128)(2,1)S(1)}, u32[]{:S(2)}, u32[]{:S(2)}) collective-permute-start(bf16[16,4096]{1,0:T(8,128)(2,1)S(1)} %pad_maximum_fusion), channel_id=1, source_target_pairs={{0,144},{1,97},{2,146},{3,99},{4,148},{5,101},{6,150},{7,103},{8,1... | collective-permute-start | bytes 393224 | tf_op jit(solution)/shard_map/ppermute | solution.py:55
  14.8 1.6 %collective-permute-start.5 = (bf16[16,4096]{1,0:T(8,128)(2,1)S(1)}, bf16[16,4096]{1,0:T(8,128)(2,1)S(1)}, u32[]{:S(2)}, u32[]{:S(2)}) collective-permute-start(bf16[16,4096]{1,0:T(8,128)(2,1)S(1)} %pad_maximum_fusion), channel_id=1, source_target_pairs={{0,128},{1,65},{2,130},{3,67},{4,132},{5,69},{6,134},{7,71},{8,136... | collective-permute-start | bytes 393224 | tf_op jit(solution)/shard_map/ppermute | solution.py:55
  16.4 0.3 collective-permute-done.3
  16.7 4.8 %collective-permute-done.4 = bf16[16,4096]{1,0:T(8,128)(2,1)S(1)} collective-permute-done((bf16[16,4096]{1,0:T(8,128)(2,1)S(1)}, bf16[16,4096]{1,0:T(8,128)(2,1)S(1)}, u32[]{:S(2)}, u32[]{:S(2)}) %collective-permute-start.4) | collective-permute-done | bytes 131104 | tf_op jit(solution)/shard_map/ppermute | solution.py:55
  21.5 4.3 %collective-permute-start.6 = (bf16[64,4096]{1,0:T(8,128)(2,1)S(1)}, bf16[64,4096]{1,0:T(8,128)(2,1)S(1)}, u32[]{:S(2)}, u32[]{:S(2)}) collective-permute-start(bf16[64,4096]{1,0:T(8,128)(2,1)S(1)} %constant_dynamic-update-slice_fusion.refs_0_), channel_id=1, source_target_pairs={{0,96},{1,15},{2,98},{3,1},{4,100},{5,3},{6,102},{7,5},{8,104},{9,... | collective-permute-start | bytes 1572872 | tf_op jit(solution)/shard_map/ppermute | solution.py:55
  25.8 0.7 add_convert_fusion
  26.5 0.4 collective-permute-start
  26.9 0.7 fusion.13
  27.6 0.7 convert_bitcast_fusion.ids_ref
  28.4 0.6 collective-permute-start.15
  29.0 2.1 %collective-permute-start.18 = (bf16[64,4096]{1,0:T(8,128)(2,1)S(1)}, bf16[64,4096]{1,0:T(8,128)(2,1)S(1)}, u32[]{:S(2)}, u32[]{:S(2)}) collective-permute-start(bf16[64,4096]{1,0:T(8,128)(2,1)S(1)} %constant_dynamic-update-slice_fusion.refs_0_), channel_id=1, source_target_pairs={{0,14},{1,145},{2,0},{3,147},{4,2},{5,149},{6,4},{7,151},{8,6},{9,... | collective-permute-start | bytes 1572872 | tf_op jit(solution)/shard_map/ppermute | solution.py:55
  31.1 2.2 %copy-done = bf16[512,4096]{1,0:T(8,128)(2,1)S(1)} copy-done((bf16[512,4096]{1,0:T(8,128)(2,1)S(1)}, bf16[512,4096]{1,0:T(8,128)(2,1)}, u32[]{:S(2)}) %copy-start) | copy-done | bytes 4194328
  33.3 4.8 %score.5 = (f32[8,512]{1,0:T(8,128)S(1)}, f32[8,512]{1,0:T(8,128)S(1)}, bf16[512,4096]{1,0:T(8,128)(2,1)S(1)}) custom-call(f32[1,64]{1,0:T(1,128)S(1)} %convert_bitcast_fusion.ids_ref, f32[1,512]{1,0:T(1,128)S(1)} %bitcast.17, f32[1,512]{1,0:T(1,128)S(1)} %collective-permute-done.other_wanted_ref, bf16[512,4096]{1,0:T(8,128)(2,1)S(1)} %copy-done, ...), custom_call_target="tpu_custom_call" | custom-call | flops 536870912 | bytes 524288 | tf_op jit(solution)/shard_map/score/pallas_call | solution.py:132
  38.1 0.0 copy-start.5
  38.2 0.0 copy-start.6
  38.2 0.0 copy-start.3
  38.2 0.0 copy-start.4
  38.3 4.3 %collective-permute-start.10 = (bf16[32,4096]{1,0:T(8,128)(2,1)S(1)}, bf16[32,4096]{1,0:T(8,128)(2,1)S(1)}, u32[]{:S(2)}, u32[]{:S(2)}) collective-permute-start(bf16[32,4096]{1,0:T(8,128)(2,1)S(1)} %slice.6), channel_id=1, source_target_pairs={{0,96},{1,15},{2,98},{3,1},{4,100},{5,3},{6,102},{7,5},{8,104},{9,... | collective-permute-start | bytes 786440 | tf_op jit(solution)/shard_map/ppermute | solution.py:55
  42.7 0.1 collective-permute-start.17
  42.8 2.7 %collective-permute-start.8 = (bf16[128,4096]{1,0:T(8,128)(2,1)S(1)}, bf16[128,4096]{1,0:T(8,128)(2,1)S(1)}, u32[]{:S(2)}, u32[]{:S(2)}) collective-permute-start(bf16[128,4096]{1,0:T(8,128)(2,1)S(1)} %constant_dynamic-update-slice_fusion.5.refs_0_), channel_id=1, source_target_pairs={{0,14},{1,145},{2,0},{3,147},{4,2},{5,149},{6,4},{7,151},{8,6},{9,... | collective-permute-start | bytes 3145736 | tf_op jit(solution)/shard_map/ppermute | solution.py:55
  45.4 0.5 collective-permute-done.10
  46.0 10.0 %collective-permute-done.11 = bf16[32,4096]{1,0:T(8,128)(2,1)S(1)} collective-permute-done((bf16[32,4096]{1,0:T(8,128)(2,1)S(1)}, bf16[32,4096]{1,0:T(8,128)(2,1)S(1)}, u32[]{:S(2)}, u32[]{:S(2)}) %collective-permute-start.11) | collective-permute-done | bytes 262176 | tf_op jit(solution)/shard_map/ppermute | solution.py:55
  56.0 0.3 collective-permute-start.12
  56.3 0.1 fusion.47
  56.3 0.8 collective-permute-done.8.refs_0_
  57.2 3.4 %collective-permute-start.9 = (bf16[128,4096]{1,0:T(8,128)(2,1)S(1)}, bf16[128,4096]{1,0:T(8,128)(2,1)S(1)}, u32[]{:S(2)}, u32[]{:S(2)}) collective-permute-start(bf16[128,4096]{1,0:T(8,128)(2,1)S(1)} %collective-permute-done.8.refs_0_), channel_id=1, source_target_pairs={{0,14},{1,145},{2,0},{3,147},{4,2},{5,149},{6,4},{7,151},{8,6},{9,... | collective-permute-start | bytes 3145736 | tf_op jit(solution)/shard_map/ppermute | solution.py:55
  60.6 0.1 fusion.48
  60.7 0.1 collective-permute-start.16
  60.8 2.7 %collective-permute-start.14 = (bf16[64,4096]{1,0:T(8,128)(2,1)S(1)}, bf16[64,4096]{1,0:T(8,128)(2,1)S(1)}, u32[]{:S(2)}, u32[]{:S(2)}) collective-permute-start(bf16[64,4096]{1,0:T(8,128)(2,1)S(1)} %constant_dynamic-update-slice_fusion.7.refs_1_), channel_id=1, source_target_pairs={{0,14},{1,145},{2,0},{3,147},{4,2},{5,149},{6,4},{7,151},{8,6},{9,... | collective-permute-start | bytes 1572872 | tf_op jit(solution)/shard_map/ppermute | solution.py:55
  63.4 0.1 fusion.49
  63.5 2.3 %collective-permute-done.12.refs_1_ = bf16[64,4096]{1,0:T(8,128)(2,1)S(1)} collective-permute-done((bf16[64,4096]{1,0:T(8,128)(2,1)S(1)}, bf16[64,4096]{1,0:T(8,128)(2,1)S(1)}, u32[]{:S(2)}, u32[]{:S(2)}) %collective-permute-start.12) | collective-permute-done | bytes 524320 | tf_op jit(solution)/shard_map/ppermute | solution.py:55
  65.8 3.3 %score.6 = (f32[8,512]{1,0:T(8,128)S(1)}, f32[8,512]{1,0:T(8,128)S(1)}) custom-call(f32[1,320]{1,0:T(1,128)S(1)} %broadcast_in_dim.32.ids_ref, f32[1,512]{1,0:T(1,128)S(1)} %bitcast.18, f32[1,512]{1,0:T(1,128)S(1)} %collective-permute-done.other_wanted_ref, bf16[512,4096]{1,0:T(8,128)(2,1)S(1)} %copy-done.1, ...), custom_call_target="tpu_custom_call" | custom-call | flops 2684354560 | bytes 2621440 | tf_op jit(solution)/shard_map/score/pallas_call | solution.py:132
  69.1 2.7 %score.7 = (f32[8,512]{1,0:T(8,128)S(1)}, f32[8,512]{1,0:T(8,128)S(1)}) custom-call(f32[1,256]{1,0:T(1,128)S(1)} %bitcast.25, f32[1,512]{1,0:T(1,128)S(1)} %bitcast.19, f32[1,512]{1,0:T(1,128)S(1)} %collective-permute-done.other_wanted_ref, bf16[512,4096]{1,0:T(8,128)(2,1)S(1)} %copy-done.1, bf16[512,4096]{1,0:T(8,128)(2,1)S(1)} %get-tuple-element.20.other_ref, ...), custom_call_target="tpu_custom_call" | custom-call | flops 2147483648 | bytes 2097152 | tf_op jit(solution)/shard_map/score/pallas_call | solution.py:132
  71.7 6.2 %collective-permute-done.14.refs_0_ = bf16[64,4096]{1,0:T(8,128)(2,1)S(1)} collective-permute-done((bf16[64,4096]{1,0:T(8,128)(2,1)S(1)}, bf16[64,4096]{1,0:T(8,128)(2,1)S(1)}, u32[]{:S(2)}, u32[]{:S(2)}) %collective-permute-start.14) | collective-permute-done | bytes 524320 | tf_op jit(solution)/shard_map/ppermute | solution.py:55
  78.0 3.1 %score.8 = (f32[8,512]{1,0:T(8,128)S(1)}, f32[8,512]{1,0:T(8,128)S(1)}) custom-call(f32[1,192]{1,0:T(1,128)S(1)} %bitcast.24, f32[1,512]{1,0:T(1,128)S(1)} %bitcast.20, f32[1,512]{1,0:T(1,128)S(1)} %collective-permute-done.other_wanted_ref, bf16[512,4096]{1,0:T(8,128)(2,1)S(1)} %copy-done.1, bf16[512,4096]{1,0:T(8,128)(2,1)S(1)} %get-tuple-element.20.other_ref, ...), custom_call_target="tpu_custom_call" | custom-call | flops 1610612736 | bytes 1572864 | tf_op jit(solution)/shard_map/score/pallas_call | solution.py:132
  81.1 0.0 copy-start.2
  81.1 3.1 %score.9 = (f32[8,512]{1,0:T(8,128)S(1)}, f32[8,512]{1,0:T(8,128)S(1)}) custom-call(f32[1,192]{1,0:T(1,128)S(1)} %bitcast.23, f32[1,512]{1,0:T(1,128)S(1)} %bitcast.21, f32[1,512]{1,0:T(1,128)S(1)} %collective-permute-done.other_wanted_ref, bf16[512,4096]{1,0:T(8,128)(2,1)S(1)} %copy-done.1, bf16[512,4096]{1,0:T(8,128)(2,1)S(1)} %get-tuple-element.20.other_ref, ...), custom_call_target="tpu_custom_call" | custom-call | flops 1610612736 | bytes 1572864 | tf_op jit(solution)/shard_map/score/pallas_call | solution.py:132
  84.2 3.0 %collective-permute-start.19 = (f32[8,512]{1,0:T(8,128)S(1)}, f32[8,512]{1,0:T(8,128)S(1)}, u32[]{:S(2)}, u32[]{:S(2)}) collective-permute-start(f32[8,512]{1,0:T(8,128)S(1)} %get-tuple-element.34), channel_id=1, source_target_pairs={{0,1},{1,0},{2,3},{3,2},{4,5},{5,4},{6,7},{7,6},{8,9},{9,8},{10,11... | collective-permute-start | bytes 49160 | tf_op jit(solution)/shard_map/ppermute | solution.py:39
  87.2 0.8 collective-permute-done.19.got_ref
  88.0 1.0 class_sums.1
  89.1 22.5 %all_to_all.9 = f32[256,1,128]{2,1,0:T(1,128)S(1)} all-to-all(f32[256,1,128]{2,1,0:T(1,128)S(1)} %bitcast.15), channel_id=1, replica_groups=mesh['xh'=2,'y'=4,'xl'=2,'z'=8,'core'=2] {'xh','y','xl','z','core'}, dimensions={0} | all-to-all | bytes 262144 | tf_op jit(solution)/shard_map/all_to_all | solution.py:235
  111.5 0.3 reduce_sum.9
  111.8 0.5 multiply_bitcast_fusion
  (38 shorter events, 0.2 us)
Async XLA Ops:
  0.0 31.1 %collective-permute-start.1 = (bf16[512,4096]{1,0:T(8,128)(2,1)}, bf16[512,4096]{1,0:T(8,128)(2,1)}, u32[]{:S(2)}, u32[]{:S(2)}) collective-permute-start(bf16[512,4096]{1,0:T(8,128)(2,1)} %particles_ref.1), channel_id=1, source_target_pairs={{0,1},{1,0},{2,3},{3,2},{4,5},{5,4},{6,7},{7,6},{8,9},{9,8},{10,11... | collective-permute-start | bytes 12582920 | tf_op jit(solution)/shard_map/ppermute | solution.py:39
  3.2 7.8 %collective-permute-start.2 = (bf16[8,4096]{1,0:T(8,128)(2,1)}, bf16[8,4096]{1,0:T(8,128)(2,1)S(1)}, u32[]{:S(2)}, u32[]{:S(2)}) collective-permute-start(bf16[8,4096]{1,0:T(8,128)(2,1)} %bitcast.27), channel_id=1, source_target_pairs={{0,8},{1,9},{2,10},{3,11},{4,12},{5,13},{6,14},{7,15},{8,0},{9,1},... | collective-permute-start | bytes 196616 | tf_op jit(solution)/shard_map/ppermute | solution.py:55
  11.9 4.8 %collective-permute-start.3 = (bf16[16,4096]{1,0:T(8,128)(2,1)S(1)}, bf16[16,4096]{1,0:T(8,128)(2,1)S(1)}, u32[]{:S(2)}, u32[]{:S(2)}) collective-permute-start(bf16[16,4096]{1,0:T(8,128)(2,1)S(1)} %pad_maximum_fusion), channel_id=1, source_target_pairs={{0,144},{1,97},{2,146},{3,99},{4,148},{5,101},{6,150},{7,103},{8,1... | collective-permute-start | bytes 393224 | tf_op jit(solution)/shard_map/ppermute | solution.py:55
  14.8 6.7 %collective-permute-start.4 = (bf16[16,4096]{1,0:T(8,128)(2,1)S(1)}, bf16[16,4096]{1,0:T(8,128)(2,1)S(1)}, u32[]{:S(2)}, u32[]{:S(2)}) collective-permute-start(bf16[16,4096]{1,0:T(8,128)(2,1)S(1)} %pad_maximum_fusion), channel_id=1, source_target_pairs={{0,16},{1,33},{2,18},{3,35},{4,20},{5,37},{6,22},{7,39},{8,24},{9,... | collective-permute-start | bytes 393224 | tf_op jit(solution)/shard_map/ppermute | solution.py:55
  14.8 6.7 %collective-permute-start.5 = (bf16[16,4096]{1,0:T(8,128)(2,1)S(1)}, bf16[16,4096]{1,0:T(8,128)(2,1)S(1)}, u32[]{:S(2)}, u32[]{:S(2)}) collective-permute-start(bf16[16,4096]{1,0:T(8,128)(2,1)S(1)} %pad_maximum_fusion), channel_id=1, source_target_pairs={{0,128},{1,65},{2,130},{3,67},{4,132},{5,69},{6,134},{7,71},{8,136... | collective-permute-start | bytes 393224 | tf_op jit(solution)/shard_map/ppermute | solution.py:55
  21.5 16.7 %collective-permute-start.6 = (bf16[64,4096]{1,0:T(8,128)(2,1)S(1)}, bf16[64,4096]{1,0:T(8,128)(2,1)S(1)}, u32[]{:S(2)}, u32[]{:S(2)}) collective-permute-start(bf16[64,4096]{1,0:T(8,128)(2,1)S(1)} %constant_dynamic-update-slice_fusion.refs_0_), channel_id=1, source_target_pairs={{0,96},{1,15},{2,98},{3,1},{4,100},{5,3},{6,102},{7,5},{8,104},{9,... | collective-permute-start | bytes 1572872 | tf_op jit(solution)/shard_map/ppermute | solution.py:55
  25.8 12.4 %collective-permute-start.7 = (bf16[64,4096]{1,0:T(8,128)(2,1)S(1)}, bf16[64,4096]{1,0:T(8,128)(2,1)S(1)}, u32[]{:S(2)}, u32[]{:S(2)}) collective-permute-start(bf16[64,4096]{1,0:T(8,128)(2,1)S(1)} %constant_dynamic-update-slice_fusion.refs_0_), channel_id=1, source_target_pairs={{0,32},{1,3},{2,34},{3,5},{4,36},{5,7},{6,38},{7,9},{8,40},{9,11},... | collective-permute-start | bytes 1572872 | tf_op jit(solution)/shard_map/ppermute | solution.py:55
  26.5 2.5 %collective-permute-start = (f32[1,512]{1,0:T(1,128)S(1)}, f32[1,512]{1,0:T(1,128)S(1)}, u32[]{:S(2)}, u32[]{:S(2)}) collective-permute-start(f32[1,512]{1,0:T(1,128)S(1)} %bitcast.16), channel_id=1, source_target_pairs={{0,1},{1,0},{2,3},{3,2},{4,5},{5,4},{6,7},{7,6},{8,9},{9,8},{10,11... | collective-permute-start | bytes 6152 | tf_op jit(solution)/shard_map/ppermute | solution.py:39
  28.4 32.3 %collective-permute-start.15 = (bf16[64,4096]{1,0:T(8,128)(2,1)S(1)}, bf16[64,4096]{1,0:T(8,128)(2,1)S(1)}, u32[]{:S(2)}, u32[]{:S(2)}) collective-permute-start(bf16[64,4096]{1,0:T(8,128)(2,1)S(1)} %constant_dynamic-update-slice_fusion.refs_0_), channel_id=1, source_target_pairs={{0,2},{1,17},{2,4},{3,19},{4,6},{5,21},{6,8},{7,23},{8,10},{9,25},... | collective-permute-start | bytes 1572872 | tf_op jit(solution)/shard_map/ppermute | solution.py:55
  29.0 31.8 %collective-permute-start.18 = (bf16[64,4096]{1,0:T(8,128)(2,1)S(1)}, bf16[64,4096]{1,0:T(8,128)(2,1)S(1)}, u32[]{:S(2)}, u32[]{:S(2)}) collective-permute-start(bf16[64,4096]{1,0:T(8,128)(2,1)S(1)} %constant_dynamic-update-slice_fusion.refs_0_), channel_id=1, source_target_pairs={{0,14},{1,145},{2,0},{3,147},{4,2},{5,149},{6,4},{7,151},{8,6},{9,... | collective-permute-start | bytes 1572872 | tf_op jit(solution)/shard_map/ppermute | solution.py:55
  31.1 2.2 %copy-start = (bf16[512,4096]{1,0:T(8,128)(2,1)S(1)}, bf16[512,4096]{1,0:T(8,128)(2,1)}, u32[]{:S(2)}) copy-start(bf16[512,4096]{1,0:T(8,128)(2,1)} %particles_ref.1) | copy-start | bytes 12582916
  33.3 23.0 %copy-start.7 = (s32[256]{0:T(256)S(1)}, s32[256]{0:T(256)}, u32[]{:S(2)}) copy-start(s32[256]{0:T(256)} %constant.425.clone) | copy-start | bytes 3076
  33.3 23.0 %copy-start.8 = (s32[256]{0:T(256)S(1)}, s32[256]{0:T(256)}, u32[]{:S(2)}) copy-start(s32[256]{0:T(256)} %constant.426.clone) | copy-start | bytes 3076
  38.1 22.5 %copy-start.5 = (s32[192]{0:T(256)S(1)}, s32[192]{0:T(256)}, u32[]{:S(2)}) copy-start(s32[192]{0:T(256)} %constant.427.clone) | copy-start | bytes 2308
  38.2 22.4 %copy-start.6 = (s32[192]{0:T(256)S(1)}, s32[192]{0:T(256)}, u32[]{:S(2)}) copy-start(s32[192]{0:T(256)} %constant.428.clone) | copy-start | bytes 2308
  38.2 25.3 %copy-start.3 = (s32[192]{0:T(256)S(1)}, s32[192]{0:T(256)}, u32[]{:S(2)}) copy-start(s32[192]{0:T(256)} %constant.429.clone) | copy-start | bytes 2308
  38.2 25.2 %copy-start.4 = (s32[192]{0:T(256)S(1)}, s32[192]{0:T(256)}, u32[]{:S(2)}) copy-start(s32[192]{0:T(256)} %constant.430.clone) | copy-start | bytes 2308
  38.2 27.6 %copy-start.1 = (bf16[512,4096]{1,0:T(8,128)(2,1)S(1)}, bf16[512,4096]{1,0:T(8,128)(2,1)}, u32[]{:S(2)}) copy-start(bf16[512,4096]{1,0:T(8,128)(2,1)} %particles_ref.1) | copy-start | bytes 12582916
  38.3 7.6 %collective-permute-start.10 = (bf16[32,4096]{1,0:T(8,128)(2,1)S(1)}, bf16[32,4096]{1,0:T(8,128)(2,1)S(1)}, u32[]{:S(2)}, u32[]{:S(2)}) collective-permute-start(bf16[32,4096]{1,0:T(8,128)(2,1)S(1)} %slice.6), channel_id=1, source_target_pairs={{0,96},{1,15},{2,98},{3,1},{4,100},{5,3},{6,102},{7,5},{8,104},{9,... | collective-permute-start | bytes 786440 | tf_op jit(solution)/shard_map/ppermute | solution.py:55
  42.7 26.4 %collective-permute-start.17 = (bf16[128,4096]{1,0:T(8,128)(2,1)S(1)}, bf16[128,4096]{1,0:T(8,128)(2,1)S(1)}, u32[]{:S(2)}, u32[]{:S(2)}) collective-permute-start(bf16[128,4096]{1,0:T(8,128)(2,1)S(1)} %constant_dynamic-update-slice_fusion.5.refs_0_), channel_id=1, source_target_pairs={{0,2},{1,17},{2,4},{3,19},{4,6},{5,21},{6,8},{7,23},{8,10},{9,25},... | collective-permute-start | bytes 3145736 | tf_op jit(solution)/shard_map/ppermute | solution.py:55
  42.8 14.4 %collective-permute-start.8 = (bf16[128,4096]{1,0:T(8,128)(2,1)S(1)}, bf16[128,4096]{1,0:T(8,128)(2,1)S(1)}, u32[]{:S(2)}, u32[]{:S(2)}) collective-permute-start(bf16[128,4096]{1,0:T(8,128)(2,1)S(1)} %constant_dynamic-update-slice_fusion.5.refs_0_), channel_id=1, source_target_pairs={{0,14},{1,145},{2,0},{3,147},{4,2},{5,149},{6,4},{7,151},{8,6},{9,... | collective-permute-start | bytes 3145736 | tf_op jit(solution)/shard_map/ppermute | solution.py:55
  45.9 10.0 %collective-permute-start.11 = (bf16[32,4096]{1,0:T(8,128)(2,1)S(1)}, bf16[32,4096]{1,0:T(8,128)(2,1)S(1)}, u32[]{:S(2)}, u32[]{:S(2)}) collective-permute-start(bf16[32,4096]{1,0:T(8,128)(2,1)S(1)} %slice.7), channel_id=1, source_target_pairs={{0,32},{1,3},{2,34},{3,5},{4,36},{5,7},{6,38},{7,9},{8,40},{9,11},... | collective-permute-start | bytes 786440 | tf_op jit(solution)/shard_map/ppermute | solution.py:55
  56.0 9.8 %collective-permute-start.12 = (bf16[64,4096]{1,0:T(8,128)(2,1)S(1)}, bf16[64,4096]{1,0:T(8,128)(2,1)S(1)}, u32[]{:S(2)}, u32[]{:S(2)}) collective-permute-start(bf16[64,4096]{1,0:T(8,128)(2,1)S(1)} %constant_dynamic-update-slice_fusion.7.refs_1_), channel_id=1, source_target_pairs={{0,2},{1,17},{2,4},{3,19},{4,6},{5,21},{6,8},{7,23},{8,10},{9,25},... | collective-permute-start | bytes 1572872 | tf_op jit(solution)/shard_map/ppermute | solution.py:55
  57.2 23.9 %collective-permute-start.9 = (bf16[128,4096]{1,0:T(8,128)(2,1)S(1)}, bf16[128,4096]{1,0:T(8,128)(2,1)S(1)}, u32[]{:S(2)}, u32[]{:S(2)}) collective-permute-start(bf16[128,4096]{1,0:T(8,128)(2,1)S(1)} %collective-permute-done.8.refs_0_), channel_id=1, source_target_pairs={{0,14},{1,145},{2,0},{3,147},{4,2},{5,149},{6,4},{7,151},{8,6},{9,... | collective-permute-start | bytes 3145736 | tf_op jit(solution)/shard_map/ppermute | solution.py:55
  60.7 11.1 %collective-permute-start.16 = (bf16[64,4096]{1,0:T(8,128)(2,1)S(1)}, bf16[64,4096]{1,0:T(8,128)(2,1)S(1)}, u32[]{:S(2)}, u32[]{:S(2)}) collective-permute-start(bf16[64,4096]{1,0:T(8,128)(2,1)S(1)} %collective-permute-done.15.refs_3_), channel_id=1, source_target_pairs={{0,2},{1,17},{2,4},{3,19},{4,6},{5,21},{6,8},{7,23},{8,10},{9,25},... | collective-permute-start | bytes 1572872 | tf_op jit(solution)/shard_map/ppermute | solution.py:55
  60.8 17.2 %collective-permute-start.14 = (bf16[64,4096]{1,0:T(8,128)(2,1)S(1)}, bf16[64,4096]{1,0:T(8,128)(2,1)S(1)}, u32[]{:S(2)}, u32[]{:S(2)}) collective-permute-start(bf16[64,4096]{1,0:T(8,128)(2,1)S(1)} %constant_dynamic-update-slice_fusion.7.refs_1_), channel_id=1, source_target_pairs={{0,14},{1,145},{2,0},{3,147},{4,2},{5,149},{6,4},{7,151},{8,6},{9,... | collective-permute-start | bytes 1572872 | tf_op jit(solution)/shard_map/ppermute | solution.py:55
  65.8 15.2 %collective-permute-start.13 = (bf16[64,4096]{1,0:T(8,128)(2,1)S(1)}, bf16[64,4096]{1,0:T(8,128)(2,1)S(1)}, u32[]{:S(2)}, u32[]{:S(2)}) collective-permute-start(bf16[64,4096]{1,0:T(8,128)(2,1)S(1)} %collective-permute-done.12.refs_1_), channel_id=1, source_target_pairs={{0,2},{1,17},{2,4},{3,19},{4,6},{5,21},{6,8},{7,23},{8,10},{9,25},... | collective-permute-start | bytes 1572872 | tf_op jit(solution)/shard_map/ppermute | solution.py:55
  81.1 7.0 %copy-start.2 = (f32[512]{0:T(512)S(1)}, f32[512]{0:T(512)}, u32[]{:S(2)}) copy-start(f32[512]{0:T(512)} %param.21) | copy-start | bytes 6148
  84.2 3.9 %collective-permute-start.19 = (f32[8,512]{1,0:T(8,128)S(1)}, f32[8,512]{1,0:T(8,128)S(1)}, u32[]{:S(2)}, u32[]{:S(2)}) collective-permute-start(f32[8,512]{1,0:T(8,128)S(1)} %get-tuple-element.34), channel_id=1, source_target_pairs={{0,1},{1,0},{2,3},{3,2},{4,5},{5,4},{6,7},{7,6},{8,9},{9,8},{10,11... | collective-permute-start | bytes 49160 | tf_op jit(solution)/shard_map/ppermute | solution.py:39

commit v5 on v4

--- a/solution.py
+++ b/solution.py
@@ -17,7 +17,7 @@
 ALL = ("xh", "y", "xl", "z", "core")
 AX, AY, AZ = 0, 1, 2
 SIZES = (XN, YN, ZN)
-STAGES = ((AX, AY), (AY, AZ), (AZ, AX))
+STAGES = ((AX, AZ), (AY, AY), (AZ, AX))
 
 
 def flat_device(x, y, z, core):
@@ -44,7 +44,8 @@
         self.rows, self.offsets = rows, offsets
 
     def part(self, start, stop):
-        return Piece(self.rows[start:stop], [o[start:stop] for o in self.offsets])
+        rows = None if self.rows is None else self.rows[start:stop]
+        return Piece(rows, [o[start:stop] for o in self.offsets])
 
     def fetch(self, axes, steps):
         def move(at, core):
@@ -52,22 +53,62 @@
             return at, core
 
         moved = [o + steps * np.eye(4, dtype=np.int32)[axis] for o, axis in zip(self.offsets, axes)]
-        return Piece(lax.ppermute(self.rows, ALL, pairs(move)), moved)
+        rows = None if self.rows is None else lax.ppermute(self.rows, ALL, pairs(move))
+        return Piece(rows, moved)
 
 
 def join(pieces):
-    return Piece(
-        jnp.concatenate([p.rows for p in pieces], axis=0),
-        [np.concatenate([p.offsets[c] for p in pieces], axis=0) for c in range(CORES)],
+    rows = None if pieces[0].rows is None else jnp.concatenate([p.rows for p in pieces], axis=0)
+    offsets = [np.concatenate([p.offsets[c] for p in pieces], axis=0) for c in range(CORES)]
+    return Piece(rows, offsets)
+
+
+def together(pieces):
+    if pieces[0].rows is not None:
+        for piece, rows in zip(pieces, lax.optimization_barrier([p.rows for p in pieces])):
+            piece.rows = rows
+
+
+def spread(piece):
+    piece = join([piece, piece.fetch((AZ, AZ), ZN // 2)])
+    return [piece] + [piece.fetch(STAGES[0], steps) for steps in (1, -1, 2)]
+
+
+def gather(near, first):
+    near, half = join(near), sum(len(p.offsets[0]) for p in near) // 2
+    last = STAGES[2]
+    ahead, behind = near.fetch(STAGES[1], 1), near.fetch(STAGES[1], -1)
+    next_, prev = [near.fetch(last, 1)], [near.fetch(last, -1)]
+    together([ahead, behind, next_[0], prev[0]])
+    far_a = ahead.part(0, half).fetch(STAGES[1], 1)
+    far_b = behind.part(half, 2 * half).fetch(STAGES[1], -1)
+    one = join([ahead, behind])
+    far_a, far_b = first([near, one], far_a, far_b)
+    chunks = [near, one, join([far_a, far_b])]
+    for chunk in chunks[1:]:
+        next_.append(chunk.fetch(last, 1))
+        prev.append(chunk.fetch(last, -1))
+    if near.rows is not None:
+        next_[1].rows, _ = lax.optimization_barrier((next_[1].rows, chunks[2].rows))
+        prev[0].rows, _ = lax.optimization_barrier((prev[0].rows, chunks[2].rows))
+    far = [prev[0].fetch(last, -1), next_[1].fetch(last, 1), prev[2].fetch(last, -1)]
+    return (
+        chunks[:2],
+        [chunks[2], next_[0], prev[0], next_[1], prev[1]],
+        [next_[2], prev[2], *far],
     )
 
 
-def row_ids(pieces, here, local):
+def row_ids(groups, here, local):
     packed = []
     for core in range(CORES):
-        d = np.concatenate([p.offsets[core] for p in pieces], axis=0)
-        x, y, z = d[:, 0] % XN, d[:, 1] % YN, d[:, 2] % ZN
-        packed.append((((x * YN + y) * ZN + z) * local + d[:, 3]).astype(np.int32))
+        parts = []
+        for group in groups:
+            d = np.concatenate([p.offsets[core] for p in group], axis=0)
+            x, y, z = d[:, 0] % XN, d[:, 1] % YN, d[:, 2] % ZN
+            rel = (((x * YN + y) * ZN + z) * local + d[:, 3]).astype(np.int32)
+            parts.append(np.pad(rel, (0, -len(rel) % LANES)))
+        packed.append(np.concatenate(parts))
     d = jnp.where(here[3] == 0, jnp.asarray(packed[0]), jnp.asarray(packed[1]))
     r, d = d % local, d // local
     z, d = (here[2] + d % ZN) % ZN, d // ZN
@@ -79,7 +120,7 @@
 BLOCK = 256
 
 
-def score_kernel(scale, n, first, ids_ref, wanted_ref, other_wanted_ref, own_ref, other_ref, *refs):
+def score_kernel(scale, n, first, at, ids_ref, wanted_ref, other_wanted_ref, own_ref, other_ref, *refs):
     pieces, refs = refs[:n], refs[n:]
     if first:
         before, (mine, theirs, kept, arrived) = None, refs
@@ -89,7 +130,8 @@
         before, (mine, theirs), kept = refs[:2], refs[2:], other_ref
     count = own_ref.shape[0]
     rows = sum(piece.shape[0] for piece in pieces)
-    column = jnp.broadcast_to(ids_ref[...], (LANES, rows)).T
+    whole = -(-rows // LANES) * LANES
+    column = jnp.broadcast_to(ids_ref[0:1, at : at + whole], (LANES, whole)).T[:rows]
     ids = jnp.concatenate([column] * (BLOCK // LANES), axis=1)
     held = jnp.concatenate([piece[...] for piece in pieces], axis=0)
     for side, (particles, wanted, after) in enumerate(
@@ -118,7 +160,7 @@
             after[2:3, cols] = chosen
 
 
-def score(pieces, ids, wanted, other_wanted, own, other, before, scale):
+def score(pieces, ids, at, wanted, other_wanted, own, other, before, scale):
     count, voxels = own.shape
     rows = sum(p.rows.shape[0] for p in pieces)
     first = before is None
@@ -130,7 +172,7 @@
         in_specs[4] = pl.BlockSpec(memory_space=pl.ANY)
         out_shape.append(jax.ShapeDtypeStruct(other.shape, other.dtype))
     return pl.pallas_call(
-        functools.partial(score_kernel, scale, len(pieces), first),
+        functools.partial(score_kernel, scale, len(pieces), first, at),
         out_shape=out_shape,
         in_specs=in_specs,
         out_specs=[whole] * len(out_shape),
@@ -196,41 +238,36 @@
 
     other = swap_cores(particles)
     wanted = (class_ids * orients + orient_ids).astype(jnp.float32)[None, :]
+    key = (class_ids + classes * (offsets + SHIFT))[None, :]
     other_wanted = swap_cores(wanted)
 
     start = np.zeros((local, 4), np.int32)
     start[:, 3] = np.arange(local)
-    piece = Piece(references.reshape(local, voxels), [start, start])
-    piece = join([piece, piece.fetch((AZ, AZ), ZN // 2)])
-    first = STAGES[0]
-    piece = join([piece, piece.fetch(first, 1), piece.fetch(first, -1), piece.fetch(first, 2)])
-
-    def take(group, kept, stats):
-        ids = row_ids(group, here, local)
-        out = score(group, ids, wanted, other_wanted, particles, kept, stats, scale)
-        return (out[2] if stats is None else kept), out[:2]
-
-    near, half = piece, piece.rows.shape[0] // 2
-    ahead, behind = near.fetch(STAGES[1], 1), near.fetch(STAGES[1], -1)
-    kept, stats = take([near], other, None)
-    ahead.rows, behind.rows, stats = lax.optimization_barrier((ahead.rows, behind.rows, stats))
-    far_a = ahead.part(0, half).fetch(STAGES[1], 1)
-    far_b = behind.part(half, 2 * half).fetch(STAGES[1], -1)
-    last = STAGES[2]
-    chunks = [near, join([ahead, behind]), join([far_a, far_b])]
-    next_, prev = [c.fetch(last, 1) for c in chunks], [c.fetch(last, -1) for c in chunks]
-    far = [prev[0].fetch(last, -1), next_[1].fetch(last, 1), prev[2].fetch(last, -1)]
-    for group in (
-        chunks[1:] + [next_[0], prev[0]],
-        [next_[1], prev[1]],
-        [next_[2], prev[2], far[0]],
-        far[1:],
-    ):
-        kept, stats = take(group, kept, stats)
+    dry = gather(spread(Piece(None, [start, start])), lambda group, *halves: halves)
+    ids = row_ids(dry, here, local)
+    near = spread(Piece(references.reshape(local, voxels), [start, start]))
+    rows, ids, wanted, key = lax.optimization_barrier((near[-1].rows, ids, wanted, key))
+    near[-1].rows = rows
+    kept, stats, at = other, None, 0
+
+    def take(group):
+        nonlocal kept, stats, at
+        out = score(group, ids, at, wanted, other_wanted, particles, kept, stats, scale)
+        kept, stats = (out[2] if stats is None else kept), out[:2]
+        count_rows = sum(len(p.offsets[0]) for p in group)
+        at += -(-count_rows // LANES) * LANES
+
+    def first(group, far_a, far_b):
+        nonlocal stats
+        take(group)
+        far_a.rows, far_b.rows, stats = lax.optimization_barrier((far_a.rows, far_b.rows, stats))
+        return far_a, far_b
+
+    for group in gather(near, first)[1:]:
+        take(group)
     mine, theirs = stats
     got = swap_cores(theirs)
-    key = class_ids + classes * (offsets + SHIFT)
-    partial_sums = class_sums(key[None, :], weights[None, :], mine, got, particles, classes, orients)
+    partial_sums = class_sums(key, weights[None, :], mine, got, particles, classes, orients)
     sent = partial_sums.reshape(devices, classes * voxels // devices)
     owned = jnp.sum(lax.all_to_all(sent, ALL, 0, 0, tiled=True), axis=0, keepdims=True)
     population = count * devices / classes

time: 113 us -> 107 us (0.947)
  waiting for transfers between devices: 27.6 us -> 31.2 us
  Pallas kernels: 17.9 us -> 14.5 us
  local copies, waits for them, and re-layouts: 3.3 us -> 1.04 us
  blocking collectives: 22.5 us -> 20.7 us
    ppermute x17, waiting for transfers between devices: 26.7 us -> 30.3 us  [fetch(): lax.ppermute(self.rows, ALL, pairs(move))]
    pallas_call x5 -> x3, Pallas kernels: 16.9 us -> 13.5 us  [score(): pl.pallas_call(functools.partial(score_kernel, scale, len(pieces), first,...]
    unnamed x24 -> x10, local copies, waits for them, and re-layouts: 3.19 us -> 0.93 us
    ppermute x17, starting transfers between devices: 30.1 us -> 28.2 us  [fetch(): lax.ppermute(self.rows, ALL, pairs(move))]
    all_to_all x1, blocking collectives: 22.5 us -> 20.7 us  [body(): lax.all_to_all(sent, ALL, 0, 0, tiled=True)]
  transfers between devices with their start and end apart: 20 -> 20, of which waited for: 9 -> 8; matrix products, arithmetic and copies ran while one was open for 4% -> 3% of each run, Pallas kernels for 12% -> 9%
where the time goes in v5:
time: 107 us
  starting transfers between devices  35.7 us (33%)
  waiting for transfers between devices  31.2 us (29%)
  blocking collectives  20.7 us (19%)
  Pallas kernels  14.5 us (14%)
  other arithmetic  3.5 us (3%)
    ppermute x17, waiting for transfers between devices, fetch(): lax.ppermute(self.rows, ALL, pairs(move))  30.3 us
    ppermute x17, starting transfers between devices, fetch(): lax.ppermute(self.rows, ALL, pairs(move))  28.2 us
    all_to_all x1, blocking collectives, body(): lax.all_to_all(sent, ALL, 0, 0, tiled=True)  20.7 us
    pallas_call x3, Pallas kernels, score(): pl.pallas_call(functools.partial(score_kernel, scale, len(pieces), first,...  13.5 us
    ppermute x3, starting transfers between devices, swap_cores(): return lax.ppermute(value, ALL, pairs(lambda at, core: (at, 1 - core)))  7.41 us
  transfers between devices with their start and end apart: 20, of which 8 were waited for; matrix products, arithmetic and copies ran while one was open for 3% of the time, Pallas kernels for 9%

profile of v5, /device:TPU:1, one launch (start us, length us, event | category | flops | bytes accessed | tf_op | source)
XLA Modules:
  0.0 106.7 jit_solution(10092629999402103054)
XLA Ops:
  0.0 7.7 %collective-permute-start = (bf16[8,4096]{1,0:T(8,128)(2,1)}, bf16[8,4096]{1,0:T(8,128)(2,1)S(1)}, u32[]{:S(2)}, u32[]{:S(2)}) collective-permute-start(bf16[8,4096]{1,0:T(8,128)(2,1)} %bitcast.17), channel_id=1, source_target_pairs={{0,8},{1,9},{2,10},{3,11},{4,12},{5,13},{6,14},{7,15},{8,0},{9,1},... | collective-permute-start | bytes 196616 | tf_op jit(solution)/shard_map/ppermute | solution.py:56
  7.7 1.0 collective-permute-start.3
  8.7 0.8 constant_dynamic-update-slice_fusion.4
  9.5 0.9 fusion.12
  10.5 0.9 multiply_add_fusion
  11.4 0.0 collective-permute-done
  11.4 0.9 pad_maximum_fusion
  12.2 2.8 %collective-permute-start.1 = (bf16[16,4096]{1,0:T(8,128)(2,1)S(1)}, bf16[16,4096]{1,0:T(8,128)(2,1)S(1)}, u32[]{:S(2)}, u32[]{:S(2)}) collective-permute-start(bf16[16,4096]{1,0:T(8,128)(2,1)S(1)} %pad_maximum_fusion), channel_id=1, source_target_pairs={{0,128},{1,13},{2,130},{3,15},{4,132},{5,1},{6,134},{7,3},{8,136},... | collective-permute-start | bytes 393224 | tf_op jit(solution)/shard_map/ppermute | solution.py:56
  15.0 0.7 collective-permute-start.4
  15.7 0.7 collective-permute-start.5
  16.5 4.6 %collective-permute-done.4 = bf16[16,4096]{1,0:T(8,128)(2,1)S(1)} collective-permute-done((bf16[16,4096]{1,0:T(8,128)(2,1)S(1)}, bf16[16,4096]{1,0:T(8,128)(2,1)S(1)}, u32[]{:S(2)}, u32[]{:S(2)}) %collective-permute-start.4) | collective-permute-done | bytes 131104 | tf_op jit(solution)/shard_map/ppermute | solution.py:56
  21.1 0.0 collective-permute-done.5
  21.2 2.8 %collective-permute-start.6 = (bf16[64,4096]{1,0:T(8,128)(2,1)S(1)}, bf16[64,4096]{1,0:T(8,128)(2,1)S(1)}, u32[]{:S(2)}, u32[]{:S(2)}) collective-permute-start(bf16[64,4096]{1,0:T(8,128)(2,1)S(1)} %constant_dynamic-update-slice_fusion.refs_0_), channel_id=1, source_target_pairs={{0,96},{1,97},{2,98},{3,99},{4,100},{5,101},{6,102},{7,103},{8,104... | collective-permute-start | bytes 1572872 | tf_op jit(solution)/shard_map/ppermute | solution.py:56
  24.0 0.0 collective-permute-start.7
  24.0 2.2 %collective-permute-start.8 = (bf16[64,4096]{1,0:T(8,128)(2,1)S(1)}, bf16[64,4096]{1,0:T(8,128)(2,1)S(1)}, u32[]{:S(2)}, u32[]{:S(2)}) collective-permute-start(bf16[64,4096]{1,0:T(8,128)(2,1)S(1)} %constant_dynamic-update-slice_fusion.refs_0_), channel_id=1, source_target_pairs={{0,14},{1,145},{2,0},{3,147},{4,2},{5,149},{6,4},{7,151},{8,6},{9,... | collective-permute-start | bytes 1572872 | tf_op jit(solution)/shard_map/ppermute | solution.py:56
  26.2 0.0 collective-permute-start.9
  26.2 7.5 %collective-permute-done.6 = bf16[64,4096]{1,0:T(8,128)(2,1)S(1)} collective-permute-done((bf16[64,4096]{1,0:T(8,128)(2,1)S(1)}, bf16[64,4096]{1,0:T(8,128)(2,1)S(1)}, u32[]{:S(2)}, u32[]{:S(2)}) %collective-permute-start.6) | collective-permute-done | bytes 524320 | tf_op jit(solution)/shard_map/ppermute | solution.py:56
  33.7 2.5 %collective-permute-start.2 = (f32[1,512]{1,0:T(1,128)S(1)}, f32[1,512]{1,0:T(1,128)S(1)}, u32[]{:S(2)}, u32[]{:S(2)}) collective-permute-start(f32[1,512]{1,0:T(1,128)S(1)} %bitcast.12), channel_id=1, source_target_pairs={{0,1},{1,0},{2,3},{3,2},{4,5},{5,4},{6,7},{7,6},{8,9},{9,8},{10,11... | collective-permute-start | bytes 6152 | tf_op jit(solution)/shard_map/ppermute | solution.py:39
  36.1 0.6 collective-permute-done.7
  36.8 0.0 collective-permute-done.8.refs_1_
  36.8 0.0 collective-permute-done.9.refs_2_
  36.8 2.9 %collective-permute-start.10 = (bf16[32,4096]{1,0:T(8,128)(2,1)S(1)}, bf16[32,4096]{1,0:T(8,128)(2,1)S(1)}, u32[]{:S(2)}, u32[]{:S(2)}) collective-permute-start(bf16[32,4096]{1,0:T(8,128)(2,1)S(1)} %slice.6), channel_id=1, source_target_pairs={{0,96},{1,97},{2,98},{3,99},{4,100},{5,101},{6,102},{7,103},{8,104... | collective-permute-start | bytes 786440 | tf_op jit(solution)/shard_map/ppermute | solution.py:56
  39.7 0.1 collective-permute-start.11
  39.9 3.1 %collective-permute-start.15 = (bf16[128,4096]{1,0:T(8,128)(2,1)S(1)}, bf16[128,4096]{1,0:T(8,128)(2,1)S(1)}, u32[]{:S(2)}, u32[]{:S(2)}) collective-permute-start(bf16[128,4096]{1,0:T(8,128)(2,1)S(1)} %constant_dynamic-update-slice_fusion.5.refs_1_), channel_id=1, source_target_pairs={{0,14},{1,145},{2,0},{3,147},{4,2},{5,149},{6,4},{7,151},{8,6},{9,... | collective-permute-start | bytes 3145736 | tf_op jit(solution)/shard_map/ppermute | solution.py:56
  43.0 0.0 collective-permute-done.2.other_wanted_ref
  43.0 0.0 collective-permute-start.18
  43.0 0.0 collective-permute-done.3.other_ref
  43.0 5.2 %score.3 = (f32[8,512]{1,0:T(8,128)S(1)}, f32[8,512]{1,0:T(8,128)S(1)}, bf16[512,4096]{1,0:T(8,128)(2,1)S(1)}) custom-call(f32[1,1152]{1,0:T(1,128)S(1)} %broadcast_in_dim.13.ids_ref, f32[1,512]{1,0:T(1,128)S(1)} %bitcast.13, f32[1,512]{1,0:T(1,128)S(1)} %collective-permute-done.2.other_wanted_ref, bf16[512,4096]{1,0:T(8,128)(2,1)S(1)} %copy-done, ...), custom_call_target="tpu_custom_call" | custom-call | flops 1610612736 | bytes 1572864 | tf_op jit(solution)/shard_map/score/pallas_call | solution.py:174
  48.2 0.0 collective-permute-done.10
  48.3 0.3 collective-permute-start.13
  48.6 6.1 %collective-permute-done.15.refs_3_ = bf16[128,4096]{1,0:T(8,128)(2,1)S(1)} collective-permute-done((bf16[128,4096]{1,0:T(8,128)(2,1)S(1)}, bf16[128,4096]{1,0:T(8,128)(2,1)S(1)}, u32[]{:S(2)}, u32[]{:S(2)}) %collective-permute-start.15) | collective-permute-done | bytes 1048608 | tf_op jit(solution)/shard_map/ppermute | solution.py:56
  54.7 3.4 %collective-permute-start.16 = (bf16[128,4096]{1,0:T(8,128)(2,1)S(1)}, bf16[128,4096]{1,0:T(8,128)(2,1)S(1)}, u32[]{:S(2)}, u32[]{:S(2)}) collective-permute-start(bf16[128,4096]{1,0:T(8,128)(2,1)S(1)} %collective-permute-done.15.refs_3_), channel_id=1, source_target_pairs={{0,14},{1,145},{2,0},{3,147},{4,2},{5,149},{6,4},{7,151},{8,6},{9,... | collective-permute-start | bytes 3145736 | tf_op jit(solution)/shard_map/ppermute | solution.py:56
  58.2 0.0 collective-permute-start.12
  58.2 1.4 %collective-permute-start.14 = (bf16[64,4096]{1,0:T(8,128)(2,1)S(1)}, bf16[64,4096]{1,0:T(8,128)(2,1)S(1)}, u32[]{:S(2)}, u32[]{:S(2)}) collective-permute-start(bf16[64,4096]{1,0:T(8,128)(2,1)S(1)} %collective-permute-done.9.refs_2_), channel_id=1, source_target_pairs={{0,2},{1,17},{2,4},{3,19},{4,6},{5,21},{6,8},{7,23},{8,10},{9,25},... | collective-permute-start | bytes 1572872 | tf_op jit(solution)/shard_map/ppermute | solution.py:56
  59.6 4.2 %collective-permute-done.13.refs_1_ = bf16[64,4096]{1,0:T(8,128)(2,1)S(1)} collective-permute-done((bf16[64,4096]{1,0:T(8,128)(2,1)S(1)}, bf16[64,4096]{1,0:T(8,128)(2,1)S(1)}, u32[]{:S(2)}, u32[]{:S(2)}) %collective-permute-start.13) | collective-permute-done | bytes 524320 | tf_op jit(solution)/shard_map/ppermute | solution.py:56
  63.8 0.0 collective-permute-start.17
  63.8 4.5 %score.4 = (f32[8,512]{1,0:T(8,128)S(1)}, f32[8,512]{1,0:T(8,128)S(1)}) custom-call(f32[1,1152]{1,0:T(1,128)S(1)} %broadcast_in_dim.13.ids_ref, f32[1,512]{1,0:T(1,128)S(1)} %bitcast.14, f32[1,512]{1,0:T(1,128)S(1)} %collective-permute-done.2.other_wanted_ref, bf16[512,4096]{1,0:T(8,128)(2,1)S(1)} %copy-done, ...), custom_call_target="tpu_custom_call" | custom-call | flops 3758096384 | bytes 3670016 | tf_op jit(solution)/shard_map/score/pallas_call | solution.py:174
  68.3 1.1 %collective-permute-done.14.refs_2_ = bf16[64,4096]{1,0:T(8,128)(2,1)S(1)} collective-permute-done((bf16[64,4096]{1,0:T(8,128)(2,1)S(1)}, bf16[64,4096]{1,0:T(8,128)(2,1)S(1)}, u32[]{:S(2)}, u32[]{:S(2)}) %collective-permute-start.14) | collective-permute-done | bytes 524320 | tf_op jit(solution)/shard_map/ppermute | solution.py:56
  69.4 6.1 %collective-permute-done.12.refs_0_ = bf16[64,4096]{1,0:T(8,128)(2,1)S(1)} collective-permute-done((bf16[64,4096]{1,0:T(8,128)(2,1)S(1)}, bf16[64,4096]{1,0:T(8,128)(2,1)S(1)}, u32[]{:S(2)}, u32[]{:S(2)}) %collective-permute-start.12) | collective-permute-done | bytes 524320 | tf_op jit(solution)/shard_map/ppermute | solution.py:56
  75.5 0.0 collective-permute-done.17.refs_4_
  75.5 0.0 collective-permute-done.16.refs_3_
  75.5 3.9 %score.5 = (f32[8,512]{1,0:T(8,128)S(1)}, f32[8,512]{1,0:T(8,128)S(1)}) custom-call(f32[1,1152]{1,0:T(1,128)S(1)} %broadcast_in_dim.13.ids_ref, f32[1,512]{1,0:T(1,128)S(1)} %bitcast.15, f32[1,512]{1,0:T(1,128)S(1)} %collective-permute-done.2.other_wanted_ref, bf16[512,4096]{1,0:T(8,128)(2,1)S(1)} %copy-done, ...), custom_call_target="tpu_custom_call" | custom-call | flops 3221225472 | bytes 3145728 | tf_op jit(solution)/shard_map/score/pallas_call | solution.py:174
  79.4 4.0 %collective-permute-start.19 = (f32[8,512]{1,0:T(8,128)S(1)}, f32[8,512]{1,0:T(8,128)S(1)}, u32[]{:S(2)}, u32[]{:S(2)}) collective-permute-start(f32[8,512]{1,0:T(8,128)S(1)} %get-tuple-element.46), channel_id=1, source_target_pairs={{0,1},{1,0},{2,3},{3,2},{4,5},{5,4},{6,7},{7,6},{8,9},{9,8},{10,11... | collective-permute-start | bytes 49160 | tf_op jit(solution)/shard_map/ppermute | solution.py:39
  83.4 0.8 collective-permute-done.19.got_ref
  84.2 1.0 class_sums.1
  85.2 20.7 %all_to_all.9 = f32[256,1,128]{2,1,0:T(1,128)S(1)} all-to-all(f32[256,1,128]{2,1,0:T(1,128)S(1)} %bitcast.10), channel_id=1, replica_groups=mesh['xh'=2,'y'=4,'xl'=2,'z'=8,'core'=2] {'xh','y','xl','z','core'}, dimensions={0} | all-to-all | bytes 262144 | tf_op jit(solution)/shard_map/all_to_all | solution.py:272
  105.9 0.3 reduce_sum.9
  106.2 0.5 multiply_bitcast_fusion
  (18 shorter events, 0.2 us)
Async XLA Ops:
  0.0 11.4 %collective-permute-start = (bf16[8,4096]{1,0:T(8,128)(2,1)}, bf16[8,4096]{1,0:T(8,128)(2,1)S(1)}, u32[]{:S(2)}, u32[]{:S(2)}) collective-permute-start(bf16[8,4096]{1,0:T(8,128)(2,1)} %bitcast.17), channel_id=1, source_target_pairs={{0,8},{1,9},{2,10},{3,11},{4,12},{5,13},{6,14},{7,15},{8,0},{9,1},... | collective-permute-start | bytes 196616 | tf_op jit(solution)/shard_map/ppermute | solution.py:56
  7.7 35.3 %collective-permute-start.3 = (bf16[512,4096]{1,0:T(8,128)(2,1)}, bf16[512,4096]{1,0:T(8,128)(2,1)}, u32[]{:S(2)}, u32[]{:S(2)}) collective-permute-start(bf16[512,4096]{1,0:T(8,128)(2,1)} %particles_ref.1), channel_id=1, source_target_pairs={{0,1},{1,0},{2,3},{3,2},{4,5},{5,4},{6,7},{7,6},{8,9},{9,8},{10,11... | collective-permute-start | bytes 12582920 | tf_op jit(solution)/shard_map/ppermute | solution.py:39
  9.5 33.5 %copy-start = (bf16[512,4096]{1,0:T(8,128)(2,1)S(1)}, bf16[512,4096]{1,0:T(8,128)(2,1)}, u32[]{:S(2)}) copy-start(bf16[512,4096]{1,0:T(8,128)(2,1)} %particles_ref.1) | copy-start | bytes 12582916
  12.2 8.9 %collective-permute-start.1 = (bf16[16,4096]{1,0:T(8,128)(2,1)S(1)}, bf16[16,4096]{1,0:T(8,128)(2,1)S(1)}, u32[]{:S(2)}, u32[]{:S(2)}) collective-permute-start(bf16[16,4096]{1,0:T(8,128)(2,1)S(1)} %pad_maximum_fusion), channel_id=1, source_target_pairs={{0,128},{1,13},{2,130},{3,15},{4,132},{5,1},{6,134},{7,3},{8,136},... | collective-permute-start | bytes 393224 | tf_op jit(solution)/shard_map/ppermute | solution.py:56
  15.0 6.1 %collective-permute-start.4 = (bf16[16,4096]{1,0:T(8,128)(2,1)S(1)}, bf16[16,4096]{1,0:T(8,128)(2,1)S(1)}, u32[]{:S(2)}, u32[]{:S(2)}) collective-permute-start(bf16[16,4096]{1,0:T(8,128)(2,1)S(1)} %pad_maximum_fusion), channel_id=1, source_target_pairs={{0,144},{1,15},{2,146},{3,1},{4,148},{5,3},{6,150},{7,5},{8,152},{... | collective-permute-start | bytes 393224 | tf_op jit(solution)/shard_map/ppermute | solution.py:56
  15.7 5.4 %collective-permute-start.5 = (bf16[16,4096]{1,0:T(8,128)(2,1)S(1)}, bf16[16,4096]{1,0:T(8,128)(2,1)S(1)}, u32[]{:S(2)}, u32[]{:S(2)}) collective-permute-start(bf16[16,4096]{1,0:T(8,128)(2,1)S(1)} %pad_maximum_fusion), channel_id=1, source_target_pairs={{0,16},{1,3},{2,18},{3,5},{4,20},{5,7},{6,22},{7,9},{8,24},{9,11},... | collective-permute-start | bytes 393224 | tf_op jit(solution)/shard_map/ppermute | solution.py:56
  21.2 12.5 %collective-permute-start.6 = (bf16[64,4096]{1,0:T(8,128)(2,1)S(1)}, bf16[64,4096]{1,0:T(8,128)(2,1)S(1)}, u32[]{:S(2)}, u32[]{:S(2)}) collective-permute-start(bf16[64,4096]{1,0:T(8,128)(2,1)S(1)} %constant_dynamic-update-slice_fusion.refs_0_), channel_id=1, source_target_pairs={{0,96},{1,97},{2,98},{3,99},{4,100},{5,101},{6,102},{7,103},{8,104... | collective-permute-start | bytes 1572872 | tf_op jit(solution)/shard_map/ppermute | solution.py:56
  24.0 12.8 %collective-permute-start.7 = (bf16[64,4096]{1,0:T(8,128)(2,1)S(1)}, bf16[64,4096]{1,0:T(8,128)(2,1)S(1)}, u32[]{:S(2)}, u32[]{:S(2)}) collective-permute-start(bf16[64,4096]{1,0:T(8,128)(2,1)S(1)} %constant_dynamic-update-slice_fusion.refs_0_), channel_id=1, source_target_pairs={{0,32},{1,33},{2,34},{3,35},{4,36},{5,37},{6,38},{7,39},{8,40},{9,... | collective-permute-start | bytes 1572872 | tf_op jit(solution)/shard_map/ppermute | solution.py:56
  24.0 12.8 %collective-permute-start.8 = (bf16[64,4096]{1,0:T(8,128)(2,1)S(1)}, bf16[64,4096]{1,0:T(8,128)(2,1)S(1)}, u32[]{:S(2)}, u32[]{:S(2)}) collective-permute-start(bf16[64,4096]{1,0:T(8,128)(2,1)S(1)} %constant_dynamic-update-slice_fusion.refs_0_), channel_id=1, source_target_pairs={{0,14},{1,145},{2,0},{3,147},{4,2},{5,149},{6,4},{7,151},{8,6},{9,... | collective-permute-start | bytes 1572872 | tf_op jit(solution)/shard_map/ppermute | solution.py:56
  26.2 10.6 %collective-permute-start.9 = (bf16[64,4096]{1,0:T(8,128)(2,1)S(1)}, bf16[64,4096]{1,0:T(8,128)(2,1)S(1)}, u32[]{:S(2)}, u32[]{:S(2)}) collective-permute-start(bf16[64,4096]{1,0:T(8,128)(2,1)S(1)} %constant_dynamic-update-slice_fusion.refs_0_), channel_id=1, source_target_pairs={{0,2},{1,17},{2,4},{3,19},{4,6},{5,21},{6,8},{7,23},{8,10},{9,25},... | collective-permute-start | bytes 1572872 | tf_op jit(solution)/shard_map/ppermute | solution.py:56
  33.7 9.4 %collective-permute-start.2 = (f32[1,512]{1,0:T(1,128)S(1)}, f32[1,512]{1,0:T(1,128)S(1)}, u32[]{:S(2)}, u32[]{:S(2)}) collective-permute-start(f32[1,512]{1,0:T(1,128)S(1)} %bitcast.12), channel_id=1, source_target_pairs={{0,1},{1,0},{2,3},{3,2},{4,5},{5,4},{6,7},{7,6},{8,9},{9,8},{10,11... | collective-permute-start | bytes 6152 | tf_op jit(solution)/shard_map/ppermute | solution.py:39
  36.8 11.4 %collective-permute-start.10 = (bf16[32,4096]{1,0:T(8,128)(2,1)S(1)}, bf16[32,4096]{1,0:T(8,128)(2,1)S(1)}, u32[]{:S(2)}, u32[]{:S(2)}) collective-permute-start(bf16[32,4096]{1,0:T(8,128)(2,1)S(1)} %slice.6), channel_id=1, source_target_pairs={{0,96},{1,97},{2,98},{3,99},{4,100},{5,101},{6,102},{7,103},{8,104... | collective-permute-start | bytes 786440 | tf_op jit(solution)/shard_map/ppermute | solution.py:56
  39.7 8.5 %collective-permute-start.11 = (bf16[32,4096]{1,0:T(8,128)(2,1)S(1)}, bf16[32,4096]{1,0:T(8,128)(2,1)S(1)}, u32[]{:S(2)}, u32[]{:S(2)}) collective-permute-start(bf16[32,4096]{1,0:T(8,128)(2,1)S(1)} %slice.7), channel_id=1, source_target_pairs={{0,32},{1,33},{2,34},{3,35},{4,36},{5,37},{6,38},{7,39},{8,40},{9,... | collective-permute-start | bytes 786440 | tf_op jit(solution)/shard_map/ppermute | solution.py:56
  39.9 14.9 %collective-permute-start.15 = (bf16[128,4096]{1,0:T(8,128)(2,1)S(1)}, bf16[128,4096]{1,0:T(8,128)(2,1)S(1)}, u32[]{:S(2)}, u32[]{:S(2)}) collective-permute-start(bf16[128,4096]{1,0:T(8,128)(2,1)S(1)} %constant_dynamic-update-slice_fusion.5.refs_1_), channel_id=1, source_target_pairs={{0,14},{1,145},{2,0},{3,147},{4,2},{5,149},{6,4},{7,151},{8,6},{9,... | collective-permute-start | bytes 3145736 | tf_op jit(solution)/shard_map/ppermute | solution.py:56
  43.0 20.8 %collective-permute-start.18 = (bf16[128,4096]{1,0:T(8,128)(2,1)S(1)}, bf16[128,4096]{1,0:T(8,128)(2,1)S(1)}, u32[]{:S(2)}, u32[]{:S(2)}) collective-permute-start(bf16[128,4096]{1,0:T(8,128)(2,1)S(1)} %constant_dynamic-update-slice_fusion.5.refs_1_), channel_id=1, source_target_pairs={{0,2},{1,17},{2,4},{3,19},{4,6},{5,21},{6,8},{7,23},{8,10},{9,25},... | collective-permute-start | bytes 3145736 | tf_op jit(solution)/shard_map/ppermute | solution.py:56
  48.3 15.5 %collective-permute-start.13 = (bf16[64,4096]{1,0:T(8,128)(2,1)S(1)}, bf16[64,4096]{1,0:T(8,128)(2,1)S(1)}, u32[]{:S(2)}, u32[]{:S(2)}) collective-permute-start(bf16[64,4096]{1,0:T(8,128)(2,1)S(1)} %constant_dynamic-update-slice_fusion.7.refs_0_), channel_id=1, source_target_pairs={{0,2},{1,17},{2,4},{3,19},{4,6},{5,21},{6,8},{7,23},{8,10},{9,25},... | collective-permute-start | bytes 1572872 | tf_op jit(solution)/shard_map/ppermute | solution.py:56
  54.7 20.8 %collective-permute-start.16 = (bf16[128,4096]{1,0:T(8,128)(2,1)S(1)}, bf16[128,4096]{1,0:T(8,128)(2,1)S(1)}, u32[]{:S(2)}, u32[]{:S(2)}) collective-permute-start(bf16[128,4096]{1,0:T(8,128)(2,1)S(1)} %collective-permute-done.15.refs_3_), channel_id=1, source_target_pairs={{0,14},{1,145},{2,0},{3,147},{4,2},{5,149},{6,4},{7,151},{8,6},{9,... | collective-permute-start | bytes 3145736 | tf_op jit(solution)/shard_map/ppermute | solution.py:56
  58.2 17.4 %collective-permute-start.12 = (bf16[64,4096]{1,0:T(8,128)(2,1)S(1)}, bf16[64,4096]{1,0:T(8,128)(2,1)S(1)}, u32[]{:S(2)}, u32[]{:S(2)}) collective-permute-start(bf16[64,4096]{1,0:T(8,128)(2,1)S(1)} %constant_dynamic-update-slice_fusion.7.refs_0_), channel_id=1, source_target_pairs={{0,14},{1,145},{2,0},{3,147},{4,2},{5,149},{6,4},{7,151},{8,6},{9,... | collective-permute-start | bytes 1572872 | tf_op jit(solution)/shard_map/ppermute | solution.py:56
  58.2 11.2 %collective-permute-start.14 = (bf16[64,4096]{1,0:T(8,128)(2,1)S(1)}, bf16[64,4096]{1,0:T(8,128)(2,1)S(1)}, u32[]{:S(2)}, u32[]{:S(2)}) collective-permute-start(bf16[64,4096]{1,0:T(8,128)(2,1)S(1)} %collective-permute-done.9.refs_2_), channel_id=1, source_target_pairs={{0,2},{1,17},{2,4},{3,19},{4,6},{5,21},{6,8},{7,23},{8,10},{9,25},... | collective-permute-start | bytes 1572872 | tf_op jit(solution)/shard_map/ppermute | solution.py:56
  63.8 11.7 %collective-permute-start.17 = (bf16[64,4096]{1,0:T(8,128)(2,1)S(1)}, bf16[64,4096]{1,0:T(8,128)(2,1)S(1)}, u32[]{:S(2)}, u32[]{:S(2)}) collective-permute-start(bf16[64,4096]{1,0:T(8,128)(2,1)S(1)} %collective-permute-done.13.refs_1_), channel_id=1, source_target_pairs={{0,2},{1,17},{2,4},{3,19},{4,6},{5,21},{6,8},{7,23},{8,10},{9,25},... | collective-permute-start | bytes 1572872 | tf_op jit(solution)/shard_map/ppermute | solution.py:56
  75.5 8.7 %copy-start.1 = (f32[512]{0:T(512)S(1)}, f32[512]{0:T(512)}, u32[]{:S(2)}) copy-start(f32[512]{0:T(512)} %param.13) | copy-start | bytes 6148
  79.4 4.8 %collective-permute-start.19 = (f32[8,512]{1,0:T(8,128)S(1)}, f32[8,512]{1,0:T(8,128)S(1)}, u32[]{:S(2)}, u32[]{:S(2)}) collective-permute-start(f32[8,512]{1,0:T(8,128)S(1)} %get-tuple-element.46), channel_id=1, source_target_pairs={{0,1},{1,0},{2,3},{3,2},{4,5},{5,4},{6,7},{7,6},{8,9},{9,8},{10,11... | collective-permute-start | bytes 49160 | tf_op jit(solution)/shard_map/ppermute | solution.py:39

commit v6 on v5

--- a/solution.py
+++ b/solution.py
@@ -63,39 +63,33 @@
     return Piece(rows, offsets)
 
 
-def together(pieces):
-    if pieces[0].rows is not None:
-        for piece, rows in zip(pieces, lax.optimization_barrier([p.rows for p in pieces])):
-            piece.rows = rows
-
-
 def spread(piece):
     piece = join([piece, piece.fetch((AZ, AZ), ZN // 2)])
     return [piece] + [piece.fetch(STAGES[0], steps) for steps in (1, -1, 2)]
 
 
-def gather(near, first):
+def gather(near, first, together):
     near, half = join(near), sum(len(p.offsets[0]) for p in near) // 2
     last = STAGES[2]
     ahead, behind = near.fetch(STAGES[1], 1), near.fetch(STAGES[1], -1)
     next_, prev = [near.fetch(last, 1)], [near.fetch(last, -1)]
     together([ahead, behind, next_[0], prev[0]])
+    far_c = prev[0].fetch(last, -1)
     far_a = ahead.part(0, half).fetch(STAGES[1], 1)
     far_b = behind.part(half, 2 * half).fetch(STAGES[1], -1)
     one = join([ahead, behind])
-    far_a, far_b = first([near, one], far_a, far_b)
+    far_a, far_b, far_c = first([near, one], far_a, far_b, far_c)
     chunks = [near, one, join([far_a, far_b])]
     for chunk in chunks[1:]:
         next_.append(chunk.fetch(last, 1))
         prev.append(chunk.fetch(last, -1))
     if near.rows is not None:
         next_[1].rows, _ = lax.optimization_barrier((next_[1].rows, chunks[2].rows))
-        prev[0].rows, _ = lax.optimization_barrier((prev[0].rows, chunks[2].rows))
-    far = [prev[0].fetch(last, -1), next_[1].fetch(last, 1), prev[2].fetch(last, -1)]
+    far = [far_c, next_[1].fetch(last, 1), prev[2].fetch(last, -1)]
     return (
         chunks[:2],
-        [chunks[2], next_[0], prev[0], next_[1], prev[1]],
-        [next_[2], prev[2], *far],
+        [chunks[2], next_[0], prev[0], far_c, next_[1], prev[1]],
+        [next_[2], prev[2], *far[1:]],
     )
 
 
@@ -243,7 +237,7 @@
 
     start = np.zeros((local, 4), np.int32)
     start[:, 3] = np.arange(local)
-    dry = gather(spread(Piece(None, [start, start])), lambda group, *halves: halves)
+    dry = gather(spread(Piece(None, [start, start])), lambda group, *halves: halves, lambda group: None)
     ids = row_ids(dry, here, local)
     near = spread(Piece(references.reshape(local, voxels), [start, start]))
     rows, ids, wanted, key = lax.optimization_barrier((near[-1].rows, ids, wanted, key))
@@ -257,13 +251,21 @@
         count_rows = sum(len(p.offsets[0]) for p in group)
         at += -(-count_rows // LANES) * LANES
 
-    def first(group, far_a, far_b):
+    def together(group):
+        nonlocal kept
+        *rows, kept = lax.optimization_barrier([p.rows for p in group] + [kept])
+        for piece, there in zip(group, rows):
+            piece.rows = there
+
+    def first(group, *far):
         nonlocal stats
         take(group)
-        far_a.rows, far_b.rows, stats = lax.optimization_barrier((far_a.rows, far_b.rows, stats))
-        return far_a, far_b
-
-    for group in gather(near, first)[1:]:
+        *rows, stats = lax.optimization_barrier([p.rows for p in far] + [stats])
+        for piece, there in zip(far, rows):
+            piece.rows = there
+        return far
+
+    for group in gather(near, first, together)[1:]:
         take(group)
     mine, theirs = stats
     got = swap_cores(theirs)

time: 107 us -> 111 us (1.037)
  waiting for transfers between devices: 31.2 us -> 33 us
  starting transfers between devices: 35.7 us -> 37.4 us
    ppermute x3, starting transfers between devices: 7.41 us -> 12 us  [swap_cores(): return lax.ppermute(value, ALL, pairs(lambda at, core: (at, 1 - core)))]
    ppermute x17, starting transfers between devices: 28.2 us -> 25.4 us  [fetch(): lax.ppermute(self.rows, ALL, pairs(move))]
    ppermute x17, waiting for transfers between devices: 30.3 us -> 32.2 us  [fetch(): lax.ppermute(self.rows, ALL, pairs(move))]
  transfers between devices with their start and end apart: 20 -> 20, of which waited for: 8 -> 10; matrix products, arithmetic and copies ran while one was open for 3% -> 3% of each run, Pallas kernels for 9% -> 9%
where the time goes in v6:
time: 111 us
  starting transfers between devices  37.4 us (34%)
  waiting for transfers between devices  33 us (30%)
  blocking collectives  21.5 us (19%)
  Pallas kernels  14.5 us (13%)
  other arithmetic  3.28 us (3%)
  local copies, waits for them, and re-layouts  1.25 us (1%)
    ppermute x17, waiting for transfers between devices, fetch(): lax.ppermute(self.rows, ALL, pairs(move))  32.2 us
    ppermute x17, starting transfers between devices, fetch(): lax.ppermute(self.rows, ALL, pairs(move))  25.4 us
    all_to_all x1, blocking collectives, body(): lax.all_to_all(sent, ALL, 0, 0, tiled=True)  21.5 us
    pallas_call x3, Pallas kernels, score(): pl.pallas_call(functools.partial(score_kernel, scale, len(pieces), first,...  13.5 us
    ppermute x3, starting transfers between devices, swap_cores(): return lax.ppermute(value, ALL, pairs(lambda at, core: (at, 1 - core)))  12 us
  transfers between devices with their start and end apart: 20, of which 10 were waited for; matrix products, arithmetic and copies ran while one was open for 3% of the time, Pallas kernels for 9%

profile of v6, /device:TPU:1, one launch (start us, length us, event | category | flops | bytes accessed | tf_op | source)
XLA Modules:
  0.0 111.0 jit_solution(12559589052974369096)
XLA Ops:
  0.0 3.2 %collective-permute-start.9 = (bf16[512,4096]{1,0:T(8,128)(2,1)}, bf16[512,4096]{1,0:T(8,128)(2,1)}, u32[]{:S(2)}, u32[]{:S(2)}) collective-permute-start(bf16[512,4096]{1,0:T(8,128)(2,1)} %particles_ref.1), channel_id=1, source_target_pairs={{0,1},{1,0},{2,3},{3,2},{4,5},{5,4},{6,7},{7,6},{8,9},{9,8},{10,11... | collective-permute-start | bytes 12582920 | tf_op jit(solution)/shard_map/ppermute | solution.py:39
  3.2 5.2 %collective-permute-start = (bf16[8,4096]{1,0:T(8,128)(2,1)}, bf16[8,4096]{1,0:T(8,128)(2,1)S(1)}, u32[]{:S(2)}, u32[]{:S(2)}) collective-permute-start(bf16[8,4096]{1,0:T(8,128)(2,1)} %bitcast.17), channel_id=1, source_target_pairs={{0,8},{1,9},{2,10},{3,11},{4,12},{5,13},{6,14},{7,15},{8,0},{9,1},... | collective-permute-start | bytes 196616 | tf_op jit(solution)/shard_map/ppermute | solution.py:56
  8.4 0.9 fusion.12
  9.3 1.1 constant_dynamic-update-slice_fusion.4
  10.4 0.7 multiply_add_fusion
  11.1 0.0 collective-permute-done
  11.1 0.9 pad_maximum_fusion
  12.0 0.8 collective-permute-start.4
  12.8 3.5 %collective-permute-start.3 = (bf16[16,4096]{1,0:T(8,128)(2,1)S(1)}, bf16[16,4096]{1,0:T(8,128)(2,1)S(1)}, u32[]{:S(2)}, u32[]{:S(2)}) collective-permute-start(bf16[16,4096]{1,0:T(8,128)(2,1)S(1)} %pad_maximum_fusion), channel_id=1, source_target_pairs={{0,144},{1,15},{2,146},{3,1},{4,148},{5,3},{6,150},{7,5},{8,152},{... | collective-permute-start | bytes 393224 | tf_op jit(solution)/shard_map/ppermute | solution.py:56
  16.3 1.5 %collective-permute-start.1 = (bf16[16,4096]{1,0:T(8,128)(2,1)S(1)}, bf16[16,4096]{1,0:T(8,128)(2,1)S(1)}, u32[]{:S(2)}, u32[]{:S(2)}) collective-permute-start(bf16[16,4096]{1,0:T(8,128)(2,1)S(1)} %pad_maximum_fusion), channel_id=1, source_target_pairs={{0,128},{1,13},{2,130},{3,15},{4,132},{5,1},{6,134},{7,3},{8,136},... | collective-permute-start | bytes 393224 | tf_op jit(solution)/shard_map/ppermute | solution.py:56
  17.8 0.5 collective-permute-done.3
  18.3 4.2 %collective-permute-done.1 = bf16[16,4096]{1,0:T(8,128)(2,1)S(1)} collective-permute-done((bf16[16,4096]{1,0:T(8,128)(2,1)S(1)}, bf16[16,4096]{1,0:T(8,128)(2,1)S(1)}, u32[]{:S(2)}, u32[]{:S(2)}) %collective-permute-start.1) | collective-permute-done | bytes 131104 | tf_op jit(solution)/shard_map/ppermute | solution.py:56
  22.5 0.0 collective-permute-done.4
  22.5 1.3 %collective-permute-start.8 = (bf16[64,4096]{1,0:T(8,128)(2,1)S(1)}, bf16[64,4096]{1,0:T(8,128)(2,1)S(1)}, u32[]{:S(2)}, u32[]{:S(2)}) collective-permute-start(bf16[64,4096]{1,0:T(8,128)(2,1)S(1)} %constant_dynamic-update-slice_fusion.refs_0_), channel_id=1, source_target_pairs={{0,2},{1,17},{2,4},{3,19},{4,6},{5,21},{6,8},{7,23},{8,10},{9,25},... | collective-permute-start | bytes 1572872 | tf_op jit(solution)/shard_map/ppermute | solution.py:56
  23.8 1.4 %collective-permute-start.7 = (bf16[64,4096]{1,0:T(8,128)(2,1)S(1)}, bf16[64,4096]{1,0:T(8,128)(2,1)S(1)}, u32[]{:S(2)}, u32[]{:S(2)}) collective-permute-start(bf16[64,4096]{1,0:T(8,128)(2,1)S(1)} %constant_dynamic-update-slice_fusion.refs_0_), channel_id=1, source_target_pairs={{0,14},{1,145},{2,0},{3,147},{4,2},{5,149},{6,4},{7,151},{8,6},{9,... | collective-permute-start | bytes 1572872 | tf_op jit(solution)/shard_map/ppermute | solution.py:56
  25.3 1.4 %collective-permute-start.6 = (bf16[64,4096]{1,0:T(8,128)(2,1)S(1)}, bf16[64,4096]{1,0:T(8,128)(2,1)S(1)}, u32[]{:S(2)}, u32[]{:S(2)}) collective-permute-start(bf16[64,4096]{1,0:T(8,128)(2,1)S(1)} %constant_dynamic-update-slice_fusion.refs_0_), channel_id=1, source_target_pairs={{0,32},{1,33},{2,34},{3,35},{4,36},{5,37},{6,38},{7,39},{8,40},{9,... | collective-permute-start | bytes 1572872 | tf_op jit(solution)/shard_map/ppermute | solution.py:56
  26.6 1.4 %collective-permute-start.5 = (bf16[64,4096]{1,0:T(8,128)(2,1)S(1)}, bf16[64,4096]{1,0:T(8,128)(2,1)S(1)}, u32[]{:S(2)}, u32[]{:S(2)}) collective-permute-start(bf16[64,4096]{1,0:T(8,128)(2,1)S(1)} %constant_dynamic-update-slice_fusion.refs_0_), channel_id=1, source_target_pairs={{0,96},{1,97},{2,98},{3,99},{4,100},{5,101},{6,102},{7,103},{8,104... | collective-permute-start | bytes 1572872 | tf_op jit(solution)/shard_map/ppermute | solution.py:56
  28.0 4.1 %collective-permute-done.8.refs_2_ = bf16[64,4096]{1,0:T(8,128)(2,1)S(1)} collective-permute-done((bf16[64,4096]{1,0:T(8,128)(2,1)S(1)}, bf16[64,4096]{1,0:T(8,128)(2,1)S(1)}, u32[]{:S(2)}, u32[]{:S(2)}) %collective-permute-start.8) | collective-permute-done | bytes 524320 | tf_op jit(solution)/shard_map/ppermute | solution.py:56
  32.1 2.1 %collective-permute-start.2 = (f32[1,512]{1,0:T(1,128)S(1)}, f32[1,512]{1,0:T(1,128)S(1)}, u32[]{:S(2)}, u32[]{:S(2)}) collective-permute-start(f32[1,512]{1,0:T(1,128)S(1)} %bitcast.11), channel_id=1, source_target_pairs={{0,1},{1,0},{2,3},{3,2},{4,5},{5,4},{6,7},{7,6},{8,9},{9,8},{10,11... | collective-permute-start | bytes 6152 | tf_op jit(solution)/shard_map/ppermute | solution.py:39
  34.2 4.0 %collective-permute-done.6 = bf16[64,4096]{1,0:T(8,128)(2,1)S(1)} collective-permute-done((bf16[64,4096]{1,0:T(8,128)(2,1)S(1)}, bf16[64,4096]{1,0:T(8,128)(2,1)S(1)}, u32[]{:S(2)}, u32[]{:S(2)}) %collective-permute-start.6) | collective-permute-done | bytes 524320 | tf_op jit(solution)/shard_map/ppermute | solution.py:56
  38.2 0.0 collective-permute-done.5
  38.2 0.0 collective-permute-done.9.other_ref
  38.3 1.1 collective-permute-start.11
  39.4 1.7 %collective-permute-start.10 = (bf16[32,4096]{1,0:T(8,128)(2,1)S(1)}, bf16[32,4096]{1,0:T(8,128)(2,1)S(1)}, u32[]{:S(2)}, u32[]{:S(2)}) collective-permute-start(bf16[32,4096]{1,0:T(8,128)(2,1)S(1)} %slice.6), channel_id=1, source_target_pairs={{0,96},{1,97},{2,98},{3,99},{4,100},{5,101},{6,102},{7,103},{8,104... | collective-permute-start | bytes 786440 | tf_op jit(solution)/shard_map/ppermute | solution.py:56
  41.1 0.0 collective-permute-start.12
  41.1 1.3 %collective-permute-start.18 = (bf16[128,4096]{1,0:T(8,128)(2,1)S(1)}, bf16[128,4096]{1,0:T(8,128)(2,1)S(1)}, u32[]{:S(2)}, u32[]{:S(2)}) collective-permute-start(bf16[128,4096]{1,0:T(8,128)(2,1)S(1)} %constant_dynamic-update-slice_fusion.5.refs_1_), channel_id=1, source_target_pairs={{0,2},{1,17},{2,4},{3,19},{4,6},{5,21},{6,8},{7,23},{8,10},{9,25},... | collective-permute-start | bytes 3145736 | tf_op jit(solution)/shard_map/ppermute | solution.py:56
  42.4 0.0 collective-permute-done.2.other_wanted_ref
  42.4 1.7 %collective-permute-start.15 = (bf16[128,4096]{1,0:T(8,128)(2,1)S(1)}, bf16[128,4096]{1,0:T(8,128)(2,1)S(1)}, u32[]{:S(2)}, u32[]{:S(2)}) collective-permute-start(bf16[128,4096]{1,0:T(8,128)(2,1)S(1)} %constant_dynamic-update-slice_fusion.5.refs_1_), channel_id=1, source_target_pairs={{0,14},{1,145},{2,0},{3,147},{4,2},{5,149},{6,4},{7,151},{8,6},{9,... | collective-permute-start | bytes 3145736 | tf_op jit(solution)/shard_map/ppermute | solution.py:56
  44.2 5.2 %score.3 = (f32[8,512]{1,0:T(8,128)S(1)}, f32[8,512]{1,0:T(8,128)S(1)}, bf16[512,4096]{1,0:T(8,128)(2,1)S(1)}) custom-call(f32[1,1152]{1,0:T(1,128)S(1)} %broadcast_in_dim.13.ids_ref, f32[1,512]{1,0:T(1,128)S(1)} %bitcast.12, f32[1,512]{1,0:T(1,128)S(1)} %collective-permute-done.2.other_wanted_ref, bf16[512,4096]{1,0:T(8,128)(2,1)S(1)} %copy-done, ...), custom_call_target="tpu_custom_call" | custom-call | flops 1610612736 | bytes 1572864 | tf_op jit(solution)/shard_map/score/pallas_call | solution.py:168
  49.3 0.0 collective-permute-done.11
  49.4 1.3 %collective-permute-done.12.refs_3_ = bf16[64,4096]{1,0:T(8,128)(2,1)S(1)} collective-permute-done((bf16[64,4096]{1,0:T(8,128)(2,1)S(1)}, bf16[64,4096]{1,0:T(8,128)(2,1)S(1)}, u32[]{:S(2)}, u32[]{:S(2)}) %collective-permute-start.12) | collective-permute-done | bytes 524320 | tf_op jit(solution)/shard_map/ppermute | solution.py:56
  50.7 0.1 collective-permute-start.14
  50.8 5.6 %collective-permute-done.15.refs_4_ = bf16[128,4096]{1,0:T(8,128)(2,1)S(1)} collective-permute-done((bf16[128,4096]{1,0:T(8,128)(2,1)S(1)}, bf16[128,4096]{1,0:T(8,128)(2,1)S(1)}, u32[]{:S(2)}, u32[]{:S(2)}) %collective-permute-start.15) | collective-permute-done | bytes 1048608 | tf_op jit(solution)/shard_map/ppermute | solution.py:56
  56.4 3.0 %collective-permute-start.16 = (bf16[128,4096]{1,0:T(8,128)(2,1)S(1)}, bf16[128,4096]{1,0:T(8,128)(2,1)S(1)}, u32[]{:S(2)}, u32[]{:S(2)}) collective-permute-start(bf16[128,4096]{1,0:T(8,128)(2,1)S(1)} %collective-permute-done.15.refs_4_), channel_id=1, source_target_pairs={{0,14},{1,145},{2,0},{3,147},{4,2},{5,149},{6,4},{7,151},{8,6},{9,... | collective-permute-start | bytes 3145736 | tf_op jit(solution)/shard_map/ppermute | solution.py:56
  59.3 0.0 collective-permute-start.13
  59.3 8.1 %collective-permute-done.14.refs_1_ = bf16[64,4096]{1,0:T(8,128)(2,1)S(1)} collective-permute-done((bf16[64,4096]{1,0:T(8,128)(2,1)S(1)}, bf16[64,4096]{1,0:T(8,128)(2,1)S(1)}, u32[]{:S(2)}, u32[]{:S(2)}) %collective-permute-start.14) | collective-permute-done | bytes 524320 | tf_op jit(solution)/shard_map/ppermute | solution.py:56
  67.5 0.0 collective-permute-done.18.refs_5_
  67.5 5.1 %score.4 = (f32[8,512]{1,0:T(8,128)S(1)}, f32[8,512]{1,0:T(8,128)S(1)}) custom-call(f32[1,1152]{1,0:T(1,128)S(1)} %broadcast_in_dim.13.ids_ref, f32[1,512]{1,0:T(1,128)S(1)} %bitcast.13, f32[1,512]{1,0:T(1,128)S(1)} %collective-permute-done.2.other_wanted_ref, bf16[512,4096]{1,0:T(8,128)(2,1)S(1)} %copy-done, ...), custom_call_target="tpu_custom_call" | custom-call | flops 4294967296 | bytes 4194304 | tf_op jit(solution)/shard_map/score/pallas_call | solution.py:168
  72.6 4.1 %collective-permute-done.13.refs_0_ = bf16[64,4096]{1,0:T(8,128)(2,1)S(1)} collective-permute-done((bf16[64,4096]{1,0:T(8,128)(2,1)S(1)}, bf16[64,4096]{1,0:T(8,128)(2,1)S(1)}, u32[]{:S(2)}, u32[]{:S(2)}) %collective-permute-start.13) | collective-permute-done | bytes 524320 | tf_op jit(solution)/shard_map/ppermute | solution.py:56
  76.7 0.3 collective-permute-done.17.refs_3_
  77.0 0.0 collective-permute-done.16.refs_2_
  77.0 3.2 %score.5 = (f32[8,512]{1,0:T(8,128)S(1)}, f32[8,512]{1,0:T(8,128)S(1)}) custom-call(f32[1,1152]{1,0:T(1,128)S(1)} %broadcast_in_dim.13.ids_ref, f32[1,512]{1,0:T(1,128)S(1)} %bitcast.14, f32[1,512]{1,0:T(1,128)S(1)} %collective-permute-done.2.other_wanted_ref, bf16[512,4096]{1,0:T(8,128)(2,1)S(1)} %copy-done, ...), custom_call_target="tpu_custom_call" | custom-call | flops 2684354560 | bytes 2621440 | tf_op jit(solution)/shard_map/score/pallas_call | solution.py:168
  80.2 6.6 %collective-permute-start.19 = (f32[8,512]{1,0:T(8,128)S(1)}, f32[8,512]{1,0:T(8,128)S(1)}, u32[]{:S(2)}, u32[]{:S(2)}) collective-permute-start(f32[8,512]{1,0:T(8,128)S(1)} %get-tuple-element.48), channel_id=1, source_target_pairs={{0,1},{1,0},{2,3},{3,2},{4,5},{5,4},{6,7},{7,6},{8,9},{9,8},{10,11... | collective-permute-start | bytes 49160 | tf_op jit(solution)/shard_map/ppermute | solution.py:39
  86.9 0.8 collective-permute-done.19.got_ref
  87.7 1.0 class_sums.1
  88.7 21.5 %all_to_all.9 = f32[256,1,128]{2,1,0:T(1,128)S(1)} all-to-all(f32[256,1,128]{2,1,0:T(1,128)S(1)} %bitcast.10), channel_id=1, replica_groups=mesh['xh'=2,'y'=4,'xl'=2,'z'=8,'core'=2] {'xh','y','xl','z','core'}, dimensions={0} | all-to-all | bytes 262144 | tf_op jit(solution)/shard_map/all_to_all | solution.py:274
  110.2 0.3 reduce_sum.9
  110.5 0.5 multiply_bitcast_fusion
  (18 shorter events, 0.2 us)
Async XLA Ops:
  0.0 38.2 %collective-permute-start.9 = (bf16[512,4096]{1,0:T(8,128)(2,1)}, bf16[512,4096]{1,0:T(8,128)(2,1)}, u32[]{:S(2)}, u32[]{:S(2)}) collective-permute-start(bf16[512,4096]{1,0:T(8,128)(2,1)} %particles_ref.1), channel_id=1, source_target_pairs={{0,1},{1,0},{2,3},{3,2},{4,5},{5,4},{6,7},{7,6},{8,9},{9,8},{10,11... | collective-permute-start | bytes 12582920 | tf_op jit(solution)/shard_map/ppermute | solution.py:39
  3.2 7.9 %collective-permute-start = (bf16[8,4096]{1,0:T(8,128)(2,1)}, bf16[8,4096]{1,0:T(8,128)(2,1)S(1)}, u32[]{:S(2)}, u32[]{:S(2)}) collective-permute-start(bf16[8,4096]{1,0:T(8,128)(2,1)} %bitcast.17), channel_id=1, source_target_pairs={{0,8},{1,9},{2,10},{3,11},{4,12},{5,13},{6,14},{7,15},{8,0},{9,1},... | collective-permute-start | bytes 196616 | tf_op jit(solution)/shard_map/ppermute | solution.py:56
  8.4 35.7 %copy-start = (bf16[512,4096]{1,0:T(8,128)(2,1)S(1)}, bf16[512,4096]{1,0:T(8,128)(2,1)}, u32[]{:S(2)}) copy-start(bf16[512,4096]{1,0:T(8,128)(2,1)} %particles_ref.1) | copy-start | bytes 12582916
  12.0 10.5 %collective-permute-start.4 = (bf16[16,4096]{1,0:T(8,128)(2,1)S(1)}, bf16[16,4096]{1,0:T(8,128)(2,1)S(1)}, u32[]{:S(2)}, u32[]{:S(2)}) collective-permute-start(bf16[16,4096]{1,0:T(8,128)(2,1)S(1)} %pad_maximum_fusion), channel_id=1, source_target_pairs={{0,16},{1,3},{2,18},{3,5},{4,20},{5,7},{6,22},{7,9},{8,24},{9,11},... | collective-permute-start | bytes 393224 | tf_op jit(solution)/shard_map/ppermute | solution.py:56
  12.8 5.5 %collective-permute-start.3 = (bf16[16,4096]{1,0:T(8,128)(2,1)S(1)}, bf16[16,4096]{1,0:T(8,128)(2,1)S(1)}, u32[]{:S(2)}, u32[]{:S(2)}) collective-permute-start(bf16[16,4096]{1,0:T(8,128)(2,1)S(1)} %pad_maximum_fusion), channel_id=1, source_target_pairs={{0,144},{1,15},{2,146},{3,1},{4,148},{5,3},{6,150},{7,5},{8,152},{... | collective-permute-start | bytes 393224 | tf_op jit(solution)/shard_map/ppermute | solution.py:56
  16.3 6.2 %collective-permute-start.1 = (bf16[16,4096]{1,0:T(8,128)(2,1)S(1)}, bf16[16,4096]{1,0:T(8,128)(2,1)S(1)}, u32[]{:S(2)}, u32[]{:S(2)}) collective-permute-start(bf16[16,4096]{1,0:T(8,128)(2,1)S(1)} %pad_maximum_fusion), channel_id=1, source_target_pairs={{0,128},{1,13},{2,130},{3,15},{4,132},{5,1},{6,134},{7,3},{8,136},... | collective-permute-start | bytes 393224 | tf_op jit(solution)/shard_map/ppermute | solution.py:56
  22.5 9.6 %collective-permute-start.8 = (bf16[64,4096]{1,0:T(8,128)(2,1)S(1)}, bf16[64,4096]{1,0:T(8,128)(2,1)S(1)}, u32[]{:S(2)}, u32[]{:S(2)}) collective-permute-start(bf16[64,4096]{1,0:T(8,128)(2,1)S(1)} %constant_dynamic-update-slice_fusion.refs_0_), channel_id=1, source_target_pairs={{0,2},{1,17},{2,4},{3,19},{4,6},{5,21},{6,8},{7,23},{8,10},{9,25},... | collective-permute-start | bytes 1572872 | tf_op jit(solution)/shard_map/ppermute | solution.py:56
  23.8 10.4 %collective-permute-start.7 = (bf16[64,4096]{1,0:T(8,128)(2,1)S(1)}, bf16[64,4096]{1,0:T(8,128)(2,1)S(1)}, u32[]{:S(2)}, u32[]{:S(2)}) collective-permute-start(bf16[64,4096]{1,0:T(8,128)(2,1)S(1)} %constant_dynamic-update-slice_fusion.refs_0_), channel_id=1, source_target_pairs={{0,14},{1,145},{2,0},{3,147},{4,2},{5,149},{6,4},{7,151},{8,6},{9,... | collective-permute-start | bytes 1572872 | tf_op jit(solution)/shard_map/ppermute | solution.py:56
  25.3 13.0 %collective-permute-start.6 = (bf16[64,4096]{1,0:T(8,128)(2,1)S(1)}, bf16[64,4096]{1,0:T(8,128)(2,1)S(1)}, u32[]{:S(2)}, u32[]{:S(2)}) collective-permute-start(bf16[64,4096]{1,0:T(8,128)(2,1)S(1)} %constant_dynamic-update-slice_fusion.refs_0_), channel_id=1, source_target_pairs={{0,32},{1,33},{2,34},{3,35},{4,36},{5,37},{6,38},{7,39},{8,40},{9,... | collective-permute-start | bytes 1572872 | tf_op jit(solution)/shard_map/ppermute | solution.py:56
  26.6 11.6 %collective-permute-start.5 = (bf16[64,4096]{1,0:T(8,128)(2,1)S(1)}, bf16[64,4096]{1,0:T(8,128)(2,1)S(1)}, u32[]{:S(2)}, u32[]{:S(2)}) collective-permute-start(bf16[64,4096]{1,0:T(8,128)(2,1)S(1)} %constant_dynamic-update-slice_fusion.refs_0_), channel_id=1, source_target_pairs={{0,96},{1,97},{2,98},{3,99},{4,100},{5,101},{6,102},{7,103},{8,104... | collective-permute-start | bytes 1572872 | tf_op jit(solution)/shard_map/ppermute | solution.py:56
  32.1 10.3 %collective-permute-start.2 = (f32[1,512]{1,0:T(1,128)S(1)}, f32[1,512]{1,0:T(1,128)S(1)}, u32[]{:S(2)}, u32[]{:S(2)}) collective-permute-start(f32[1,512]{1,0:T(1,128)S(1)} %bitcast.11), channel_id=1, source_target_pairs={{0,1},{1,0},{2,3},{3,2},{4,5},{5,4},{6,7},{7,6},{8,9},{9,8},{10,11... | collective-permute-start | bytes 6152 | tf_op jit(solution)/shard_map/ppermute | solution.py:39
  38.3 11.0 %collective-permute-start.11 = (bf16[32,4096]{1,0:T(8,128)(2,1)S(1)}, bf16[32,4096]{1,0:T(8,128)(2,1)S(1)}, u32[]{:S(2)}, u32[]{:S(2)}) collective-permute-start(bf16[32,4096]{1,0:T(8,128)(2,1)S(1)} %slice.7), channel_id=1, source_target_pairs={{0,32},{1,33},{2,34},{3,35},{4,36},{5,37},{6,38},{7,39},{8,40},{9,... | collective-permute-start | bytes 786440 | tf_op jit(solution)/shard_map/ppermute | solution.py:56
  39.4 10.0 %collective-permute-start.10 = (bf16[32,4096]{1,0:T(8,128)(2,1)S(1)}, bf16[32,4096]{1,0:T(8,128)(2,1)S(1)}, u32[]{:S(2)}, u32[]{:S(2)}) collective-permute-start(bf16[32,4096]{1,0:T(8,128)(2,1)S(1)} %slice.6), channel_id=1, source_target_pairs={{0,96},{1,97},{2,98},{3,99},{4,100},{5,101},{6,102},{7,103},{8,104... | collective-permute-start | bytes 786440 | tf_op jit(solution)/shard_map/ppermute | solution.py:56
  41.1 9.5 %collective-permute-start.12 = (bf16[64,4096]{1,0:T(8,128)(2,1)S(1)}, bf16[64,4096]{1,0:T(8,128)(2,1)S(1)}, u32[]{:S(2)}, u32[]{:S(2)}) collective-permute-start(bf16[64,4096]{1,0:T(8,128)(2,1)S(1)} %collective-permute-done.8.refs_2_), channel_id=1, source_target_pairs={{0,2},{1,17},{2,4},{3,19},{4,6},{5,21},{6,8},{7,23},{8,10},{9,25},... | collective-permute-start | bytes 1572872 | tf_op jit(solution)/shard_map/ppermute | solution.py:56
  41.1 26.4 %collective-permute-start.18 = (bf16[128,4096]{1,0:T(8,128)(2,1)S(1)}, bf16[128,4096]{1,0:T(8,128)(2,1)S(1)}, u32[]{:S(2)}, u32[]{:S(2)}) collective-permute-start(bf16[128,4096]{1,0:T(8,128)(2,1)S(1)} %constant_dynamic-update-slice_fusion.5.refs_1_), channel_id=1, source_target_pairs={{0,2},{1,17},{2,4},{3,19},{4,6},{5,21},{6,8},{7,23},{8,10},{9,25},... | collective-permute-start | bytes 3145736 | tf_op jit(solution)/shard_map/ppermute | solution.py:56
  42.4 13.9 %collective-permute-start.15 = (bf16[128,4096]{1,0:T(8,128)(2,1)S(1)}, bf16[128,4096]{1,0:T(8,128)(2,1)S(1)}, u32[]{:S(2)}, u32[]{:S(2)}) collective-permute-start(bf16[128,4096]{1,0:T(8,128)(2,1)S(1)} %constant_dynamic-update-slice_fusion.5.refs_1_), channel_id=1, source_target_pairs={{0,14},{1,145},{2,0},{3,147},{4,2},{5,149},{6,4},{7,151},{8,6},{9,... | collective-permute-start | bytes 3145736 | tf_op jit(solution)/shard_map/ppermute | solution.py:56
  50.7 16.8 %collective-permute-start.14 = (bf16[64,4096]{1,0:T(8,128)(2,1)S(1)}, bf16[64,4096]{1,0:T(8,128)(2,1)S(1)}, u32[]{:S(2)}, u32[]{:S(2)}) collective-permute-start(bf16[64,4096]{1,0:T(8,128)(2,1)S(1)} %constant_dynamic-update-slice_fusion.7.refs_0_), channel_id=1, source_target_pairs={{0,2},{1,17},{2,4},{3,19},{4,6},{5,21},{6,8},{7,23},{8,10},{9,25},... | collective-permute-start | bytes 1572872 | tf_op jit(solution)/shard_map/ppermute | solution.py:56
  56.4 20.7 %collective-permute-start.16 = (bf16[128,4096]{1,0:T(8,128)(2,1)S(1)}, bf16[128,4096]{1,0:T(8,128)(2,1)S(1)}, u32[]{:S(2)}, u32[]{:S(2)}) collective-permute-start(bf16[128,4096]{1,0:T(8,128)(2,1)S(1)} %collective-permute-done.15.refs_4_), channel_id=1, source_target_pairs={{0,14},{1,145},{2,0},{3,147},{4,2},{5,149},{6,4},{7,151},{8,6},{9,... | collective-permute-start | bytes 3145736 | tf_op jit(solution)/shard_map/ppermute | solution.py:56
  59.3 17.4 %collective-permute-start.13 = (bf16[64,4096]{1,0:T(8,128)(2,1)S(1)}, bf16[64,4096]{1,0:T(8,128)(2,1)S(1)}, u32[]{:S(2)}, u32[]{:S(2)}) collective-permute-start(bf16[64,4096]{1,0:T(8,128)(2,1)S(1)} %constant_dynamic-update-slice_fusion.7.refs_0_), channel_id=1, source_target_pairs={{0,14},{1,145},{2,0},{3,147},{4,2},{5,149},{6,4},{7,151},{8,6},{9,... | collective-permute-start | bytes 1572872 | tf_op jit(solution)/shard_map/ppermute | solution.py:56
  67.5 9.5 %collective-permute-start.17 = (bf16[64,4096]{1,0:T(8,128)(2,1)S(1)}, bf16[64,4096]{1,0:T(8,128)(2,1)S(1)}, u32[]{:S(2)}, u32[]{:S(2)}) collective-permute-start(bf16[64,4096]{1,0:T(8,128)(2,1)S(1)} %collective-permute-done.14.refs_1_), channel_id=1, source_target_pairs={{0,2},{1,17},{2,4},{3,19},{4,6},{5,21},{6,8},{7,23},{8,10},{9,25},... | collective-permute-start | bytes 1572872 | tf_op jit(solution)/shard_map/ppermute | solution.py:56
  77.0 10.7 %copy-start.1 = (f32[512]{0:T(512)S(1)}, f32[512]{0:T(512)}, u32[]{:S(2)}) copy-start(f32[512]{0:T(512)} %param.13) | copy-start | bytes 6148
  80.2 7.5 %collective-permute-start.19 = (f32[8,512]{1,0:T(8,128)S(1)}, f32[8,512]{1,0:T(8,128)S(1)}, u32[]{:S(2)}, u32[]{:S(2)}) collective-permute-start(f32[8,512]{1,0:T(8,128)S(1)} %get-tuple-element.48), channel_id=1, source_target_pairs={{0,1},{1,0},{2,3},{3,2},{4,5},{5,4},{6,7},{7,6},{8,9},{9,8},{10,11... | collective-permute-start | bytes 49160 | tf_op jit(solution)/shard_map/ppermute | solution.py:39

commit v7 on v6

--- a/solution.py
+++ b/solution.py
@@ -83,13 +83,17 @@
     for chunk in chunks[1:]:
         next_.append(chunk.fetch(last, 1))
         prev.append(chunk.fetch(last, -1))
-    if near.rows is not None:
-        next_[1].rows, _ = lax.optimization_barrier((next_[1].rows, chunks[2].rows))
-    far = [far_c, next_[1].fetch(last, 1), prev[2].fetch(last, -1)]
+    side_a, side_b = far_c.fetch(STAGES[1], 1), far_c.fetch(STAGES[1], -1)
+    far = [
+        side_a,
+        side_b,
+        side_a.part(0, half).fetch(STAGES[1], 1),
+        side_b.part(half, 2 * half).fetch(STAGES[1], -1),
+    ]
     return (
         chunks[:2],
         [chunks[2], next_[0], prev[0], far_c, next_[1], prev[1]],
-        [next_[2], prev[2], *far[1:]],
+        [next_[2], prev[2], *far],
     )
 
 

time: 111 us -> 104 us (0.937)
  waiting for transfers between devices: 33 us -> 26.4 us
  blocking collectives: 21.5 us -> 19.9 us
    ppermute x17 -> x19, waiting for transfers between devices: 32.2 us -> 25.6 us  [fetch(): lax.ppermute(self.rows, ALL, pairs(move))]
    ppermute x17 -> x19, starting transfers between devices: 25.4 us -> 27.2 us  [fetch(): lax.ppermute(self.rows, ALL, pairs(move))]
    all_to_all x1, blocking collectives: 21.5 us -> 19.9 us  [body(): lax.all_to_all(sent, ALL, 0, 0, tiled=True)]
  transfers between devices with their start and end apart: 20 -> 22, of which waited for: 10 -> 9; matrix products, arithmetic and copies ran while one was open for 3% -> 4% of each run, Pallas kernels for 9% -> 10%
where the time goes in v7:
time: 104 us
  starting transfers between devices  38.5 us (37%)
  waiting for transfers between devices  26.4 us (25%)
  blocking collectives  19.9 us (19%)
  Pallas kernels  14.5 us (14%)
  other arithmetic  3.28 us (3%)
  local copies, waits for them, and re-layouts  1.29 us (1%)
    ppermute x19, starting transfers between devices, fetch(): lax.ppermute(self.rows, ALL, pairs(move))  27.2 us
    ppermute x19, waiting for transfers between devices, fetch(): lax.ppermute(self.rows, ALL, pairs(move))  25.6 us
    all_to_all x1, blocking collectives, body(): lax.all_to_all(sent, ALL, 0, 0, tiled=True)  19.9 us
    pallas_call x3, Pallas kernels, score(): pl.pallas_call(functools.partial(score_kernel, scale, len(pieces), first,...  13.5 us
    ppermute x3, starting transfers between devices, swap_cores(): return lax.ppermute(value, ALL, pairs(lambda at, core: (at, 1 - core)))  11.3 us
  transfers between devices with their start and end apart: 22, of which 9 were waited for; matrix products, arithmetic and copies ran while one was open for 4% of the time, Pallas kernels for 10%

profile of v7, /device:TPU:1, one launch (start us, length us, event | category | flops | bytes accessed | tf_op | source)
XLA Modules:
  0.0 104.1 jit_solution(8919332303334192789)
XLA Ops:
  0.0 3.2 %collective-permute-start.9 = (bf16[512,4096]{1,0:T(8,128)(2,1)}, bf16[512,4096]{1,0:T(8,128)(2,1)}, u32[]{:S(2)}, u32[]{:S(2)}) collective-permute-start(bf16[512,4096]{1,0:T(8,128)(2,1)} %particles_ref.1), channel_id=1, source_target_pairs={{0,1},{1,0},{2,3},{3,2},{4,5},{5,4},{6,7},{7,6},{8,9},{9,8},{10,11... | collective-permute-start | bytes 12582920 | tf_op jit(solution)/shard_map/ppermute | solution.py:39
  3.2 5.2 %collective-permute-start = (bf16[8,4096]{1,0:T(8,128)(2,1)}, bf16[8,4096]{1,0:T(8,128)(2,1)S(1)}, u32[]{:S(2)}, u32[]{:S(2)}) collective-permute-start(bf16[8,4096]{1,0:T(8,128)(2,1)} %bitcast.17), channel_id=1, source_target_pairs={{0,8},{1,9},{2,10},{3,11},{4,12},{5,13},{6,14},{7,15},{8,0},{9,1},... | collective-permute-start | bytes 196616 | tf_op jit(solution)/shard_map/ppermute | solution.py:56
  8.4 0.9 fusion.12
  9.3 1.1 %constant_dynamic-update-slice_fusion.4 = bf16[64,4096]{1,0:T(8,128)(2,1)S(1)} fusion(bf16[1,8,4096]{2,1,0:T(8,128)(2,1)} %param.8), kind=kLoop, calls=%fused_computation.5 | loop fusion | bytes 131072
  10.4 0.7 multiply_add_fusion
  11.1 0.0 collective-permute-done
  11.1 0.9 pad_maximum_fusion
  12.0 4.3 %collective-permute-start.1 = (bf16[16,4096]{1,0:T(8,128)(2,1)S(1)}, bf16[16,4096]{1,0:T(8,128)(2,1)S(1)}, u32[]{:S(2)}, u32[]{:S(2)}) collective-permute-start(bf16[16,4096]{1,0:T(8,128)(2,1)S(1)} %pad_maximum_fusion), channel_id=1, source_target_pairs={{0,128},{1,13},{2,130},{3,15},{4,132},{5,1},{6,134},{7,3},{8,136},... | collective-permute-start | bytes 393224 | tf_op jit(solution)/shard_map/ppermute | solution.py:56
  16.3 0.7 collective-permute-start.3
  17.0 0.7 collective-permute-start.4
  17.8 3.8 %collective-permute-done.3 = bf16[16,4096]{1,0:T(8,128)(2,1)S(1)} collective-permute-done((bf16[16,4096]{1,0:T(8,128)(2,1)S(1)}, bf16[16,4096]{1,0:T(8,128)(2,1)S(1)}, u32[]{:S(2)}, u32[]{:S(2)}) %collective-permute-start.3) | collective-permute-done | bytes 131104 | tf_op jit(solution)/shard_map/ppermute | solution.py:56
  21.6 0.0 collective-permute-done.1
  21.6 0.7 collective-permute-done.4
  22.4 3.1 %collective-permute-start.5 = (bf16[64,4096]{1,0:T(8,128)(2,1)S(1)}, bf16[64,4096]{1,0:T(8,128)(2,1)S(1)}, u32[]{:S(2)}, u32[]{:S(2)}) collective-permute-start(bf16[64,4096]{1,0:T(8,128)(2,1)S(1)} %constant_dynamic-update-slice_fusion.refs_0_), channel_id=1, source_target_pairs={{0,96},{1,97},{2,98},{3,99},{4,100},{5,101},{6,102},{7,103},{8,104... | collective-permute-start | bytes 1572872 | tf_op jit(solution)/shard_map/ppermute | solution.py:56
  25.5 0.0 collective-permute-start.6
  25.5 2.5 %collective-permute-start.7 = (bf16[64,4096]{1,0:T(8,128)(2,1)S(1)}, bf16[64,4096]{1,0:T(8,128)(2,1)S(1)}, u32[]{:S(2)}, u32[]{:S(2)}) collective-permute-start(bf16[64,4096]{1,0:T(8,128)(2,1)S(1)} %constant_dynamic-update-slice_fusion.refs_0_), channel_id=1, source_target_pairs={{0,14},{1,145},{2,0},{3,147},{4,2},{5,149},{6,4},{7,151},{8,6},{9,... | collective-permute-start | bytes 1572872 | tf_op jit(solution)/shard_map/ppermute | solution.py:56
  28.0 8.4 %collective-permute-done.5 = bf16[64,4096]{1,0:T(8,128)(2,1)S(1)} collective-permute-done((bf16[64,4096]{1,0:T(8,128)(2,1)S(1)}, bf16[64,4096]{1,0:T(8,128)(2,1)S(1)}, u32[]{:S(2)}, u32[]{:S(2)}) %collective-permute-start.5) | collective-permute-done | bytes 524320 | tf_op jit(solution)/shard_map/ppermute | solution.py:56
  36.4 1.2 %collective-permute-start.2 = (f32[1,512]{1,0:T(1,128)S(1)}, f32[1,512]{1,0:T(1,128)S(1)}, u32[]{:S(2)}, u32[]{:S(2)}) collective-permute-start(f32[1,512]{1,0:T(1,128)S(1)} %bitcast.11), channel_id=1, source_target_pairs={{0,1},{1,0},{2,3},{3,2},{4,5},{5,4},{6,7},{7,6},{8,9},{9,8},{10,11... | collective-permute-start | bytes 6152 | tf_op jit(solution)/shard_map/ppermute | solution.py:39
  37.6 1.9 %collective-permute-done.6 = bf16[64,4096]{1,0:T(8,128)(2,1)S(1)} collective-permute-done((bf16[64,4096]{1,0:T(8,128)(2,1)S(1)}, bf16[64,4096]{1,0:T(8,128)(2,1)S(1)}, u32[]{:S(2)}, u32[]{:S(2)}) %collective-permute-start.6) | collective-permute-done | bytes 524320 | tf_op jit(solution)/shard_map/ppermute | solution.py:56
  39.5 0.0 collective-permute-done.7.refs_1_
  39.5 0.0 collective-permute-done.8.refs_2_
  39.5 0.0 collective-permute-done.9.other_ref
  39.6 1.6 %collective-permute-start.10 = (bf16[32,4096]{1,0:T(8,128)(2,1)S(1)}, bf16[32,4096]{1,0:T(8,128)(2,1)S(1)}, u32[]{:S(2)}, u32[]{:S(2)}) collective-permute-start(bf16[32,4096]{1,0:T(8,128)(2,1)S(1)} %slice.12), channel_id=1, source_target_pairs={{0,96},{1,97},{2,98},{3,99},{4,100},{5,101},{6,102},{7,103},{8,104... | collective-permute-start | bytes 786440 | tf_op jit(solution)/shard_map/ppermute | solution.py:56
  41.2 0.1 collective-permute-start.11
  41.3 1.3 %collective-permute-start.12 = (bf16[64,4096]{1,0:T(8,128)(2,1)S(1)}, bf16[64,4096]{1,0:T(8,128)(2,1)S(1)}, u32[]{:S(2)}, u32[]{:S(2)}) collective-permute-start(bf16[64,4096]{1,0:T(8,128)(2,1)S(1)} %collective-permute-done.8.refs_2_), channel_id=1, source_target_pairs={{0,2},{1,17},{2,4},{3,19},{4,6},{5,21},{6,8},{7,23},{8,10},{9,25},... | collective-permute-start | bytes 1572872 | tf_op jit(solution)/shard_map/ppermute | solution.py:56
  42.6 1.6 %collective-permute-start.19 = (bf16[128,4096]{1,0:T(8,128)(2,1)S(1)}, bf16[128,4096]{1,0:T(8,128)(2,1)S(1)}, u32[]{:S(2)}, u32[]{:S(2)}) collective-permute-start(bf16[128,4096]{1,0:T(8,128)(2,1)S(1)} %constant_dynamic-update-slice_fusion.5.refs_1_), channel_id=1, source_target_pairs={{0,14},{1,145},{2,0},{3,147},{4,2},{5,149},{6,4},{7,151},{8,6},{9,... | collective-permute-start | bytes 3145736 | tf_op jit(solution)/shard_map/ppermute | solution.py:56
  44.2 0.0 collective-permute-start.20
  44.2 5.2 %score.3 = (f32[8,512]{1,0:T(8,128)S(1)}, f32[8,512]{1,0:T(8,128)S(1)}, bf16[512,4096]{1,0:T(8,128)(2,1)S(1)}) custom-call(f32[1,1152]{1,0:T(1,128)S(1)} %broadcast_in_dim.13.ids_ref, f32[1,512]{1,0:T(1,128)S(1)} %bitcast.12, f32[1,512]{1,0:T(1,128)S(1)} %collective-permute-done.2.other_wanted_ref, bf16[512,4096]{1,0:T(8,128)(2,1)S(1)} %copy-done, ...), custom_call_target="tpu_custom_call" | custom-call | flops 1610612736 | bytes 1572864 | tf_op jit(solution)/shard_map/score/pallas_call | solution.py:172
  49.4 0.0 collective-permute-done.11
  49.4 1.5 %collective-permute-done.12.refs_3_ = bf16[64,4096]{1,0:T(8,128)(2,1)S(1)} collective-permute-done((bf16[64,4096]{1,0:T(8,128)(2,1)S(1)}, bf16[64,4096]{1,0:T(8,128)(2,1)S(1)}, u32[]{:S(2)}, u32[]{:S(2)}) %collective-permute-start.12) | collective-permute-done | bytes 524320 | tf_op jit(solution)/shard_map/ppermute | solution.py:56
  50.9 2.6 %collective-permute-start.15 = (bf16[64,4096]{1,0:T(8,128)(2,1)S(1)}, bf16[64,4096]{1,0:T(8,128)(2,1)S(1)}, u32[]{:S(2)}, u32[]{:S(2)}) collective-permute-start(bf16[64,4096]{1,0:T(8,128)(2,1)S(1)} %collective-permute-done.12.refs_3_), channel_id=1, source_target_pairs={{0,96},{1,97},{2,98},{3,99},{4,100},{5,101},{6,102},{7,103},{8,104... | collective-permute-start | bytes 1572872 | tf_op jit(solution)/shard_map/ppermute | solution.py:56
  53.6 1.3 %collective-permute-start.13 = (bf16[64,4096]{1,0:T(8,128)(2,1)S(1)}, bf16[64,4096]{1,0:T(8,128)(2,1)S(1)}, u32[]{:S(2)}, u32[]{:S(2)}) collective-permute-start(bf16[64,4096]{1,0:T(8,128)(2,1)S(1)} %constant_dynamic-update-slice_fusion.7.refs_0_), channel_id=1, source_target_pairs={{0,14},{1,145},{2,0},{3,147},{4,2},{5,149},{6,4},{7,151},{8,6},{9,... | collective-permute-start | bytes 1572872 | tf_op jit(solution)/shard_map/ppermute | solution.py:56
  54.9 5.5 %collective-permute-done.15.refs_2_ = bf16[64,4096]{1,0:T(8,128)(2,1)S(1)} collective-permute-done((bf16[64,4096]{1,0:T(8,128)(2,1)S(1)}, bf16[64,4096]{1,0:T(8,128)(2,1)S(1)}, u32[]{:S(2)}, u32[]{:S(2)}) %collective-permute-start.15) | collective-permute-done | bytes 524320 | tf_op jit(solution)/shard_map/ppermute | solution.py:56
  60.4 0.5 collective-permute-start.14
  60.9 2.6 %collective-permute-done.16.refs_3_ = bf16[64,4096]{1,0:T(8,128)(2,1)S(1)} collective-permute-done((bf16[64,4096]{1,0:T(8,128)(2,1)S(1)}, bf16[64,4096]{1,0:T(8,128)(2,1)S(1)}, u32[]{:S(2)}, u32[]{:S(2)}) %collective-permute-start.16) | collective-permute-done | bytes 524320 | tf_op jit(solution)/shard_map/ppermute | solution.py:56
  63.5 0.4 collective-permute-start.17
  63.9 0.0 collective-permute-done.19.refs_4_
  63.9 1.4 %collective-permute-start.18 = (bf16[32,4096]{1,0:T(8,128)(2,1)S(1)}, bf16[32,4096]{1,0:T(8,128)(2,1)S(1)}, u32[]{:S(2)}, u32[]{:S(2)}) collective-permute-start(bf16[32,4096]{1,0:T(8,128)(2,1)S(1)} %slice.17), channel_id=1, source_target_pairs={{0,32},{1,33},{2,34},{3,35},{4,36},{5,37},{6,38},{7,39},{8,40},{9,... | collective-permute-start | bytes 786440 | tf_op jit(solution)/shard_map/ppermute | solution.py:56
  65.3 5.1 %score.4 = (f32[8,512]{1,0:T(8,128)S(1)}, f32[8,512]{1,0:T(8,128)S(1)}) custom-call(f32[1,1152]{1,0:T(1,128)S(1)} %broadcast_in_dim.13.ids_ref, f32[1,512]{1,0:T(1,128)S(1)} %bitcast.13, f32[1,512]{1,0:T(1,128)S(1)} %collective-permute-done.2.other_wanted_ref, bf16[512,4096]{1,0:T(8,128)(2,1)S(1)} %copy-done, ...), custom_call_target="tpu_custom_call" | custom-call | flops 4294967296 | bytes 4194304 | tf_op jit(solution)/shard_map/score/pallas_call | solution.py:172
  70.4 0.0 collective-permute-done.17.refs_4_
  70.4 1.1 %collective-permute-done.18.refs_5_ = bf16[32,4096]{1,0:T(8,128)(2,1)S(1)} collective-permute-done((bf16[32,4096]{1,0:T(8,128)(2,1)S(1)}, bf16[32,4096]{1,0:T(8,128)(2,1)S(1)}, u32[]{:S(2)}, u32[]{:S(2)}) %collective-permute-start.18) | collective-permute-done | bytes 262176 | tf_op jit(solution)/shard_map/ppermute | solution.py:56
  71.5 3.2 %score.5 = (f32[8,512]{1,0:T(8,128)S(1)}, f32[8,512]{1,0:T(8,128)S(1)}) custom-call(f32[1,1152]{1,0:T(1,128)S(1)} %broadcast_in_dim.13.ids_ref, f32[1,512]{1,0:T(1,128)S(1)} %bitcast.14, f32[1,512]{1,0:T(1,128)S(1)} %collective-permute-done.2.other_wanted_ref, bf16[512,4096]{1,0:T(8,128)(2,1)S(1)} %copy-done, ...), custom_call_target="tpu_custom_call" | custom-call | flops 2684354560 | bytes 2621440 | tf_op jit(solution)/shard_map/score/pallas_call | solution.py:172
  74.7 6.8 %collective-permute-start.21 = (f32[8,512]{1,0:T(8,128)S(1)}, f32[8,512]{1,0:T(8,128)S(1)}, u32[]{:S(2)}, u32[]{:S(2)}) collective-permute-start(f32[8,512]{1,0:T(8,128)S(1)} %get-tuple-element.46), channel_id=1, source_target_pairs={{0,1},{1,0},{2,3},{3,2},{4,5},{5,4},{6,7},{7,6},{8,9},{9,8},{10,11... | collective-permute-start | bytes 49160 | tf_op jit(solution)/shard_map/ppermute | solution.py:39
  81.5 0.8 collective-permute-done.21.got_ref
  82.4 1.0 class_sums.1
  83.4 19.9 %all_to_all.9 = f32[256,1,128]{2,1,0:T(1,128)S(1)} all-to-all(f32[256,1,128]{2,1,0:T(1,128)S(1)} %bitcast.10), channel_id=1, replica_groups=mesh['xh'=2,'y'=4,'xl'=2,'z'=8,'core'=2] {'xh','y','xl','z','core'}, dimensions={0} | all-to-all | bytes 262144 | tf_op jit(solution)/shard_map/all_to_all | solution.py:278
  103.3 0.3 reduce_sum.9
  103.5 0.5 multiply_bitcast_fusion
  (24 shorter events, 0.2 us)
Async XLA Ops:
  0.0 39.5 %collective-permute-start.9 = (bf16[512,4096]{1,0:T(8,128)(2,1)}, bf16[512,4096]{1,0:T(8,128)(2,1)}, u32[]{:S(2)}, u32[]{:S(2)}) collective-permute-start(bf16[512,4096]{1,0:T(8,128)(2,1)} %particles_ref.1), channel_id=1, source_target_pairs={{0,1},{1,0},{2,3},{3,2},{4,5},{5,4},{6,7},{7,6},{8,9},{9,8},{10,11... | collective-permute-start | bytes 12582920 | tf_op jit(solution)/shard_map/ppermute | solution.py:39
  3.2 7.9 %collective-permute-start = (bf16[8,4096]{1,0:T(8,128)(2,1)}, bf16[8,4096]{1,0:T(8,128)(2,1)S(1)}, u32[]{:S(2)}, u32[]{:S(2)}) collective-permute-start(bf16[8,4096]{1,0:T(8,128)(2,1)} %bitcast.17), channel_id=1, source_target_pairs={{0,8},{1,9},{2,10},{3,11},{4,12},{5,13},{6,14},{7,15},{8,0},{9,1},... | collective-permute-start | bytes 196616 | tf_op jit(solution)/shard_map/ppermute | solution.py:56
  8.4 35.8 %copy-start = (bf16[512,4096]{1,0:T(8,128)(2,1)S(1)}, bf16[512,4096]{1,0:T(8,128)(2,1)}, u32[]{:S(2)}) copy-start(bf16[512,4096]{1,0:T(8,128)(2,1)} %particles_ref.1) | copy-start | bytes 12582916
  12.0 9.6 %collective-permute-start.1 = (bf16[16,4096]{1,0:T(8,128)(2,1)S(1)}, bf16[16,4096]{1,0:T(8,128)(2,1)S(1)}, u32[]{:S(2)}, u32[]{:S(2)}) collective-permute-start(bf16[16,4096]{1,0:T(8,128)(2,1)S(1)} %pad_maximum_fusion), channel_id=1, source_target_pairs={{0,128},{1,13},{2,130},{3,15},{4,132},{5,1},{6,134},{7,3},{8,136},... | collective-permute-start | bytes 393224 | tf_op jit(solution)/shard_map/ppermute | solution.py:56
  16.3 5.3 %collective-permute-start.3 = (bf16[16,4096]{1,0:T(8,128)(2,1)S(1)}, bf16[16,4096]{1,0:T(8,128)(2,1)S(1)}, u32[]{:S(2)}, u32[]{:S(2)}) collective-permute-start(bf16[16,4096]{1,0:T(8,128)(2,1)S(1)} %pad_maximum_fusion), channel_id=1, source_target_pairs={{0,144},{1,15},{2,146},{3,1},{4,148},{5,3},{6,150},{7,5},{8,152},{... | collective-permute-start | bytes 393224 | tf_op jit(solution)/shard_map/ppermute | solution.py:56
  17.0 5.3 %collective-permute-start.4 = (bf16[16,4096]{1,0:T(8,128)(2,1)S(1)}, bf16[16,4096]{1,0:T(8,128)(2,1)S(1)}, u32[]{:S(2)}, u32[]{:S(2)}) collective-permute-start(bf16[16,4096]{1,0:T(8,128)(2,1)S(1)} %pad_maximum_fusion), channel_id=1, source_target_pairs={{0,16},{1,3},{2,18},{3,5},{4,20},{5,7},{6,22},{7,9},{8,24},{9,11},... | collective-permute-start | bytes 393224 | tf_op jit(solution)/shard_map/ppermute | solution.py:56
  22.4 14.0 %collective-permute-start.5 = (bf16[64,4096]{1,0:T(8,128)(2,1)S(1)}, bf16[64,4096]{1,0:T(8,128)(2,1)S(1)}, u32[]{:S(2)}, u32[]{:S(2)}) collective-permute-start(bf16[64,4096]{1,0:T(8,128)(2,1)S(1)} %constant_dynamic-update-slice_fusion.refs_0_), channel_id=1, source_target_pairs={{0,96},{1,97},{2,98},{3,99},{4,100},{5,101},{6,102},{7,103},{8,104... | collective-permute-start | bytes 1572872 | tf_op jit(solution)/shard_map/ppermute | solution.py:56
  25.5 14.0 %collective-permute-start.6 = (bf16[64,4096]{1,0:T(8,128)(2,1)S(1)}, bf16[64,4096]{1,0:T(8,128)(2,1)S(1)}, u32[]{:S(2)}, u32[]{:S(2)}) collective-permute-start(bf16[64,4096]{1,0:T(8,128)(2,1)S(1)} %constant_dynamic-update-slice_fusion.refs_0_), channel_id=1, source_target_pairs={{0,32},{1,33},{2,34},{3,35},{4,36},{5,37},{6,38},{7,39},{8,40},{9,... | collective-permute-start | bytes 1572872 | tf_op jit(solution)/shard_map/ppermute | solution.py:56
  25.5 14.0 %collective-permute-start.7 = (bf16[64,4096]{1,0:T(8,128)(2,1)S(1)}, bf16[64,4096]{1,0:T(8,128)(2,1)S(1)}, u32[]{:S(2)}, u32[]{:S(2)}) collective-permute-start(bf16[64,4096]{1,0:T(8,128)(2,1)S(1)} %constant_dynamic-update-slice_fusion.refs_0_), channel_id=1, source_target_pairs={{0,14},{1,145},{2,0},{3,147},{4,2},{5,149},{6,4},{7,151},{8,6},{9,... | collective-permute-start | bytes 1572872 | tf_op jit(solution)/shard_map/ppermute | solution.py:56
  28.0 11.5 %collective-permute-start.8 = (bf16[64,4096]{1,0:T(8,128)(2,1)S(1)}, bf16[64,4096]{1,0:T(8,128)(2,1)S(1)}, u32[]{:S(2)}, u32[]{:S(2)}) collective-permute-start(bf16[64,4096]{1,0:T(8,128)(2,1)S(1)} %constant_dynamic-update-slice_fusion.refs_0_), channel_id=1, source_target_pairs={{0,2},{1,17},{2,4},{3,19},{4,6},{5,21},{6,8},{7,23},{8,10},{9,25},... | collective-permute-start | bytes 1572872 | tf_op jit(solution)/shard_map/ppermute | solution.py:56
  36.4 7.8 %collective-permute-start.2 = (f32[1,512]{1,0:T(1,128)S(1)}, f32[1,512]{1,0:T(1,128)S(1)}, u32[]{:S(2)}, u32[]{:S(2)}) collective-permute-start(f32[1,512]{1,0:T(1,128)S(1)} %bitcast.11), channel_id=1, source_target_pairs={{0,1},{1,0},{2,3},{3,2},{4,5},{5,4},{6,7},{7,6},{8,9},{9,8},{10,11... | collective-permute-start | bytes 6152 | tf_op jit(solution)/shard_map/ppermute | solution.py:39
  39.6 9.8 %collective-permute-start.10 = (bf16[32,4096]{1,0:T(8,128)(2,1)S(1)}, bf16[32,4096]{1,0:T(8,128)(2,1)S(1)}, u32[]{:S(2)}, u32[]{:S(2)}) collective-permute-start(bf16[32,4096]{1,0:T(8,128)(2,1)S(1)} %slice.12), channel_id=1, source_target_pairs={{0,96},{1,97},{2,98},{3,99},{4,100},{5,101},{6,102},{7,103},{8,104... | collective-permute-start | bytes 786440 | tf_op jit(solution)/shard_map/ppermute | solution.py:56
  41.2 8.2 %collective-permute-start.11 = (bf16[32,4096]{1,0:T(8,128)(2,1)S(1)}, bf16[32,4096]{1,0:T(8,128)(2,1)S(1)}, u32[]{:S(2)}, u32[]{:S(2)}) collective-permute-start(bf16[32,4096]{1,0:T(8,128)(2,1)S(1)} %slice.13), channel_id=1, source_target_pairs={{0,32},{1,33},{2,34},{3,35},{4,36},{5,37},{6,38},{7,39},{8,40},{9,... | collective-permute-start | bytes 786440 | tf_op jit(solution)/shard_map/ppermute | solution.py:56
  41.3 9.6 %collective-permute-start.12 = (bf16[64,4096]{1,0:T(8,128)(2,1)S(1)}, bf16[64,4096]{1,0:T(8,128)(2,1)S(1)}, u32[]{:S(2)}, u32[]{:S(2)}) collective-permute-start(bf16[64,4096]{1,0:T(8,128)(2,1)S(1)} %collective-permute-done.8.refs_2_), channel_id=1, source_target_pairs={{0,2},{1,17},{2,4},{3,19},{4,6},{5,21},{6,8},{7,23},{8,10},{9,25},... | collective-permute-start | bytes 1572872 | tf_op jit(solution)/shard_map/ppermute | solution.py:56
  42.6 21.3 %collective-permute-start.19 = (bf16[128,4096]{1,0:T(8,128)(2,1)S(1)}, bf16[128,4096]{1,0:T(8,128)(2,1)S(1)}, u32[]{:S(2)}, u32[]{:S(2)}) collective-permute-start(bf16[128,4096]{1,0:T(8,128)(2,1)S(1)} %constant_dynamic-update-slice_fusion.5.refs_1_), channel_id=1, source_target_pairs={{0,14},{1,145},{2,0},{3,147},{4,2},{5,149},{6,4},{7,151},{8,6},{9,... | collective-permute-start | bytes 3145736 | tf_op jit(solution)/shard_map/ppermute | solution.py:56
  44.2 21.1 %collective-permute-start.20 = (bf16[128,4096]{1,0:T(8,128)(2,1)S(1)}, bf16[128,4096]{1,0:T(8,128)(2,1)S(1)}, u32[]{:S(2)}, u32[]{:S(2)}) collective-permute-start(bf16[128,4096]{1,0:T(8,128)(2,1)S(1)} %constant_dynamic-update-slice_fusion.5.refs_1_), channel_id=1, source_target_pairs={{0,2},{1,17},{2,4},{3,19},{4,6},{5,21},{6,8},{7,23},{8,10},{9,25},... | collective-permute-start | bytes 3145736 | tf_op jit(solution)/shard_map/ppermute | solution.py:56
  50.9 9.4 %collective-permute-start.15 = (bf16[64,4096]{1,0:T(8,128)(2,1)S(1)}, bf16[64,4096]{1,0:T(8,128)(2,1)S(1)}, u32[]{:S(2)}, u32[]{:S(2)}) collective-permute-start(bf16[64,4096]{1,0:T(8,128)(2,1)S(1)} %collective-permute-done.12.refs_3_), channel_id=1, source_target_pairs={{0,96},{1,97},{2,98},{3,99},{4,100},{5,101},{6,102},{7,103},{8,104... | collective-permute-start | bytes 1572872 | tf_op jit(solution)/shard_map/ppermute | solution.py:56
  53.5 10.0 %collective-permute-start.16 = (bf16[64,4096]{1,0:T(8,128)(2,1)S(1)}, bf16[64,4096]{1,0:T(8,128)(2,1)S(1)}, u32[]{:S(2)}, u32[]{:S(2)}) collective-permute-start(bf16[64,4096]{1,0:T(8,128)(2,1)S(1)} %collective-permute-done.12.refs_3_), channel_id=1, source_target_pairs={{0,32},{1,33},{2,34},{3,35},{4,36},{5,37},{6,38},{7,39},{8,40},{9,... | collective-permute-start | bytes 1572872 | tf_op jit(solution)/shard_map/ppermute | solution.py:56
  53.6 16.8 %collective-permute-start.13 = (bf16[64,4096]{1,0:T(8,128)(2,1)S(1)}, bf16[64,4096]{1,0:T(8,128)(2,1)S(1)}, u32[]{:S(2)}, u32[]{:S(2)}) collective-permute-start(bf16[64,4096]{1,0:T(8,128)(2,1)S(1)} %constant_dynamic-update-slice_fusion.7.refs_0_), channel_id=1, source_target_pairs={{0,14},{1,145},{2,0},{3,147},{4,2},{5,149},{6,4},{7,151},{8,6},{9,... | collective-permute-start | bytes 1572872 | tf_op jit(solution)/shard_map/ppermute | solution.py:56
  60.4 10.0 %collective-permute-start.14 = (bf16[64,4096]{1,0:T(8,128)(2,1)S(1)}, bf16[64,4096]{1,0:T(8,128)(2,1)S(1)}, u32[]{:S(2)}, u32[]{:S(2)}) collective-permute-start(bf16[64,4096]{1,0:T(8,128)(2,1)S(1)} %constant_dynamic-update-slice_fusion.7.refs_0_), channel_id=1, source_target_pairs={{0,2},{1,17},{2,4},{3,19},{4,6},{5,21},{6,8},{7,23},{8,10},{9,25},... | collective-permute-start | bytes 1572872 | tf_op jit(solution)/shard_map/ppermute | solution.py:56
  63.5 6.9 %collective-permute-start.17 = (bf16[32,4096]{1,0:T(8,128)(2,1)S(1)}, bf16[32,4096]{1,0:T(8,128)(2,1)S(1)}, u32[]{:S(2)}, u32[]{:S(2)}) collective-permute-start(bf16[32,4096]{1,0:T(8,128)(2,1)S(1)} %slice.16), channel_id=1, source_target_pairs={{0,96},{1,97},{2,98},{3,99},{4,100},{5,101},{6,102},{7,103},{8,104... | collective-permute-start | bytes 786440 | tf_op jit(solution)/shard_map/ppermute | solution.py:56
  63.9 7.6 %collective-permute-start.18 = (bf16[32,4096]{1,0:T(8,128)(2,1)S(1)}, bf16[32,4096]{1,0:T(8,128)(2,1)S(1)}, u32[]{:S(2)}, u32[]{:S(2)}) collective-permute-start(bf16[32,4096]{1,0:T(8,128)(2,1)S(1)} %slice.17), channel_id=1, source_target_pairs={{0,32},{1,33},{2,34},{3,35},{4,36},{5,37},{6,38},{7,39},{8,40},{9,... | collective-permute-start | bytes 786440 | tf_op jit(solution)/shard_map/ppermute | solution.py:56
  71.5 10.9 %copy-start.1 = (f32[512]{0:T(512)S(1)}, f32[512]{0:T(512)}, u32[]{:S(2)}) copy-start(f32[512]{0:T(512)} %param.13) | copy-start | bytes 6148
  74.7 7.6 %collective-permute-start.21 = (f32[8,512]{1,0:T(8,128)S(1)}, f32[8,512]{1,0:T(8,128)S(1)}, u32[]{:S(2)}, u32[]{:S(2)}) collective-permute-start(f32[8,512]{1,0:T(8,128)S(1)} %get-tuple-element.46), channel_id=1, source_target_pairs={{0,1},{1,0},{2,3},{3,2},{4,5},{5,4},{6,7},{7,6},{8,9},{9,8},{10,11... | collective-permute-start | bytes 49160 | tf_op jit(solution)/shard_map/ppermute | solution.py:39

commit v8 on v7

--- a/solution.py
+++ b/solution.py
@@ -73,7 +73,7 @@
     last = STAGES[2]
     ahead, behind = near.fetch(STAGES[1], 1), near.fetch(STAGES[1], -1)
     next_, prev = [near.fetch(last, 1)], [near.fetch(last, -1)]
-    together([ahead, behind, next_[0], prev[0]])
+    together([ahead, next_[0], prev[0]])
     far_c = prev[0].fetch(last, -1)
     far_a = ahead.part(0, half).fetch(STAGES[1], 1)
     far_b = behind.part(half, 2 * half).fetch(STAGES[1], -1)

time: 104 us -> 102 us (0.981)
  starting transfers between devices: 38.5 us -> 35.8 us
    ppermute x3, starting transfers between devices: 11.3 us -> 9.04 us  [swap_cores(): return lax.ppermute(value, ALL, pairs(lambda at, core: (at, 1 - core)))]
  transfers between devices with their start and end apart: 22 -> 22, of which waited for: 9 -> 8; matrix products, arithmetic and copies ran while one was open for 4% -> 4% of each run, Pallas kernels for 10% -> 10%
where the time goes in v8:
time: 102 us
  starting transfers between devices  35.8 us (35%)
  waiting for transfers between devices  26.5 us (26%)
  blocking collectives  20.5 us (20%)
  Pallas kernels  14.5 us (14%)
  other arithmetic  3.28 us (3%)
  local copies, waits for them, and re-layouts  1.29 us (1%)
    ppermute x19, starting transfers between devices, fetch(): lax.ppermute(self.rows, ALL, pairs(move))  26.8 us
    ppermute x19, waiting for transfers between devices, fetch(): lax.ppermute(self.rows, ALL, pairs(move))  25.7 us
    all_to_all x1, blocking collectives, body(): lax.all_to_all(sent, ALL, 0, 0, tiled=True)  20.5 us
    pallas_call x3, Pallas kernels, score(): pl.pallas_call(functools.partial(score_kernel, scale, len(pieces), first,...  13.5 us
    ppermute x3, starting transfers between devices, swap_cores(): return lax.ppermute(value, ALL, pairs(lambda at, core: (at, 1 - core)))  9.04 us
  transfers between devices with their start and end apart: 22, of which 8 were waited for; matrix products, arithmetic and copies ran while one was open for 4% of the time, Pallas kernels for 10%

profile of v8, /device:TPU:1, one launch (start us, length us, event | category | flops | bytes accessed | tf_op | source)
XLA Modules:
  0.0 102.1 jit_solution(12457054763847999061)
XLA Ops:
  0.0 3.2 %collective-permute-start.8 = (bf16[512,4096]{1,0:T(8,128)(2,1)}, bf16[512,4096]{1,0:T(8,128)(2,1)}, u32[]{:S(2)}, u32[]{:S(2)}) collective-permute-start(bf16[512,4096]{1,0:T(8,128)(2,1)} %particles_ref.1), channel_id=1, source_target_pairs={{0,1},{1,0},{2,3},{3,2},{4,5},{5,4},{6,7},{7,6},{8,9},{9,8},{10,11... | collective-permute-start | bytes 12582920 | tf_op jit(solution)/shard_map/ppermute | solution.py:39
  3.2 5.2 %collective-permute-start = (bf16[8,4096]{1,0:T(8,128)(2,1)}, bf16[8,4096]{1,0:T(8,128)(2,1)S(1)}, u32[]{:S(2)}, u32[]{:S(2)}) collective-permute-start(bf16[8,4096]{1,0:T(8,128)(2,1)} %bitcast.17), channel_id=1, source_target_pairs={{0,8},{1,9},{2,10},{3,11},{4,12},{5,13},{6,14},{7,15},{8,0},{9,1},... | collective-permute-start | bytes 196616 | tf_op jit(solution)/shard_map/ppermute | solution.py:56
  8.4 0.9 fusion.12
  9.3 1.1 %constant_dynamic-update-slice_fusion.4 = bf16[64,4096]{1,0:T(8,128)(2,1)S(1)} fusion(bf16[1,8,4096]{2,1,0:T(8,128)(2,1)} %param.8), kind=kLoop, calls=%fused_computation.5 | loop fusion | bytes 131072
  10.4 0.7 multiply_add_fusion
  11.1 0.9 pad_maximum_fusion
  12.0 4.3 %collective-permute-start.1 = (bf16[16,4096]{1,0:T(8,128)(2,1)S(1)}, bf16[16,4096]{1,0:T(8,128)(2,1)S(1)}, u32[]{:S(2)}, u32[]{:S(2)}) collective-permute-start(bf16[16,4096]{1,0:T(8,128)(2,1)S(1)} %pad_maximum_fusion), channel_id=1, source_target_pairs={{0,128},{1,13},{2,130},{3,15},{4,132},{5,1},{6,134},{7,3},{8,136},... | collective-permute-start | bytes 393224 | tf_op jit(solution)/shard_map/ppermute | solution.py:56
  16.3 0.7 collective-permute-start.3
  17.0 0.7 collective-permute-start.4
  17.8 3.8 %collective-permute-done.3 = bf16[16,4096]{1,0:T(8,128)(2,1)S(1)} collective-permute-done((bf16[16,4096]{1,0:T(8,128)(2,1)S(1)}, bf16[16,4096]{1,0:T(8,128)(2,1)S(1)}, u32[]{:S(2)}, u32[]{:S(2)}) %collective-permute-start.3) | collective-permute-done | bytes 131104 | tf_op jit(solution)/shard_map/ppermute | solution.py:56
  21.6 0.7 collective-permute-done.4
  22.4 1.7 %collective-permute-start.9 = (bf16[64,4096]{1,0:T(8,128)(2,1)S(1)}, bf16[64,4096]{1,0:T(8,128)(2,1)S(1)}, u32[]{:S(2)}, u32[]{:S(2)}) collective-permute-start(bf16[64,4096]{1,0:T(8,128)(2,1)S(1)} %constant_dynamic-update-slice_fusion.refs_0_), channel_id=1, source_target_pairs={{0,32},{1,33},{2,34},{3,35},{4,36},{5,37},{6,38},{7,39},{8,40},{9,... | collective-permute-start | bytes 1572872 | tf_op jit(solution)/shard_map/ppermute | solution.py:56
  24.1 1.5 %collective-permute-start.5 = (bf16[64,4096]{1,0:T(8,128)(2,1)S(1)}, bf16[64,4096]{1,0:T(8,128)(2,1)S(1)}, u32[]{:S(2)}, u32[]{:S(2)}) collective-permute-start(bf16[64,4096]{1,0:T(8,128)(2,1)S(1)} %constant_dynamic-update-slice_fusion.refs_0_), channel_id=1, source_target_pairs={{0,96},{1,97},{2,98},{3,99},{4,100},{5,101},{6,102},{7,103},{8,104... | collective-permute-start | bytes 1572872 | tf_op jit(solution)/shard_map/ppermute | solution.py:56
  25.6 2.5 %collective-permute-start.6 = (bf16[64,4096]{1,0:T(8,128)(2,1)S(1)}, bf16[64,4096]{1,0:T(8,128)(2,1)S(1)}, u32[]{:S(2)}, u32[]{:S(2)}) collective-permute-start(bf16[64,4096]{1,0:T(8,128)(2,1)S(1)} %constant_dynamic-update-slice_fusion.refs_0_), channel_id=1, source_target_pairs={{0,14},{1,145},{2,0},{3,147},{4,2},{5,149},{6,4},{7,151},{8,6},{9,... | collective-permute-start | bytes 1572872 | tf_op jit(solution)/shard_map/ppermute | solution.py:56
  28.1 0.0 collective-permute-start.7
  28.1 9.2 %collective-permute-done.9 = bf16[64,4096]{1,0:T(8,128)(2,1)S(1)} collective-permute-done((bf16[64,4096]{1,0:T(8,128)(2,1)S(1)}, bf16[64,4096]{1,0:T(8,128)(2,1)S(1)}, u32[]{:S(2)}, u32[]{:S(2)}) %collective-permute-start.9) | collective-permute-done | bytes 524320 | tf_op jit(solution)/shard_map/ppermute | solution.py:56
  37.2 1.1 %collective-permute-start.2 = (f32[1,512]{1,0:T(1,128)S(1)}, f32[1,512]{1,0:T(1,128)S(1)}, u32[]{:S(2)}, u32[]{:S(2)}) collective-permute-start(f32[1,512]{1,0:T(1,128)S(1)} %bitcast.11), channel_id=1, source_target_pairs={{0,1},{1,0},{2,3},{3,2},{4,5},{5,4},{6,7},{7,6},{8,9},{9,8},{10,11... | collective-permute-start | bytes 6152 | tf_op jit(solution)/shard_map/ppermute | solution.py:39
  38.4 0.1 collective-permute-start.11
  38.5 0.0 collective-permute-done.6.refs_1_
  38.5 0.0 collective-permute-done.7.refs_2_
  38.5 0.0 collective-permute-done.8.other_ref
  38.6 2.7 %collective-permute-start.10 = (bf16[32,4096]{1,0:T(8,128)(2,1)S(1)}, bf16[32,4096]{1,0:T(8,128)(2,1)S(1)}, u32[]{:S(2)}, u32[]{:S(2)}) collective-permute-start(bf16[32,4096]{1,0:T(8,128)(2,1)S(1)} %slice.12), channel_id=1, source_target_pairs={{0,96},{1,97},{2,98},{3,99},{4,100},{5,101},{6,102},{7,103},{8,104... | collective-permute-start | bytes 786440 | tf_op jit(solution)/shard_map/ppermute | solution.py:56
  41.3 0.0 collective-permute-start.12
  41.4 2.7 %collective-permute-start.19 = (bf16[128,4096]{1,0:T(8,128)(2,1)S(1)}, bf16[128,4096]{1,0:T(8,128)(2,1)S(1)}, u32[]{:S(2)}, u32[]{:S(2)}) collective-permute-start(bf16[128,4096]{1,0:T(8,128)(2,1)S(1)} %constant_dynamic-update-slice_fusion.5.refs_1_), channel_id=1, source_target_pairs={{0,14},{1,145},{2,0},{3,147},{4,2},{5,149},{6,4},{7,151},{8,6},{9,... | collective-permute-start | bytes 3145736 | tf_op jit(solution)/shard_map/ppermute | solution.py:56
  44.1 0.0 collective-permute-start.20
  44.1 5.2 %score.3 = (f32[8,512]{1,0:T(8,128)S(1)}, f32[8,512]{1,0:T(8,128)S(1)}, bf16[512,4096]{1,0:T(8,128)(2,1)S(1)}) custom-call(f32[1,1152]{1,0:T(1,128)S(1)} %broadcast_in_dim.13.ids_ref, f32[1,512]{1,0:T(1,128)S(1)} %bitcast.12, f32[1,512]{1,0:T(1,128)S(1)} %collective-permute-done.2.other_wanted_ref, bf16[512,4096]{1,0:T(8,128)(2,1)S(1)} %copy-done, ...), custom_call_target="tpu_custom_call" | custom-call | flops 1610612736 | bytes 1572864 | tf_op jit(solution)/shard_map/score/pallas_call | solution.py:172
  49.3 0.0 collective-permute-done.11
  49.3 0.0 collective-permute-done.10
  49.3 1.5 %collective-permute-done.12.refs_3_ = bf16[64,4096]{1,0:T(8,128)(2,1)S(1)} collective-permute-done((bf16[64,4096]{1,0:T(8,128)(2,1)S(1)}, bf16[64,4096]{1,0:T(8,128)(2,1)S(1)}, u32[]{:S(2)}, u32[]{:S(2)}) %collective-permute-start.12) | collective-permute-done | bytes 524320 | tf_op jit(solution)/shard_map/ppermute | solution.py:56
  50.9 0.2 collective-permute-start.15
  51.1 1.2 %collective-permute-start.16 = (bf16[64,4096]{1,0:T(8,128)(2,1)S(1)}, bf16[64,4096]{1,0:T(8,128)(2,1)S(1)}, u32[]{:S(2)}, u32[]{:S(2)}) collective-permute-start(bf16[64,4096]{1,0:T(8,128)(2,1)S(1)} %collective-permute-done.12.refs_3_), channel_id=1, source_target_pairs={{0,32},{1,33},{2,34},{3,35},{4,36},{5,37},{6,38},{7,39},{8,40},{9,... | collective-permute-start | bytes 1572872 | tf_op jit(solution)/shard_map/ppermute | solution.py:56
  52.4 1.3 %collective-permute-start.13 = (bf16[64,4096]{1,0:T(8,128)(2,1)S(1)}, bf16[64,4096]{1,0:T(8,128)(2,1)S(1)}, u32[]{:S(2)}, u32[]{:S(2)}) collective-permute-start(bf16[64,4096]{1,0:T(8,128)(2,1)S(1)} %constant_dynamic-update-slice_fusion.7.refs_0_), channel_id=1, source_target_pairs={{0,14},{1,145},{2,0},{3,147},{4,2},{5,149},{6,4},{7,151},{8,6},{9,... | collective-permute-start | bytes 1572872 | tf_op jit(solution)/shard_map/ppermute | solution.py:56
  53.7 7.8 %collective-permute-done.15.refs_2_ = bf16[64,4096]{1,0:T(8,128)(2,1)S(1)} collective-permute-done((bf16[64,4096]{1,0:T(8,128)(2,1)S(1)}, bf16[64,4096]{1,0:T(8,128)(2,1)S(1)}, u32[]{:S(2)}, u32[]{:S(2)}) %collective-permute-start.15) | collective-permute-done | bytes 524320 | tf_op jit(solution)/shard_map/ppermute | solution.py:56
  61.5 0.9 collective-permute-done.16.refs_3_
  62.5 0.4 collective-permute-start.17
  62.9 0.0 collective-permute-done.19.refs_4_
  62.9 1.4 %collective-permute-start.18 = (bf16[32,4096]{1,0:T(8,128)(2,1)S(1)}, bf16[32,4096]{1,0:T(8,128)(2,1)S(1)}, u32[]{:S(2)}, u32[]{:S(2)}) collective-permute-start(bf16[32,4096]{1,0:T(8,128)(2,1)S(1)} %slice.18), channel_id=1, source_target_pairs={{0,32},{1,33},{2,34},{3,35},{4,36},{5,37},{6,38},{7,39},{8,40},{9,... | collective-permute-start | bytes 786440 | tf_op jit(solution)/shard_map/ppermute | solution.py:56
  64.3 0.0 collective-permute-done.20.refs_5_
  64.3 5.1 %score.4 = (f32[8,512]{1,0:T(8,128)S(1)}, f32[8,512]{1,0:T(8,128)S(1)}) custom-call(f32[1,1152]{1,0:T(1,128)S(1)} %broadcast_in_dim.13.ids_ref, f32[1,512]{1,0:T(1,128)S(1)} %bitcast.13, f32[1,512]{1,0:T(1,128)S(1)} %collective-permute-done.2.other_wanted_ref, bf16[512,4096]{1,0:T(8,128)(2,1)S(1)} %copy-done, ...), custom_call_target="tpu_custom_call" | custom-call | flops 4294967296 | bytes 4194304 | tf_op jit(solution)/shard_map/score/pallas_call | solution.py:172
  69.3 0.0 collective-permute-done.13.refs_0_
  69.3 1.7 %collective-permute-done.14.refs_1_ = bf16[64,4096]{1,0:T(8,128)(2,1)S(1)} collective-permute-done((bf16[64,4096]{1,0:T(8,128)(2,1)S(1)}, bf16[64,4096]{1,0:T(8,128)(2,1)S(1)}, u32[]{:S(2)}, u32[]{:S(2)}) %collective-permute-start.14) | collective-permute-done | bytes 524320 | tf_op jit(solution)/shard_map/ppermute | solution.py:56
  71.0 3.2 %score.5 = (f32[8,512]{1,0:T(8,128)S(1)}, f32[8,512]{1,0:T(8,128)S(1)}) custom-call(f32[1,1152]{1,0:T(1,128)S(1)} %broadcast_in_dim.13.ids_ref, f32[1,512]{1,0:T(1,128)S(1)} %bitcast.14, f32[1,512]{1,0:T(1,128)S(1)} %collective-permute-done.2.other_wanted_ref, bf16[512,4096]{1,0:T(8,128)(2,1)S(1)} %copy-done, ...), custom_call_target="tpu_custom_call" | custom-call | flops 2684354560 | bytes 2621440 | tf_op jit(solution)/shard_map/score/pallas_call | solution.py:172
  74.3 4.7 %collective-permute-start.21 = (f32[8,512]{1,0:T(8,128)S(1)}, f32[8,512]{1,0:T(8,128)S(1)}, u32[]{:S(2)}, u32[]{:S(2)}) collective-permute-start(f32[8,512]{1,0:T(8,128)S(1)} %get-tuple-element.44), channel_id=1, source_target_pairs={{0,1},{1,0},{2,3},{3,2},{4,5},{5,4},{6,7},{7,6},{8,9},{9,8},{10,11... | collective-permute-start | bytes 49160 | tf_op jit(solution)/shard_map/ppermute | solution.py:39
  78.9 0.8 collective-permute-done.21.got_ref
  79.8 1.0 class_sums.1
  80.8 20.5 %all_to_all.9 = f32[256,1,128]{2,1,0:T(1,128)S(1)} all-to-all(f32[256,1,128]{2,1,0:T(1,128)S(1)} %bitcast.10), channel_id=1, replica_groups=mesh['xh'=2,'y'=4,'xl'=2,'z'=8,'core'=2] {'xh','y','xl','z','core'}, dimensions={0} | all-to-all | bytes 262144 | tf_op jit(solution)/shard_map/all_to_all | solution.py:278
  101.3 0.3 reduce_sum.9
  101.6 0.5 multiply_bitcast_fusion
  (24 shorter events, 0.2 us)
Async XLA Ops:
  0.0 38.5 %collective-permute-start.8 = (bf16[512,4096]{1,0:T(8,128)(2,1)}, bf16[512,4096]{1,0:T(8,128)(2,1)}, u32[]{:S(2)}, u32[]{:S(2)}) collective-permute-start(bf16[512,4096]{1,0:T(8,128)(2,1)} %particles_ref.1), channel_id=1, source_target_pairs={{0,1},{1,0},{2,3},{3,2},{4,5},{5,4},{6,7},{7,6},{8,9},{9,8},{10,11... | collective-permute-start | bytes 12582920 | tf_op jit(solution)/shard_map/ppermute | solution.py:39
  3.2 7.9 %collective-permute-start = (bf16[8,4096]{1,0:T(8,128)(2,1)}, bf16[8,4096]{1,0:T(8,128)(2,1)S(1)}, u32[]{:S(2)}, u32[]{:S(2)}) collective-permute-start(bf16[8,4096]{1,0:T(8,128)(2,1)} %bitcast.17), channel_id=1, source_target_pairs={{0,8},{1,9},{2,10},{3,11},{4,12},{5,13},{6,14},{7,15},{8,0},{9,1},... | collective-permute-start | bytes 196616 | tf_op jit(solution)/shard_map/ppermute | solution.py:56
  8.4 35.7 %copy-start = (bf16[512,4096]{1,0:T(8,128)(2,1)S(1)}, bf16[512,4096]{1,0:T(8,128)(2,1)}, u32[]{:S(2)}) copy-start(bf16[512,4096]{1,0:T(8,128)(2,1)} %particles_ref.1) | copy-start | bytes 12582916
  12.0 9.6 %collective-permute-start.1 = (bf16[16,4096]{1,0:T(8,128)(2,1)S(1)}, bf16[16,4096]{1,0:T(8,128)(2,1)S(1)}, u32[]{:S(2)}, u32[]{:S(2)}) collective-permute-start(bf16[16,4096]{1,0:T(8,128)(2,1)S(1)} %pad_maximum_fusion), channel_id=1, source_target_pairs={{0,128},{1,13},{2,130},{3,15},{4,132},{5,1},{6,134},{7,3},{8,136},... | collective-permute-start | bytes 393224 | tf_op jit(solution)/shard_map/ppermute | solution.py:56
  16.3 5.3 %collective-permute-start.3 = (bf16[16,4096]{1,0:T(8,128)(2,1)S(1)}, bf16[16,4096]{1,0:T(8,128)(2,1)S(1)}, u32[]{:S(2)}, u32[]{:S(2)}) collective-permute-start(bf16[16,4096]{1,0:T(8,128)(2,1)S(1)} %pad_maximum_fusion), channel_id=1, source_target_pairs={{0,144},{1,15},{2,146},{3,1},{4,148},{5,3},{6,150},{7,5},{8,152},{... | collective-permute-start | bytes 393224 | tf_op jit(solution)/shard_map/ppermute | solution.py:56
  17.0 5.3 %collective-permute-start.4 = (bf16[16,4096]{1,0:T(8,128)(2,1)S(1)}, bf16[16,4096]{1,0:T(8,128)(2,1)S(1)}, u32[]{:S(2)}, u32[]{:S(2)}) collective-permute-start(bf16[16,4096]{1,0:T(8,128)(2,1)S(1)} %pad_maximum_fusion), channel_id=1, source_target_pairs={{0,16},{1,3},{2,18},{3,5},{4,20},{5,7},{6,22},{7,9},{8,24},{9,11},... | collective-permute-start | bytes 393224 | tf_op jit(solution)/shard_map/ppermute | solution.py:56
  22.4 14.8 %collective-permute-start.9 = (bf16[64,4096]{1,0:T(8,128)(2,1)S(1)}, bf16[64,4096]{1,0:T(8,128)(2,1)S(1)}, u32[]{:S(2)}, u32[]{:S(2)}) collective-permute-start(bf16[64,4096]{1,0:T(8,128)(2,1)S(1)} %constant_dynamic-update-slice_fusion.refs_0_), channel_id=1, source_target_pairs={{0,32},{1,33},{2,34},{3,35},{4,36},{5,37},{6,38},{7,39},{8,40},{9,... | collective-permute-start | bytes 1572872 | tf_op jit(solution)/shard_map/ppermute | solution.py:56
  24.1 14.3 %collective-permute-start.5 = (bf16[64,4096]{1,0:T(8,128)(2,1)S(1)}, bf16[64,4096]{1,0:T(8,128)(2,1)S(1)}, u32[]{:S(2)}, u32[]{:S(2)}) collective-permute-start(bf16[64,4096]{1,0:T(8,128)(2,1)S(1)} %constant_dynamic-update-slice_fusion.refs_0_), channel_id=1, source_target_pairs={{0,96},{1,97},{2,98},{3,99},{4,100},{5,101},{6,102},{7,103},{8,104... | collective-permute-start | bytes 1572872 | tf_op jit(solution)/shard_map/ppermute | solution.py:56
  25.6 12.9 %collective-permute-start.6 = (bf16[64,4096]{1,0:T(8,128)(2,1)S(1)}, bf16[64,4096]{1,0:T(8,128)(2,1)S(1)}, u32[]{:S(2)}, u32[]{:S(2)}) collective-permute-start(bf16[64,4096]{1,0:T(8,128)(2,1)S(1)} %constant_dynamic-update-slice_fusion.refs_0_), channel_id=1, source_target_pairs={{0,14},{1,145},{2,0},{3,147},{4,2},{5,149},{6,4},{7,151},{8,6},{9,... | collective-permute-start | bytes 1572872 | tf_op jit(solution)/shard_map/ppermute | solution.py:56
  28.1 10.4 %collective-permute-start.7 = (bf16[64,4096]{1,0:T(8,128)(2,1)S(1)}, bf16[64,4096]{1,0:T(8,128)(2,1)S(1)}, u32[]{:S(2)}, u32[]{:S(2)}) collective-permute-start(bf16[64,4096]{1,0:T(8,128)(2,1)S(1)} %constant_dynamic-update-slice_fusion.refs_0_), channel_id=1, source_target_pairs={{0,2},{1,17},{2,4},{3,19},{4,6},{5,21},{6,8},{7,23},{8,10},{9,25},... | collective-permute-start | bytes 1572872 | tf_op jit(solution)/shard_map/ppermute | solution.py:56
  37.2 6.9 %collective-permute-start.2 = (f32[1,512]{1,0:T(1,128)S(1)}, f32[1,512]{1,0:T(1,128)S(1)}, u32[]{:S(2)}, u32[]{:S(2)}) collective-permute-start(f32[1,512]{1,0:T(1,128)S(1)} %bitcast.11), channel_id=1, source_target_pairs={{0,1},{1,0},{2,3},{3,2},{4,5},{5,4},{6,7},{7,6},{8,9},{9,8},{10,11... | collective-permute-start | bytes 6152 | tf_op jit(solution)/shard_map/ppermute | solution.py:39
  38.4 10.9 %collective-permute-start.11 = (bf16[32,4096]{1,0:T(8,128)(2,1)S(1)}, bf16[32,4096]{1,0:T(8,128)(2,1)S(1)}, u32[]{:S(2)}, u32[]{:S(2)}) collective-permute-start(bf16[32,4096]{1,0:T(8,128)(2,1)S(1)} %slice.16), channel_id=1, source_target_pairs={{0,32},{1,33},{2,34},{3,35},{4,36},{5,37},{6,38},{7,39},{8,40},{9,... | collective-permute-start | bytes 786440 | tf_op jit(solution)/shard_map/ppermute | solution.py:56
  38.6 10.7 %collective-permute-start.10 = (bf16[32,4096]{1,0:T(8,128)(2,1)S(1)}, bf16[32,4096]{1,0:T(8,128)(2,1)S(1)}, u32[]{:S(2)}, u32[]{:S(2)}) collective-permute-start(bf16[32,4096]{1,0:T(8,128)(2,1)S(1)} %slice.12), channel_id=1, source_target_pairs={{0,96},{1,97},{2,98},{3,99},{4,100},{5,101},{6,102},{7,103},{8,104... | collective-permute-start | bytes 786440 | tf_op jit(solution)/shard_map/ppermute | solution.py:56
  41.3 9.5 %collective-permute-start.12 = (bf16[64,4096]{1,0:T(8,128)(2,1)S(1)}, bf16[64,4096]{1,0:T(8,128)(2,1)S(1)}, u32[]{:S(2)}, u32[]{:S(2)}) collective-permute-start(bf16[64,4096]{1,0:T(8,128)(2,1)S(1)} %collective-permute-done.7.refs_2_), channel_id=1, source_target_pairs={{0,2},{1,17},{2,4},{3,19},{4,6},{5,21},{6,8},{7,23},{8,10},{9,25},... | collective-permute-start | bytes 1572872 | tf_op jit(solution)/shard_map/ppermute | solution.py:56
  41.4 21.5 %collective-permute-start.19 = (bf16[128,4096]{1,0:T(8,128)(2,1)S(1)}, bf16[128,4096]{1,0:T(8,128)(2,1)S(1)}, u32[]{:S(2)}, u32[]{:S(2)}) collective-permute-start(bf16[128,4096]{1,0:T(8,128)(2,1)S(1)} %constant_dynamic-update-slice_fusion.5.refs_1_), channel_id=1, source_target_pairs={{0,14},{1,145},{2,0},{3,147},{4,2},{5,149},{6,4},{7,151},{8,6},{9,... | collective-permute-start | bytes 3145736 | tf_op jit(solution)/shard_map/ppermute | solution.py:56
  44.1 20.1 %collective-permute-start.20 = (bf16[128,4096]{1,0:T(8,128)(2,1)S(1)}, bf16[128,4096]{1,0:T(8,128)(2,1)S(1)}, u32[]{:S(2)}, u32[]{:S(2)}) collective-permute-start(bf16[128,4096]{1,0:T(8,128)(2,1)S(1)} %constant_dynamic-update-slice_fusion.5.refs_1_), channel_id=1, source_target_pairs={{0,2},{1,17},{2,4},{3,19},{4,6},{5,21},{6,8},{7,23},{8,10},{9,25},... | collective-permute-start | bytes 3145736 | tf_op jit(solution)/shard_map/ppermute | solution.py:56
  50.9 10.6 %collective-permute-start.15 = (bf16[64,4096]{1,0:T(8,128)(2,1)S(1)}, bf16[64,4096]{1,0:T(8,128)(2,1)S(1)}, u32[]{:S(2)}, u32[]{:S(2)}) collective-permute-start(bf16[64,4096]{1,0:T(8,128)(2,1)S(1)} %collective-permute-done.12.refs_3_), channel_id=1, source_target_pairs={{0,96},{1,97},{2,98},{3,99},{4,100},{5,101},{6,102},{7,103},{8,104... | collective-permute-start | bytes 1572872 | tf_op jit(solution)/shard_map/ppermute | solution.py:56
  51.1 11.3 %collective-permute-start.16 = (bf16[64,4096]{1,0:T(8,128)(2,1)S(1)}, bf16[64,4096]{1,0:T(8,128)(2,1)S(1)}, u32[]{:S(2)}, u32[]{:S(2)}) collective-permute-start(bf16[64,4096]{1,0:T(8,128)(2,1)S(1)} %collective-permute-done.12.refs_3_), channel_id=1, source_target_pairs={{0,32},{1,33},{2,34},{3,35},{4,36},{5,37},{6,38},{7,39},{8,40},{9,... | collective-permute-start | bytes 1572872 | tf_op jit(solution)/shard_map/ppermute | solution.py:56
  52.4 17.0 %collective-permute-start.13 = (bf16[64,4096]{1,0:T(8,128)(2,1)S(1)}, bf16[64,4096]{1,0:T(8,128)(2,1)S(1)}, u32[]{:S(2)}, u32[]{:S(2)}) collective-permute-start(bf16[64,4096]{1,0:T(8,128)(2,1)S(1)} %constant_dynamic-update-slice_fusion.7.refs_0_), channel_id=1, source_target_pairs={{0,14},{1,145},{2,0},{3,147},{4,2},{5,149},{6,4},{7,151},{8,6},{9,... | collective-permute-start | bytes 1572872 | tf_op jit(solution)/shard_map/ppermute | solution.py:56
  61.5 9.5 %collective-permute-start.14 = (bf16[64,4096]{1,0:T(8,128)(2,1)S(1)}, bf16[64,4096]{1,0:T(8,128)(2,1)S(1)}, u32[]{:S(2)}, u32[]{:S(2)}) collective-permute-start(bf16[64,4096]{1,0:T(8,128)(2,1)S(1)} %constant_dynamic-update-slice_fusion.7.refs_0_), channel_id=1, source_target_pairs={{0,2},{1,17},{2,4},{3,19},{4,6},{5,21},{6,8},{7,23},{8,10},{9,25},... | collective-permute-start | bytes 1572872 | tf_op jit(solution)/shard_map/ppermute | solution.py:56
  62.5 8.6 %collective-permute-start.17 = (bf16[32,4096]{1,0:T(8,128)(2,1)S(1)}, bf16[32,4096]{1,0:T(8,128)(2,1)S(1)}, u32[]{:S(2)}, u32[]{:S(2)}) collective-permute-start(bf16[32,4096]{1,0:T(8,128)(2,1)S(1)} %slice.17), channel_id=1, source_target_pairs={{0,96},{1,97},{2,98},{3,99},{4,100},{5,101},{6,102},{7,103},{8,104... | collective-permute-start | bytes 786440 | tf_op jit(solution)/shard_map/ppermute | solution.py:56
  62.9 8.2 %collective-permute-start.18 = (bf16[32,4096]{1,0:T(8,128)(2,1)S(1)}, bf16[32,4096]{1,0:T(8,128)(2,1)S(1)}, u32[]{:S(2)}, u32[]{:S(2)}) collective-permute-start(bf16[32,4096]{1,0:T(8,128)(2,1)S(1)} %slice.18), channel_id=1, source_target_pairs={{0,32},{1,33},{2,34},{3,35},{4,36},{5,37},{6,38},{7,39},{8,40},{9,... | collective-permute-start | bytes 786440 | tf_op jit(solution)/shard_map/ppermute | solution.py:56
  71.0 8.7 %copy-start.1 = (f32[512]{0:T(512)S(1)}, f32[512]{0:T(512)}, u32[]{:S(2)}) copy-start(f32[512]{0:T(512)} %param.13) | copy-start | bytes 6148
  74.3 5.5 %collective-permute-start.21 = (f32[8,512]{1,0:T(8,128)S(1)}, f32[8,512]{1,0:T(8,128)S(1)}, u32[]{:S(2)}, u32[]{:S(2)}) collective-permute-start(f32[8,512]{1,0:T(8,128)S(1)} %get-tuple-element.44), channel_id=1, source_target_pairs={{0,1},{1,0},{2,3},{3,2},{4,5},{5,4},{6,7},{7,6},{8,9},{9,8},{10,11... | collective-permute-start | bytes 49160 | tf_op jit(solution)/shard_map/ppermute | solution.py:39

commit v9 on v8

--- a/solution.py
+++ b/solution.py
@@ -17,7 +17,7 @@
 ALL = ("xh", "y", "xl", "z", "core")
 AX, AY, AZ = 0, 1, 2
 SIZES = (XN, YN, ZN)
-STAGES = ((AX, AZ), (AY, AY), (AZ, AX))
+STAGES = ((AY, AX), (AZ, AZ), (AX, AY))
 
 
 def flat_device(x, y, z, core):

time: 102 us -> 104 us (1.020)
  waiting for transfers between devices: 26.5 us -> 22.7 us
  starting transfers between devices: 35.8 us -> 39.5 us
  blocking collectives: 20.5 us -> 22.5 us
    ppermute x19, waiting for transfers between devices: 25.7 us -> 21.8 us  [fetch(): lax.ppermute(self.rows, ALL, pairs(move))]
    ppermute x3, starting transfers between devices: 9.04 us -> 11.8 us  [swap_cores(): return lax.ppermute(value, ALL, pairs(lambda at, core: (at, 1 - core)))]
    all_to_all x1, blocking collectives: 20.5 us -> 22.5 us  [body(): lax.all_to_all(sent, ALL, 0, 0, tiled=True)]
  transfers between devices with their start and end apart: 22 -> 22, of which waited for: 8 -> 7; matrix products, arithmetic and copies ran while one was open for 4% -> 4% of each run, Pallas kernels for 10% -> 10%
where the time goes in v9:
time: 104 us
  starting transfers between devices  39.5 us (38%)
  waiting for transfers between devices  22.7 us (22%)
  blocking collectives  22.5 us (22%)
  Pallas kernels  14.5 us (14%)
  other arithmetic  3.28 us (3%)
  local copies, waits for them, and re-layouts  1.29 us (1%)
    ppermute x19, starting transfers between devices, fetch(): lax.ppermute(self.rows, ALL, pairs(move))  27.7 us
    all_to_all x1, blocking collectives, body(): lax.all_to_all(sent, ALL, 0, 0, tiled=True)  22.5 us
    ppermute x19, waiting for transfers between devices, fetch(): lax.ppermute(self.rows, ALL, pairs(move))  21.8 us
    pallas_call x3, Pallas kernels, score(): pl.pallas_call(functools.partial(score_kernel, scale, len(pieces), first,...  13.5 us
    ppermute x3, starting transfers between devices, swap_cores(): return lax.ppermute(value, ALL, pairs(lambda at, core: (at, 1 - core)))  11.8 us
  transfers between devices with their start and end apart: 22, of which 7 were waited for; matrix products, arithmetic and copies ran while one was open for 4% of the time, Pallas kernels for 10%

profile of v9, /device:TPU:1, one launch (start us, length us, event | category | flops | bytes accessed | tf_op | source)
XLA Modules:
  0.0 103.9 jit_solution(11053720695572024914)
XLA Ops:
  0.0 3.2 %collective-permute-start.8 = (bf16[512,4096]{1,0:T(8,128)(2,1)}, bf16[512,4096]{1,0:T(8,128)(2,1)}, u32[]{:S(2)}, u32[]{:S(2)}) collective-permute-start(bf16[512,4096]{1,0:T(8,128)(2,1)} %particles_ref.1), channel_id=1, source_target_pairs={{0,1},{1,0},{2,3},{3,2},{4,5},{5,4},{6,7},{7,6},{8,9},{9,8},{10,11... | collective-permute-start | bytes 12582920 | tf_op jit(solution)/shard_map/ppermute | solution.py:39
  3.2 5.2 %collective-permute-start = (bf16[8,4096]{1,0:T(8,128)(2,1)}, bf16[8,4096]{1,0:T(8,128)(2,1)S(1)}, u32[]{:S(2)}, u32[]{:S(2)}) collective-permute-start(bf16[8,4096]{1,0:T(8,128)(2,1)} %bitcast.17), channel_id=1, source_target_pairs={{0,8},{1,9},{2,10},{3,11},{4,12},{5,13},{6,14},{7,15},{8,0},{9,1},... | collective-permute-start | bytes 196616 | tf_op jit(solution)/shard_map/ppermute | solution.py:56
  8.4 0.9 fusion.12
  9.3 1.1 %constant_dynamic-update-slice_fusion.4 = bf16[64,4096]{1,0:T(8,128)(2,1)S(1)} fusion(bf16[1,8,4096]{2,1,0:T(8,128)(2,1)} %param.8), kind=kLoop, calls=%fused_computation.5 | loop fusion | bytes 131072
  10.4 0.7 multiply_add_fusion
  11.1 0.0 collective-permute-done
  11.1 0.9 pad_maximum_fusion
  12.0 2.8 %collective-permute-start.1 = (bf16[16,4096]{1,0:T(8,128)(2,1)S(1)}, bf16[16,4096]{1,0:T(8,128)(2,1)S(1)}, u32[]{:S(2)}, u32[]{:S(2)}) collective-permute-start(bf16[16,4096]{1,0:T(8,128)(2,1)S(1)} %pad_maximum_fusion), channel_id=1, source_target_pairs={{0,64},{1,129},{2,66},{3,131},{4,68},{5,133},{6,70},{7,135},{8,72}... | collective-permute-start | bytes 393224 | tf_op jit(solution)/shard_map/ppermute | solution.py:56
  14.8 0.9 collective-permute-start.3
  15.7 0.6 collective-permute-start.4
  16.3 2.9 %collective-permute-done.3 = bf16[16,4096]{1,0:T(8,128)(2,1)S(1)} collective-permute-done((bf16[16,4096]{1,0:T(8,128)(2,1)S(1)}, bf16[16,4096]{1,0:T(8,128)(2,1)S(1)}, u32[]{:S(2)}, u32[]{:S(2)}) %collective-permute-start.3) | collective-permute-done | bytes 131104 | tf_op jit(solution)/shard_map/ppermute | solution.py:56
  19.2 0.0 collective-permute-done.1
  19.2 1.5 %collective-permute-done.4 = bf16[16,4096]{1,0:T(8,128)(2,1)S(1)} collective-permute-done((bf16[16,4096]{1,0:T(8,128)(2,1)S(1)}, bf16[16,4096]{1,0:T(8,128)(2,1)S(1)}, u32[]{:S(2)}, u32[]{:S(2)}) %collective-permute-start.4) | collective-permute-done | bytes 131104 | tf_op jit(solution)/shard_map/ppermute | solution.py:56
  20.7 0.8 collective-permute-start.9
  21.5 3.5 %collective-permute-start.5 = (bf16[64,4096]{1,0:T(8,128)(2,1)S(1)}, bf16[64,4096]{1,0:T(8,128)(2,1)S(1)}, u32[]{:S(2)}, u32[]{:S(2)}) collective-permute-start(bf16[64,4096]{1,0:T(8,128)(2,1)S(1)} %constant_dynamic-update-slice_fusion.refs_0_), channel_id=1, source_target_pairs={{0,14},{1,15},{2,0},{3,1},{4,2},{5,3},{6,4},{7,5},{8,6},{9,7},{10,... | collective-permute-start | bytes 1572872 | tf_op jit(solution)/shard_map/ppermute | solution.py:56
  25.0 2.7 %collective-permute-start.6 = (bf16[64,4096]{1,0:T(8,128)(2,1)S(1)}, bf16[64,4096]{1,0:T(8,128)(2,1)S(1)}, u32[]{:S(2)}, u32[]{:S(2)}) collective-permute-start(bf16[64,4096]{1,0:T(8,128)(2,1)S(1)} %constant_dynamic-update-slice_fusion.refs_0_), channel_id=1, source_target_pairs={{0,144},{1,97},{2,146},{3,99},{4,148},{5,101},{6,150},{7,103},{8,1... | collective-permute-start | bytes 1572872 | tf_op jit(solution)/shard_map/ppermute | solution.py:56
  27.8 0.0 collective-permute-start.7
  27.8 6.9 %collective-permute-done.9 = bf16[64,4096]{1,0:T(8,128)(2,1)S(1)} collective-permute-done((bf16[64,4096]{1,0:T(8,128)(2,1)S(1)}, bf16[64,4096]{1,0:T(8,128)(2,1)S(1)}, u32[]{:S(2)}, u32[]{:S(2)}) %collective-permute-start.9) | collective-permute-done | bytes 524320 | tf_op jit(solution)/shard_map/ppermute | solution.py:56
  34.6 3.2 %collective-permute-start.2 = (f32[1,512]{1,0:T(1,128)S(1)}, f32[1,512]{1,0:T(1,128)S(1)}, u32[]{:S(2)}, u32[]{:S(2)}) collective-permute-start(f32[1,512]{1,0:T(1,128)S(1)} %bitcast.11), channel_id=1, source_target_pairs={{0,1},{1,0},{2,3},{3,2},{4,5},{5,4},{6,7},{7,6},{8,9},{9,8},{10,11... | collective-permute-start | bytes 6152 | tf_op jit(solution)/shard_map/ppermute | solution.py:39
  37.9 0.1 collective-permute-start.11
  38.0 0.0 collective-permute-done.6.refs_1_
  38.0 0.0 collective-permute-done.7.refs_2_
  38.1 2.7 %collective-permute-start.10 = (bf16[32,4096]{1,0:T(8,128)(2,1)S(1)}, bf16[32,4096]{1,0:T(8,128)(2,1)S(1)}, u32[]{:S(2)}, u32[]{:S(2)}) collective-permute-start(bf16[32,4096]{1,0:T(8,128)(2,1)S(1)} %slice.12), channel_id=1, source_target_pairs={{0,14},{1,15},{2,0},{3,1},{4,2},{5,3},{6,4},{7,5},{8,6},{9,7},{10,... | collective-permute-start | bytes 786440 | tf_op jit(solution)/shard_map/ppermute | solution.py:56
  40.8 1.3 %collective-permute-start.12 = (bf16[64,4096]{1,0:T(8,128)(2,1)S(1)}, bf16[64,4096]{1,0:T(8,128)(2,1)S(1)}, u32[]{:S(2)}, u32[]{:S(2)}) collective-permute-start(bf16[64,4096]{1,0:T(8,128)(2,1)S(1)} %collective-permute-done.7.refs_2_), channel_id=1, source_target_pairs={{0,16},{1,33},{2,18},{3,35},{4,20},{5,37},{6,22},{7,39},{8,24},{9,... | collective-permute-start | bytes 1572872 | tf_op jit(solution)/shard_map/ppermute | solution.py:56
  42.1 1.5 %collective-permute-start.19 = (bf16[128,4096]{1,0:T(8,128)(2,1)S(1)}, bf16[128,4096]{1,0:T(8,128)(2,1)S(1)}, u32[]{:S(2)}, u32[]{:S(2)}) collective-permute-start(bf16[128,4096]{1,0:T(8,128)(2,1)S(1)} %constant_dynamic-update-slice_fusion.5.refs_1_), channel_id=1, source_target_pairs={{0,144},{1,97},{2,146},{3,99},{4,148},{5,101},{6,150},{7,103},{8,1... | collective-permute-start | bytes 3145736 | tf_op jit(solution)/shard_map/ppermute | solution.py:56
  43.6 0.1 collective-permute-start.20
  43.8 5.2 %score.3 = (f32[8,512]{1,0:T(8,128)S(1)}, f32[8,512]{1,0:T(8,128)S(1)}, bf16[512,4096]{1,0:T(8,128)(2,1)S(1)}) custom-call(f32[1,1152]{1,0:T(1,128)S(1)} %broadcast_in_dim.13.ids_ref, f32[1,512]{1,0:T(1,128)S(1)} %bitcast.12, f32[1,512]{1,0:T(1,128)S(1)} %collective-permute-done.2.other_wanted_ref, bf16[512,4096]{1,0:T(8,128)(2,1)S(1)} %copy-done, ...), custom_call_target="tpu_custom_call" | custom-call | flops 1610612736 | bytes 1572864 | tf_op jit(solution)/shard_map/score/pallas_call | solution.py:172
  49.0 0.0 collective-permute-done.10
  49.0 1.4 %collective-permute-done.12.refs_3_ = bf16[64,4096]{1,0:T(8,128)(2,1)S(1)} collective-permute-done((bf16[64,4096]{1,0:T(8,128)(2,1)S(1)}, bf16[64,4096]{1,0:T(8,128)(2,1)S(1)}, u32[]{:S(2)}, u32[]{:S(2)}) %collective-permute-start.12) | collective-permute-done | bytes 524320 | tf_op jit(solution)/shard_map/ppermute | solution.py:56
  50.4 0.6 collective-permute-start.15
  51.0 0.8 collective-permute-start.16
  51.9 1.5 %collective-permute-start.13 = (bf16[64,4096]{1,0:T(8,128)(2,1)S(1)}, bf16[64,4096]{1,0:T(8,128)(2,1)S(1)}, u32[]{:S(2)}, u32[]{:S(2)}) collective-permute-start(bf16[64,4096]{1,0:T(8,128)(2,1)S(1)} %constant_dynamic-update-slice_fusion.7.refs_0_), channel_id=1, source_target_pairs={{0,144},{1,97},{2,146},{3,99},{4,148},{5,101},{6,150},{7,103},{8,1... | collective-permute-start | bytes 1572872 | tf_op jit(solution)/shard_map/ppermute | solution.py:56
  53.4 7.2 %collective-permute-done.15.refs_2_ = bf16[64,4096]{1,0:T(8,128)(2,1)S(1)} collective-permute-done((bf16[64,4096]{1,0:T(8,128)(2,1)S(1)}, bf16[64,4096]{1,0:T(8,128)(2,1)S(1)}, u32[]{:S(2)}, u32[]{:S(2)}) %collective-permute-start.15) | collective-permute-done | bytes 524320 | tf_op jit(solution)/shard_map/ppermute | solution.py:56
  60.6 0.6 collective-permute-start.14
  61.2 0.7 collective-permute-start.17
  61.9 0.0 collective-permute-done.19.refs_4_
  61.9 1.2 %collective-permute-start.18 = (bf16[32,4096]{1,0:T(8,128)(2,1)S(1)}, bf16[32,4096]{1,0:T(8,128)(2,1)S(1)}, u32[]{:S(2)}, u32[]{:S(2)}) collective-permute-start(bf16[32,4096]{1,0:T(8,128)(2,1)S(1)} %slice.18), channel_id=1, source_target_pairs={{0,2},{1,3},{2,4},{3,5},{4,6},{5,7},{6,8},{7,9},{8,10},{9,11},{10,... | collective-permute-start | bytes 786440 | tf_op jit(solution)/shard_map/ppermute | solution.py:56
  63.1 0.0 collective-permute-done.20.refs_5_
  63.1 5.1 %score.4 = (f32[8,512]{1,0:T(8,128)S(1)}, f32[8,512]{1,0:T(8,128)S(1)}) custom-call(f32[1,1152]{1,0:T(1,128)S(1)} %broadcast_in_dim.13.ids_ref, f32[1,512]{1,0:T(1,128)S(1)} %bitcast.13, f32[1,512]{1,0:T(1,128)S(1)} %collective-permute-done.2.other_wanted_ref, bf16[512,4096]{1,0:T(8,128)(2,1)S(1)} %copy-done, ...), custom_call_target="tpu_custom_call" | custom-call | flops 4294967296 | bytes 4194304 | tf_op jit(solution)/shard_map/score/pallas_call | solution.py:172
  68.2 2.0 %collective-permute-done.14.refs_1_ = bf16[64,4096]{1,0:T(8,128)(2,1)S(1)} collective-permute-done((bf16[64,4096]{1,0:T(8,128)(2,1)S(1)}, bf16[64,4096]{1,0:T(8,128)(2,1)S(1)}, u32[]{:S(2)}, u32[]{:S(2)}) %collective-permute-start.14) | collective-permute-done | bytes 524320 | tf_op jit(solution)/shard_map/ppermute | solution.py:56
  70.1 0.0 collective-permute-done.17.refs_4_
  70.1 3.2 %score.5 = (f32[8,512]{1,0:T(8,128)S(1)}, f32[8,512]{1,0:T(8,128)S(1)}) custom-call(f32[1,1152]{1,0:T(1,128)S(1)} %broadcast_in_dim.13.ids_ref, f32[1,512]{1,0:T(1,128)S(1)} %bitcast.14, f32[1,512]{1,0:T(1,128)S(1)} %collective-permute-done.2.other_wanted_ref, bf16[512,4096]{1,0:T(8,128)(2,1)S(1)} %copy-done, ...), custom_call_target="tpu_custom_call" | custom-call | flops 2684354560 | bytes 2621440 | tf_op jit(solution)/shard_map/score/pallas_call | solution.py:172
  73.4 5.3 %collective-permute-start.21 = (f32[8,512]{1,0:T(8,128)S(1)}, f32[8,512]{1,0:T(8,128)S(1)}, u32[]{:S(2)}, u32[]{:S(2)}) collective-permute-start(f32[8,512]{1,0:T(8,128)S(1)} %get-tuple-element.44), channel_id=1, source_target_pairs={{0,1},{1,0},{2,3},{3,2},{4,5},{5,4},{6,7},{7,6},{8,9},{9,8},{10,11... | collective-permute-start | bytes 49160 | tf_op jit(solution)/shard_map/ppermute | solution.py:39
  78.7 0.8 collective-permute-done.21.got_ref
  79.6 1.0 class_sums.1
  80.6 22.5 %all_to_all.9 = f32[256,1,128]{2,1,0:T(1,128)S(1)} all-to-all(f32[256,1,128]{2,1,0:T(1,128)S(1)} %bitcast.10), channel_id=1, replica_groups=mesh['xh'=2,'y'=4,'xl'=2,'z'=8,'core'=2] {'xh','y','xl','z','core'}, dimensions={0} | all-to-all | bytes 262144 | tf_op jit(solution)/shard_map/all_to_all | solution.py:278
  103.0 0.3 reduce_sum.9
  103.3 0.5 multiply_bitcast_fusion
  (24 shorter events, 0.2 us)
Async XLA Ops:
  0.0 38.0 %collective-permute-start.8 = (bf16[512,4096]{1,0:T(8,128)(2,1)}, bf16[512,4096]{1,0:T(8,128)(2,1)}, u32[]{:S(2)}, u32[]{:S(2)}) collective-permute-start(bf16[512,4096]{1,0:T(8,128)(2,1)} %particles_ref.1), channel_id=1, source_target_pairs={{0,1},{1,0},{2,3},{3,2},{4,5},{5,4},{6,7},{7,6},{8,9},{9,8},{10,11... | collective-permute-start | bytes 12582920 | tf_op jit(solution)/shard_map/ppermute | solution.py:39
  3.2 7.9 %collective-permute-start = (bf16[8,4096]{1,0:T(8,128)(2,1)}, bf16[8,4096]{1,0:T(8,128)(2,1)S(1)}, u32[]{:S(2)}, u32[]{:S(2)}) collective-permute-start(bf16[8,4096]{1,0:T(8,128)(2,1)} %bitcast.17), channel_id=1, source_target_pairs={{0,8},{1,9},{2,10},{3,11},{4,12},{5,13},{6,14},{7,15},{8,0},{9,1},... | collective-permute-start | bytes 196616 | tf_op jit(solution)/shard_map/ppermute | solution.py:56
  8.4 35.4 %copy-start = (bf16[512,4096]{1,0:T(8,128)(2,1)S(1)}, bf16[512,4096]{1,0:T(8,128)(2,1)}, u32[]{:S(2)}) copy-start(bf16[512,4096]{1,0:T(8,128)(2,1)} %particles_ref.1) | copy-start | bytes 12582916
  12.0 7.2 %collective-permute-start.1 = (bf16[16,4096]{1,0:T(8,128)(2,1)S(1)}, bf16[16,4096]{1,0:T(8,128)(2,1)S(1)}, u32[]{:S(2)}, u32[]{:S(2)}) collective-permute-start(bf16[16,4096]{1,0:T(8,128)(2,1)S(1)} %pad_maximum_fusion), channel_id=1, source_target_pairs={{0,64},{1,129},{2,66},{3,131},{4,68},{5,133},{6,70},{7,135},{8,72}... | collective-permute-start | bytes 393224 | tf_op jit(solution)/shard_map/ppermute | solution.py:56
  14.8 4.4 %collective-permute-start.3 = (bf16[16,4096]{1,0:T(8,128)(2,1)S(1)}, bf16[16,4096]{1,0:T(8,128)(2,1)S(1)}, u32[]{:S(2)}, u32[]{:S(2)}) collective-permute-start(bf16[16,4096]{1,0:T(8,128)(2,1)S(1)} %pad_maximum_fusion), channel_id=1, source_target_pairs={{0,96},{1,145},{2,98},{3,147},{4,100},{5,149},{6,102},{7,151},{8,1... | collective-permute-start | bytes 393224 | tf_op jit(solution)/shard_map/ppermute | solution.py:56
  15.7 5.0 %collective-permute-start.4 = (bf16[16,4096]{1,0:T(8,128)(2,1)S(1)}, bf16[16,4096]{1,0:T(8,128)(2,1)S(1)}, u32[]{:S(2)}, u32[]{:S(2)}) collective-permute-start(bf16[16,4096]{1,0:T(8,128)(2,1)S(1)} %pad_maximum_fusion), channel_id=1, source_target_pairs={{0,32},{1,17},{2,34},{3,19},{4,36},{5,21},{6,38},{7,23},{8,40},{9,... | collective-permute-start | bytes 393224 | tf_op jit(solution)/shard_map/ppermute | solution.py:56
  20.7 13.9 %collective-permute-start.9 = (bf16[64,4096]{1,0:T(8,128)(2,1)S(1)}, bf16[64,4096]{1,0:T(8,128)(2,1)S(1)}, u32[]{:S(2)}, u32[]{:S(2)}) collective-permute-start(bf16[64,4096]{1,0:T(8,128)(2,1)S(1)} %constant_dynamic-update-slice_fusion.refs_0_), channel_id=1, source_target_pairs={{0,2},{1,3},{2,4},{3,5},{4,6},{5,7},{6,8},{7,9},{8,10},{9,11},{10,... | collective-permute-start | bytes 1572872 | tf_op jit(solution)/shard_map/ppermute | solution.py:56
  21.5 16.3 %collective-permute-start.5 = (bf16[64,4096]{1,0:T(8,128)(2,1)S(1)}, bf16[64,4096]{1,0:T(8,128)(2,1)S(1)}, u32[]{:S(2)}, u32[]{:S(2)}) collective-permute-start(bf16[64,4096]{1,0:T(8,128)(2,1)S(1)} %constant_dynamic-update-slice_fusion.refs_0_), channel_id=1, source_target_pairs={{0,14},{1,15},{2,0},{3,1},{4,2},{5,3},{6,4},{7,5},{8,6},{9,7},{10,... | collective-permute-start | bytes 1572872 | tf_op jit(solution)/shard_map/ppermute | solution.py:56
  25.0 12.9 %collective-permute-start.6 = (bf16[64,4096]{1,0:T(8,128)(2,1)S(1)}, bf16[64,4096]{1,0:T(8,128)(2,1)S(1)}, u32[]{:S(2)}, u32[]{:S(2)}) collective-permute-start(bf16[64,4096]{1,0:T(8,128)(2,1)S(1)} %constant_dynamic-update-slice_fusion.refs_0_), channel_id=1, source_target_pairs={{0,144},{1,97},{2,146},{3,99},{4,148},{5,101},{6,150},{7,103},{8,1... | collective-permute-start | bytes 1572872 | tf_op jit(solution)/shard_map/ppermute | solution.py:56
  27.8 10.2 %collective-permute-start.7 = (bf16[64,4096]{1,0:T(8,128)(2,1)S(1)}, bf16[64,4096]{1,0:T(8,128)(2,1)S(1)}, u32[]{:S(2)}, u32[]{:S(2)}) collective-permute-start(bf16[64,4096]{1,0:T(8,128)(2,1)S(1)} %constant_dynamic-update-slice_fusion.refs_0_), channel_id=1, source_target_pairs={{0,16},{1,33},{2,18},{3,35},{4,20},{5,37},{6,22},{7,39},{8,24},{9,... | collective-permute-start | bytes 1572872 | tf_op jit(solution)/shard_map/ppermute | solution.py:56
  34.6 9.0 %collective-permute-start.2 = (f32[1,512]{1,0:T(1,128)S(1)}, f32[1,512]{1,0:T(1,128)S(1)}, u32[]{:S(2)}, u32[]{:S(2)}) collective-permute-start(f32[1,512]{1,0:T(1,128)S(1)} %bitcast.11), channel_id=1, source_target_pairs={{0,1},{1,0},{2,3},{3,2},{4,5},{5,4},{6,7},{7,6},{8,9},{9,8},{10,11... | collective-permute-start | bytes 6152 | tf_op jit(solution)/shard_map/ppermute | solution.py:39
  37.9 11.1 %collective-permute-start.11 = (bf16[32,4096]{1,0:T(8,128)(2,1)S(1)}, bf16[32,4096]{1,0:T(8,128)(2,1)S(1)}, u32[]{:S(2)}, u32[]{:S(2)}) collective-permute-start(bf16[32,4096]{1,0:T(8,128)(2,1)S(1)} %slice.16), channel_id=1, source_target_pairs={{0,2},{1,3},{2,4},{3,5},{4,6},{5,7},{6,8},{7,9},{8,10},{9,11},{10,... | collective-permute-start | bytes 786440 | tf_op jit(solution)/shard_map/ppermute | solution.py:56
  38.1 10.9 %collective-permute-start.10 = (bf16[32,4096]{1,0:T(8,128)(2,1)S(1)}, bf16[32,4096]{1,0:T(8,128)(2,1)S(1)}, u32[]{:S(2)}, u32[]{:S(2)}) collective-permute-start(bf16[32,4096]{1,0:T(8,128)(2,1)S(1)} %slice.12), channel_id=1, source_target_pairs={{0,14},{1,15},{2,0},{3,1},{4,2},{5,3},{6,4},{7,5},{8,6},{9,7},{10,... | collective-permute-start | bytes 786440 | tf_op jit(solution)/shard_map/ppermute | solution.py:56
  40.8 9.6 %collective-permute-start.12 = (bf16[64,4096]{1,0:T(8,128)(2,1)S(1)}, bf16[64,4096]{1,0:T(8,128)(2,1)S(1)}, u32[]{:S(2)}, u32[]{:S(2)}) collective-permute-start(bf16[64,4096]{1,0:T(8,128)(2,1)S(1)} %collective-permute-done.7.refs_2_), channel_id=1, source_target_pairs={{0,16},{1,33},{2,18},{3,35},{4,20},{5,37},{6,22},{7,39},{8,24},{9,... | collective-permute-start | bytes 1572872 | tf_op jit(solution)/shard_map/ppermute | solution.py:56
  42.1 19.8 %collective-permute-start.19 = (bf16[128,4096]{1,0:T(8,128)(2,1)S(1)}, bf16[128,4096]{1,0:T(8,128)(2,1)S(1)}, u32[]{:S(2)}, u32[]{:S(2)}) collective-permute-start(bf16[128,4096]{1,0:T(8,128)(2,1)S(1)} %constant_dynamic-update-slice_fusion.5.refs_1_), channel_id=1, source_target_pairs={{0,144},{1,97},{2,146},{3,99},{4,148},{5,101},{6,150},{7,103},{8,1... | collective-permute-start | bytes 3145736 | tf_op jit(solution)/shard_map/ppermute | solution.py:56
  43.6 19.4 %collective-permute-start.20 = (bf16[128,4096]{1,0:T(8,128)(2,1)S(1)}, bf16[128,4096]{1,0:T(8,128)(2,1)S(1)}, u32[]{:S(2)}, u32[]{:S(2)}) collective-permute-start(bf16[128,4096]{1,0:T(8,128)(2,1)S(1)} %constant_dynamic-update-slice_fusion.5.refs_1_), channel_id=1, source_target_pairs={{0,16},{1,33},{2,18},{3,35},{4,20},{5,37},{6,22},{7,39},{8,24},{9,... | collective-permute-start | bytes 3145736 | tf_op jit(solution)/shard_map/ppermute | solution.py:56
  50.4 10.2 %collective-permute-start.15 = (bf16[64,4096]{1,0:T(8,128)(2,1)S(1)}, bf16[64,4096]{1,0:T(8,128)(2,1)S(1)}, u32[]{:S(2)}, u32[]{:S(2)}) collective-permute-start(bf16[64,4096]{1,0:T(8,128)(2,1)S(1)} %collective-permute-done.12.refs_3_), channel_id=1, source_target_pairs={{0,14},{1,15},{2,0},{3,1},{4,2},{5,3},{6,4},{7,5},{8,6},{9,7},{10,... | collective-permute-start | bytes 1572872 | tf_op jit(solution)/shard_map/ppermute | solution.py:56
  51.0 10.2 %collective-permute-start.16 = (bf16[64,4096]{1,0:T(8,128)(2,1)S(1)}, bf16[64,4096]{1,0:T(8,128)(2,1)S(1)}, u32[]{:S(2)}, u32[]{:S(2)}) collective-permute-start(bf16[64,4096]{1,0:T(8,128)(2,1)S(1)} %collective-permute-done.12.refs_3_), channel_id=1, source_target_pairs={{0,2},{1,3},{2,4},{3,5},{4,6},{5,7},{6,8},{7,9},{8,10},{9,11},{10,... | collective-permute-start | bytes 1572872 | tf_op jit(solution)/shard_map/ppermute | solution.py:56
  51.9 16.3 %collective-permute-start.13 = (bf16[64,4096]{1,0:T(8,128)(2,1)S(1)}, bf16[64,4096]{1,0:T(8,128)(2,1)S(1)}, u32[]{:S(2)}, u32[]{:S(2)}) collective-permute-start(bf16[64,4096]{1,0:T(8,128)(2,1)S(1)} %constant_dynamic-update-slice_fusion.7.refs_0_), channel_id=1, source_target_pairs={{0,144},{1,97},{2,146},{3,99},{4,148},{5,101},{6,150},{7,103},{8,1... | collective-permute-start | bytes 1572872 | tf_op jit(solution)/shard_map/ppermute | solution.py:56
  60.6 9.5 %collective-permute-start.14 = (bf16[64,4096]{1,0:T(8,128)(2,1)S(1)}, bf16[64,4096]{1,0:T(8,128)(2,1)S(1)}, u32[]{:S(2)}, u32[]{:S(2)}) collective-permute-start(bf16[64,4096]{1,0:T(8,128)(2,1)S(1)} %constant_dynamic-update-slice_fusion.7.refs_0_), channel_id=1, source_target_pairs={{0,16},{1,33},{2,18},{3,35},{4,20},{5,37},{6,22},{7,39},{8,24},{9,... | collective-permute-start | bytes 1572872 | tf_op jit(solution)/shard_map/ppermute | solution.py:56
  61.2 8.9 %collective-permute-start.17 = (bf16[32,4096]{1,0:T(8,128)(2,1)S(1)}, bf16[32,4096]{1,0:T(8,128)(2,1)S(1)}, u32[]{:S(2)}, u32[]{:S(2)}) collective-permute-start(bf16[32,4096]{1,0:T(8,128)(2,1)S(1)} %slice.17), channel_id=1, source_target_pairs={{0,14},{1,15},{2,0},{3,1},{4,2},{5,3},{6,4},{7,5},{8,6},{9,7},{10,... | collective-permute-start | bytes 786440 | tf_op jit(solution)/shard_map/ppermute | solution.py:56
  61.9 8.2 %collective-permute-start.18 = (bf16[32,4096]{1,0:T(8,128)(2,1)S(1)}, bf16[32,4096]{1,0:T(8,128)(2,1)S(1)}, u32[]{:S(2)}, u32[]{:S(2)}) collective-permute-start(bf16[32,4096]{1,0:T(8,128)(2,1)S(1)} %slice.18), channel_id=1, source_target_pairs={{0,2},{1,3},{2,4},{3,5},{4,6},{5,7},{6,8},{7,9},{8,10},{9,11},{10,... | collective-permute-start | bytes 786440 | tf_op jit(solution)/shard_map/ppermute | solution.py:56
  70.1 9.4 %copy-start.1 = (f32[512]{0:T(512)S(1)}, f32[512]{0:T(512)}, u32[]{:S(2)}) copy-start(f32[512]{0:T(512)} %param.13) | copy-start | bytes 6148
  73.4 6.2 %collective-permute-start.21 = (f32[8,512]{1,0:T(8,128)S(1)}, f32[8,512]{1,0:T(8,128)S(1)}, u32[]{:S(2)}, u32[]{:S(2)}) collective-permute-start(f32[8,512]{1,0:T(8,128)S(1)} %get-tuple-element.44), channel_id=1, source_target_pairs={{0,1},{1,0},{2,3},{3,2},{4,5},{5,4},{6,7},{7,6},{8,9},{9,8},{10,11... | collective-permute-start | bytes 49160 | tf_op jit(solution)/shard_map/ppermute | solution.py:39
